TPU v7x, 1024 devices: a whole 8x8x8 slice. The times are simulated.
1024 devices in a mesh: elem: 64 (over y, z_hi, core), plane: 16 (over z_lo, x).
Axes of the slice: x: 8, y: 8, z: 8 (z_hi: 4, z_lo: 2; z = z_hi * 2 + z_lo), core: 2. Of those that a mesh axis runs over, the one named last changes fastest.
Arguments:
- velocity_modes: bfloat16 [3, 512, 512, 144], P(None, 'plane', 'elem'), may hold values from -0.8 to 0.8
- metric: float32 [512, 4], P('elem'), may hold values from 0.5 to 2
- face_partner: int32 [512, 4], P('elem'), may hold values from -1 to 511, as said below
- face_side: int32 [512, 4], P('elem'), may hold values from 0 to 3
- face_flip: int32 [512, 4], P('elem'), may hold values from 0 to 1
Outputs:
- nonlinear_term: bfloat16 [3, 512, 512, 144], P(None, 'plane', 'elem')
Inputs may be any that keep to these rules, and one draw needn't show every extreme that they name: `face_partner`: the faces are mutual: if face f of element e names p with side s and flip t, face s of p names e with side f and flip t. Every partner lies on the same index of elem or on the one before or after it, cyclically; on each index exactly 2 elements have a face whose partner lies on the index before, and exactly 2 on the index after.
All inputs are finite; a program needn't handle non-finite values.
Results may differ from a plain program's by a relative error of at most 0.0076.
Values may be sent and summed in bfloat16 or wider, within the bound.
No kernel may reach another device: no remote copies, remote signals or barrier semaphores. Data moves between devices by JAX's collectives and lax.ppermute only.
A program may use at most 32 MiB of HBM per device.

v0:
```python
import jax
import jax.numpy as jnp
import numpy as np
from jax import lax
from jax.sharding import PartitionSpec as P


def padded(shard, sides, width):
    for axis, dim in sides:
        peers, length = (lax.axis_size(axis), shard.shape[dim])
        up = [(i, (i + 1) % peers) for i in range(peers)]
        down = [(j, i) for i, j in up]
        last = lax.slice_in_dim(shard, length - width, length, axis=dim)
        initial = lax.slice_in_dim(shard, 0, width, axis=dim)
        before = lax.ppermute(last, axis, up)
        after = lax.ppermute(initial, axis, down)
        shard = jnp.concatenate([before, shard, after], axis=dim)
    return shard


def for_sending(shard):
    return jax.tree.map(lambda a: a.astype(jnp.bfloat16) if a.dtype == jnp.float32 else a, shard)


def legendre_tables():
    node_points = -np.cos(np.pi * np.arange(12) / 11.0)
    values = np.zeros((12, 12))
    slopes = np.zeros((12, 12))
    values[:, 0] = 1.0
    values[:, 1] = node_points
    slopes[:, 1] = 1.0
    for degree in range(1, 11):
        values[:, degree + 1] = (
            (2 * degree + 1) * node_points * values[:, degree] - degree * values[:, degree - 1]
        ) / (degree + 1)
        slopes[:, degree + 1] = slopes[:, degree - 1] + (2 * degree + 1) * values[:, degree]
    basis_table = np.kron(values, values).T
    along_xi = np.kron(slopes, values).T
    along_eta = np.kron(values, slopes).T
    return tuple(
        (
            jnp.asarray(table, dtype=jnp.float32).astype(jnp.bfloat16)
            for table in (basis_table, along_xi, along_eta)
        )
    )


def fourier_tables(planes, phys):
    plane_index = jnp.arange(planes, dtype=jnp.int32)
    wave_number = plane_index // 2
    is_imag = plane_index % 2 == 1
    point_index = jnp.arange(phys, dtype=jnp.int32)
    turn_count = point_index[:, None] * wave_number[None, :] % phys
    phase_angle = turn_count.astype(jnp.float32) * (2.0 * np.pi / phys)
    weight = jnp.where(wave_number == 0, 1.0, 2.0).astype(jnp.float32)
    inverse = jnp.where(
        is_imag[None, :],
        -weight[None, :] * jnp.sin(phase_angle),
        weight[None, :] * jnp.cos(phase_angle),
    )
    forward = jnp.where(is_imag[None, :], -jnp.sin(phase_angle), jnp.cos(phase_angle)).T / phys
    return (inverse.astype(jnp.bfloat16), forward.astype(jnp.bfloat16))


def element_fields(mode_block, geometry, tables):
    basis_table, along_xi, along_eta = tables
    point_values = jnp.dot(mode_block, basis_table, preferred_element_type=jnp.float32).astype(
        jnp.bfloat16
    )
    d_xi = jnp.dot(mode_block, along_xi, preferred_element_type=jnp.float32)
    d_eta = jnp.dot(mode_block, along_eta, preferred_element_type=jnp.float32)
    coef = [geometry[:, k][None, None, :, None] for k in range(4)]
    grad_x = d_xi * coef[0] + d_eta * coef[1]
    grad_y = d_xi * coef[2] + d_eta * coef[3]
    grads = jnp.stack([grad_x, grad_y], axis=1).astype(jnp.bfloat16)
    dims_in = mode_block.shape
    return (point_values, grads.reshape(6, dims_in[1], dims_in[2], dims_in[3]))


def face_traces(grads):
    fields, planes, elems, npts = grads.shape
    grid_view = grads.reshape(fields, planes, elems, 12, 12)
    face_rows = jnp.stack(
        [grid_view[..., 0, :], grid_view[..., 11, :], grid_view[..., :, 0], grid_view[..., :, 11]],
        axis=3,
    )
    return face_rows.transpose(2, 3, 4, 0, 1).reshape(elems, 4, 12, fields * planes)


def average_rows(own_rows, other_rows, partner, flip):
    other_rows = jnp.where(flip[:, :, None, None] == 1, other_rows[:, :, ::-1, :], other_rows)
    return jnp.where(
        partner[:, :, None, None] >= 0,
        0.5 * (own_rows.astype(jnp.float32) + other_rows.astype(jnp.float32)),
        own_rows.astype(jnp.float32),
    ).astype(jnp.bfloat16)


def write_faces(grads, restored):
    fields, planes, elems, npts = grads.shape
    grid_view = grads.reshape(fields, planes, elems, 12, 12)
    grid_view = grid_view.at[..., 0, 1:11].set(restored[..., 0, :])
    grid_view = grid_view.at[..., 11, 1:11].set(restored[..., 1, :])
    grid_view = grid_view.at[..., 1:11, 0].set(restored[..., 2, :])
    grid_view = grid_view.at[..., 1:11, 11].set(restored[..., 3, :])
    return grid_view.reshape(fields, planes, elems, npts)


def z_gradients(values, first_plane):
    dims_in = values.shape
    paired = values.astype(jnp.float32).reshape(dims_in[0], dims_in[1] // 2, 2, -1)
    wave_number = (first_plane // 2 + jnp.arange(dims_in[1] // 2, dtype=jnp.int32)).astype(
        jnp.float32
    ) / 32.0
    scale = wave_number[None, :, None]
    turned = jnp.stack([-scale * paired[:, :, 1], scale * paired[:, :, 0]], axis=2)
    return turned.reshape(dims_in).astype(jnp.bfloat16)


def advection(physical):
    terms = []
    for comp in range(3):
        term = (
            physical[:, 0] * physical[:, 3 + 2 * comp]
            + physical[:, 1] * physical[:, 4 + 2 * comp]
            + physical[:, 2] * physical[:, 9 + comp]
        )
        terms.append(term)
    return jnp.stack(terms, axis=1).astype(jnp.bfloat16)


def on_device(velocity_modes, metric, face_partner, face_side, face_flip):
    tables = legendre_tables()
    planes_dev = velocity_modes.shape[1]
    elems = velocity_modes.shape[2]
    npts = velocity_modes.shape[3]
    point_values, grads = element_fields(velocity_modes, metric, tables)
    own_rows = face_traces(grads)
    my_index = lax.axis_index("elem")
    elem_count = lax.axis_size("elem")
    first_elem = my_index * elems
    wider = padded(own_rows, (("elem", 0),), elems)
    offset = jnp.where(
        face_partner >= 0, (face_partner - first_elem + elems) % (elem_count * elems), elems
    )
    other_rows = wider[offset, face_side]
    averaged = average_rows(own_rows, other_rows, face_partner, face_flip)
    plane_count = lax.axis_size("plane")
    line_cols = elems * npts // plane_count
    all_planes = planes_dev * plane_count
    inverse, forward = fourier_tables(all_planes, 3 * all_planes // 2)
    restored = averaged.reshape(elems, 4, 12, 6, planes_dev).transpose(3, 4, 0, 1, 2)[..., 1:11]
    outgoing_fields = jnp.concatenate([point_values, write_faces(grads, restored)], axis=0)
    field_count = outgoing_fields.shape[0]
    shaped = outgoing_fields.reshape(field_count, planes_dev, plane_count, line_cols)
    flattened = lax.all_to_all(shaped, "plane", split_axis=2, concat_axis=1, tiled=True)[:, :, 0, :]
    if field_count == 9:
        flattened = jnp.concatenate([flattened, z_gradients(flattened[0:3], 0)], axis=0)
    col_count = flattened.shape[2]

    def one_block(first_col):
        physical = jnp.einsum("jp,fpc->cfj", inverse, flattened, preferred_element_type=jnp.float32)
        adv = advection(physical)
        return jnp.einsum("pj,cgj->cgp", forward, adv, preferred_element_type=jnp.float32).astype(
            jnp.bfloat16
        )

    starts = jnp.arange(col_count // col_count, dtype=jnp.int32) * col_count
    results = lax.map(one_block, starts).reshape(col_count, 3, all_planes).transpose(1, 2, 0)
    combined = lax.all_to_all(
        for_sending(results[:, :, None, :]), "plane", split_axis=1, concat_axis=2, tiled=True
    )
    return combined.reshape(3, planes_dev, elems, npts)


def solution(mesh):
    placed = (
        P(None, "plane", "elem", None),
        P("elem", None),
        P("elem", None),
        P("elem", None),
        P("elem", None),
    )
    return jax.shard_map(
        on_device,
        mesh=mesh,
        in_specs=placed,
        out_specs=P(None, "plane", "elem", None),
        check_vma=False,
    )
```

profile of v0, /device:TPU:18, one launch (start us, length us, event | category | flops | bytes accessed | tf_op | source)
XLA Modules:
  0.0 111.3 jit_solution(11821981829340013538)
XLA Ops:
  0.0 0.8 slice_bitcast_fusion.11
  0.8 0.2 copy-done
  1.1 1.1 %fusion.43 = f32[144,3,32,8]{0,2,3,1:T(8,128)S(1)} fusion(bf16[144,144,1,1]{1,0,3,2:T(8,128)(2,1)} %constant.251, bf16[3,32,8,144]{3,2,1,0:T(8,128)(2,1)S(1)} %copy-done), kind=kOutput, calls=%fused_computation.64 | convolution fusion | flops 31850496 | bytes 705024 | tf_op jit(solution)/shard_map/dot_general | solution.py:71
  2.2 1.2 %fusion.34 = (bf16[3,1,32,8,144]{4,2,3,0,1:T(8,128)(2,1)S(1)}, bf16[3,1,32,8,144]{4,2,3,0,1:T(8,128)(2,1)S(1)}) fusion(f32[144,3,32,8]{0,2,3,1:T(8,128)S(1)} %fusion.43, f32[8]{0:T(128)S(1)} %get-tuple-element.80, f32[8]{0:T(128)S(1)} %get-tuple-element.79, f32[8]{0:T(128)S(1)} %get-tuple-element.81, f32[8]{0:T(128)S(1)} %get-tuple-element.82, ...), kind=kOutput, calls=%fused_computation.51 | convolution fusion | flops 32735232 | bytes 1147520 | tf_op jit(solution)/shard_map/dot_general | solution.py:70
  3.4 0.2 pad_maximum_fusion.1
  3.6 1.1 copy.105
  4.8 0.2 maximum_bitcast_fusion
  5.0 0.3 copy.109
  5.2 0.4 reshape.258
  5.7 1.9 %collective-permute-start = (bf16[8,4,12,192]{3,2,1,0:T(8,128)(2,1)S(1)}, bf16[8,4,12,192]{3,2,1,0:T(8,128)(2,1)S(1)}, u32[]{:S(2)}, u32[]{:S(2)}) collective-permute-start(bf16[8,4,12,192]{3,2,1,0:T(8,128)(2,1)S(1)} %copy.110), channel_id=1, source_target_pairs={{0,16},{16,32},{32,48},{48,64},{64,80},{80,96},{96,112},{112,128},... | collective-permute-start | bytes 442376 | tf_op jit(solution)/shard_map/ppermute | solution.py:15
  7.7 15.6 %collective-permute-start.1 = (bf16[8,4,12,192]{3,2,1,0:T(8,128)(2,1)S(1)}, bf16[8,4,12,192]{3,2,1,0:T(8,128)(2,1)}, u32[]{:S(2)}, u32[]{:S(2)}) collective-permute-start(bf16[8,4,12,192]{3,2,1,0:T(8,128)(2,1)S(1)} %copy.110), channel_id=1, source_target_pairs={{16,0},{32,16},{48,32},{64,48},{80,64},{96,80},{112,96},{128,112},... | collective-permute-start | bytes 442376 | tf_op jit(solution)/shard_map/ppermute | solution.py:16
  23.3 0.3 fusion.10
  23.6 0.1 copy.113
  23.7 0.1 reshape.266
  23.8 1.3 %copy.133 = bf16[3,32,8,144]{1,3,2,0:T(8,128)(2,1)} copy(bf16[3,32,8,144]{3,1,2,0:T(8,128)(2,1)S(1)} %fusion.10) | data formatting | bytes 442368 | tf_op jit(solution)/shard_map/concatenate | solution.py:153
  25.1 0.6 fusion.85
  25.6 1.4 %collective-permute-done = bf16[8,4,12,192]{3,2,1,0:T(8,128)(2,1)S(1)} collective-permute-done((bf16[8,4,12,192]{3,2,1,0:T(8,128)(2,1)S(1)}, bf16[8,4,12,192]{3,2,1,0:T(8,128)(2,1)S(1)}, u32[]{:S(2)}, u32[]{:S(2)}) %collective-permute-start) | collective-permute-done | bytes 147488 | tf_op jit(solution)/shard_map/ppermute | solution.py:15
  27.0 0.7 copy-done.1
  27.8 1.2 %pad_maximum_fusion.2 = bf16[24,4,12,192]{3,2,1,0:T(8,128)(2,1)S(1)} fusion(bf16[8,4,12,192]{3,2,1,0:T(8,128)(2,1)} %collective-permute-done.1, bf16[8,4,12,192]{3,2,1,0:T(8,128)(2,1)S(1)} %copy.110, bf16[8,4,12,192]{3,2,1,0:T(8,128)(2,1)} %copy-done.1), kind=kLoop, calls=%fused_computation.29 | loop fusion | flops 442368 | bytes 884736 | tf_op jit(solution)/shard_map/concatenate | solution.py:17
  29.0 0.6 gather_fusion
  29.6 0.1 copy.115
  29.7 0.2 fusion.33
  29.9 0.4 reshape.259
  30.3 0.1 copy.149
  30.4 1.2 %fusion.60 = bf16[6,32,8,12,12]{1,2,4,3,0:T(8,128)(2,1)S(1)} fusion(bf16[6,32,8,12,12]{1,2,4,3,0:T(8,128)(2,1)S(1)} %bitcast.103, s32[]{:T(128)} %bitcast.24, s32[]{:T(128)} %bitcast.25, bf16[6,32,8,4,12]{1,2,4,0,3:T(8,128)(2,1)S(1)} %bitcast.111), kind=kLoop, calls=%fused_computation.99 | loop fusion | bytes 245768 | tf_op jit(solution)/shard_map/scatter | solution.py:102
  31.8 2.0 %copy.120 = bf16[6,32,8,12,12]{1,4,3,2,0:T(8,128)(2,1)} copy(bf16[6,32,8,12,12]{1,2,4,3,0:T(8,128)(2,1)S(1)} %fusion.57) | data formatting | bytes 884736 | tf_op jit(solution)/shard_map/scatter | solution.py:105
  33.8 4.1 %concatenate.32 = bf16[6,32,16,72]{1,3,2,0:T(8,128)(2,1)} reshape(bf16[6,32,8,12,12]{1,4,3,2,0:T(8,128)(2,1)} %copy.120) | data formatting | bytes 884736 | tf_op jit(solution)/shard_map/concatenate | solution.py:153
  37.9 2.2 %pad_maximum_fusion = bf16[9,32,16,72]{1,3,2,0:T(8,128)(2,1)S(1)} fusion(bf16[6,32,16,72]{1,3,2,0:T(8,128)(2,1)} %concatenate.32, bf16[3,32,16,72]{1,3,2,0:T(8,128)(2,1)} %bitcast.107), kind=kLoop, calls=%fused_computation.1 | loop fusion | flops 331776 | bytes 1327104 | tf_op jit(solution)/shard_map/concatenate | solution.py:153
  40.1 2.3 %copy.122 = bf16[9,32,16,72]{3,1,0,2:T(8,128)(2,1)} copy(bf16[9,32,16,72]{1,3,2,0:T(8,128)(2,1)S(1)} %pad_maximum_fusion) | data formatting | bytes 1327104 | tf_op jit(solution)/shard_map/concatenate | solution.py:153
  42.5 9.4 %all-to-all-start = ((bf16[9,32,16,72]{3,1,0,2:T(8,128)(2,1)}), bf16[9,32,16,72]{3,1,0,2:T(8,128)(2,1)S(1)}, u32[]{:S(2)}, u32[]{:S(2)}) async-start(bf16[9,32,16,72]{3,1,0,2:T(8,128)(2,1)} %copy.122), calls=%async_computation | async-start | bytes 2359296 | tf_op jit(solution)/shard_map/all_to_all | solution.py:156
  51.9 24.9 %all-to-all-done = bf16[9,32,16,72]{3,1,0,2:T(8,128)(2,1)S(1)} async-done(((bf16[9,32,16,72]{3,1,0,2:T(8,128)(2,1)}), bf16[9,32,16,72]{3,1,0,2:T(8,128)(2,1)S(1)}, u32[]{:S(2)}, u32[]{:S(2)}) %all-to-all-start) | async-done | bytes 663584 | tf_op jit(solution)/shard_map/all_to_all | solution.py:156
  76.8 0.1 slice_convert_fusion
  76.9 0.3 copy.123
  77.1 0.1 copy.124
  77.2 1.1 fusion.37
  78.3 1.0 pad_maximum_fusion.3
  79.3 0.2 copy.126
  79.5 0.8 copy.125
  80.3 7.1 %convolution_bitcast_fusion = f32[72,12,768]{2,0,1:T(8,128)S(1)} fusion(bf16[3,512,72]{1,2,0:T(8,128)(2,1)S(1)} %copy.126, bf16[9,512,72]{1,2,0:T(8,128)(2,1)S(1)} %copy.125, f32[512]{0:T(512)S(1)} %get-tuple-element.89, s32[512]{0:T(512)S(1)} %add_select_fusion.2, f32[512]{0:T(512)S(1)} %get-tuple-element.90, pred[512]{0:T(512)(128)(4,1)S(1)} %fusion.63), kind=kOutput, calls=%fused_computation.4 | convolution fusion | flops 685031424 | bytes 3545600 | tf_op jit(solution)/shard_map/while/body/eval_jaxpr/jp,fpc->cfj/dot_general | solution.py:162
  87.4 0.2 fusion.55
  87.5 7.1 %fusion.11 = bf16[3,512,1,72]{1,3,0,2:T(8,128)(2,1)S(1)} fusion(s32[512]{0:T(512)S(1)} %add_select_fusion.2, pred[512]{0:T(512)(128)(4,1)S(1)} %fusion.63, bf16[72,1,768]{2,0,1:T(8,128)(2,1)S(1)} %get-tuple-element.70, bf16[72,1,768]{2,0,1:T(8,128)(2,1)S(1)} %get-tuple-element.69, bf16[72,1,768]{2,0,1:T(8,128)(2,1)S(1)} %get-tuple-element.68), kind=kOutput, calls=%fused_computation.22 | convolution fusion | flops 175423488 | bytes 555520 | tf_op jit(solution)/shard_map/while/body/eval_jaxpr/pj,cgj->cgp/dot_general | solution.py:164
  94.6 0.3 copy.127
  94.9 0.7 reshape.289
  95.7 13.7 %all_to_all.30 = bf16[16,2,3456]{2,1,0:T(2,128)(2,1)S(1)} all-to-all(bf16[16,2,3456]{2,1,0:T(2,128)(2,1)S(1)} %reshape.289), channel_id=1, replica_groups=mesh['elem'=64,'plane'=16] {'plane'}, dimensions={0} | all-to-all | bytes 442368 | tf_op jit(solution)/shard_map/all_to_all | solution.py:170
  109.3 0.8 reshape.290
  110.2 0.1 copy.128
  110.2 0.2 copy.129
  110.4 1.0 reshape.264
  (24 shorter events, 0.3 us)
Async XLA Ops:
  0.0 1.1 copy-start
  4.9 18.4 %copy-start.2 = (bf16[144,144,1,1]{1,0,3,2:T(8,128)(2,1)S(1)}, bf16[144,144,1,1]{1,0,3,2:T(8,128)(2,1)}, u32[]{:S(2)}) copy-start(bf16[144,144,1,1]{1,0,3,2:T(8,128)(2,1)} %constant.249) | copy-start | bytes 124420
  4.9 18.6 %copy-start.3 = (s32[8,4]{0,1:T(4,128)S(1)}, s32[8,4]{0,1:T(4,128)}, u32[]{:S(2)}) copy-start(s32[8,4]{0,1:T(4,128)} %param.18) | copy-start | bytes 388
  4.9 18.6 %copy-start.4 = (s32[8,4]{0,1:T(4,128)S(1)}, s32[8,4]{0,1:T(4,128)}, u32[]{:S(2)}) copy-start(s32[8,4]{0,1:T(4,128)} %param.19) | copy-start | bytes 388
  5.0 18.6 %copy-start.5 = (s32[8,4]{0,1:T(4,128)S(1)}, s32[8,4]{0,1:T(4,128)}, u32[]{:S(2)}) copy-start(s32[8,4]{0,1:T(4,128)} %param.20) | copy-start | bytes 388
  5.7 21.3 %collective-permute-start = (bf16[8,4,12,192]{3,2,1,0:T(8,128)(2,1)S(1)}, bf16[8,4,12,192]{3,2,1,0:T(8,128)(2,1)S(1)}, u32[]{:S(2)}, u32[]{:S(2)}) collective-permute-start(bf16[8,4,12,192]{3,2,1,0:T(8,128)(2,1)S(1)} %copy.110), channel_id=1, source_target_pairs={{0,16},{16,32},{32,48},{48,64},{64,80},{80,96},{96,112},{112,128},... | collective-permute-start | bytes 442376 | tf_op jit(solution)/shard_map/ppermute | solution.py:15
  7.7 20.1 %collective-permute-start.1 = (bf16[8,4,12,192]{3,2,1,0:T(8,128)(2,1)S(1)}, bf16[8,4,12,192]{3,2,1,0:T(8,128)(2,1)}, u32[]{:S(2)}, u32[]{:S(2)}) collective-permute-start(bf16[8,4,12,192]{3,2,1,0:T(8,128)(2,1)S(1)} %copy.110), channel_id=1, source_target_pairs={{16,0},{32,16},{48,32},{64,48},{80,64},{96,80},{112,96},{128,112},... | collective-permute-start | bytes 442376 | tf_op jit(solution)/shard_map/ppermute | solution.py:16
  27.0 0.7 copy-start.1
  42.5 34.3 %all-to-all-start = ((bf16[9,32,16,72]{3,1,0,2:T(8,128)(2,1)}), bf16[9,32,16,72]{3,1,0,2:T(8,128)(2,1)S(1)}, u32[]{:S(2)}, u32[]{:S(2)}) async-start(bf16[9,32,16,72]{3,1,0,2:T(8,128)(2,1)} %copy.122), calls=%async_computation | async-start | bytes 2359296 | tf_op jit(solution)/shard_map/all_to_all | solution.py:156
where the time goes:
time: 112 us; the launch traced here: 111 us
  starting transfers between devices  26.9 us (24%)
  waiting for transfers between devices  26.3 us (23%)
  local copies, waits for them, and re-layouts  20.9 us (19%)
  matrix products  16.8 us (15%)
  blocking collectives  13.7 us (12%)
  other arithmetic  6.38 us (6%)
    all_to_all x1, waiting for transfers between devices, on_device(): lax.all_to_all(shaped, 'plane', split_axis=2, concat_axis=1, tiled=True)  24.9 us
    ppermute x1, starting transfers between devices, padded(): after = lax.ppermute(initial, axis, down)  15.6 us
    all_to_all x1, blocking collectives, on_device(): lax.all_to_all(for_sending(results[:, :, None, :]), 'plane', split_axis=1...  13.7 us
    all_to_all x1, starting transfers between devices, on_device(): lax.all_to_all(shaped, 'plane', split_axis=2, concat_axis=1, tiled=True)  9.36 us
    concatenate x3, local copies, waits for them, and re-layouts, on_device(): jnp.concatenate([point_values, write_faces(grads, restored)], axis=0)  7.7 us
    dot_general x1, matrix products, one_block(): jnp.einsum('pj,cgj->cgp', forward, adv, preferred_element_type=jnp.float32)  7.1 us
    dot_general x1, matrix products, one_block(): jnp.einsum('jp,fpc->cfj', inverse, flattened, preferred_element_type=jnp....  7.07 us
    unnamed x15, local copies, waits for them, and re-layouts  2.52 us
  transfers between devices with their start and end apart: 3, of which 2 were waited for; matrix products, arithmetic and copies ran while one was open for 2% of the time, Pallas kernels for 0%

commit v1 on v0

v1 whole, which is shorter than its diff:
```python
import functools

import jax
import jax.numpy as jnp
import numpy as np
from jax import lax
from jax.experimental import pallas as pl
from jax.experimental.pallas import tpu as pltpu
from jax.sharding import PartitionSpec as P

F32, BF16 = jnp.float32, jnp.bfloat16
NT = (((1,), (1,)), ((), ()))
INTERPRET = False


def bf16(table):
    return jnp.asarray(np.asarray(table, np.float32)).astype(BF16)


def legendre_tables():
    points = -np.cos(np.pi * np.arange(12) / 11.0)
    values, slopes = np.zeros((12, 12)), np.zeros((12, 12))
    values[:, 0] = 1.0
    values[:, 1] = points
    slopes[:, 1] = 1.0
    for n in range(1, 11):
        values[:, n + 1] = ((2 * n + 1) * points * values[:, n] - n * values[:, n - 1]) / (n + 1)
        slopes[:, n + 1] = slopes[:, n - 1] + (2 * n + 1) * values[:, n]
    return np.kron(values, values), np.kron(slopes, values), np.kron(values, slopes)


def face_points(face):
    t = np.arange(12)
    return (t, 132 + t, 12 * t, 12 * t + 11)[face]


def trace_table():
    _, xi, eta = legendre_tables()
    table = np.zeros((272, 144))
    table[np.arange(16), 128 + np.arange(16)] = 1.0
    for face in range(4):
        q = face_points(face)
        for at, rows in ((16, xi[q]), (80, eta[q]), (144, xi[q[::-1]]), (208, eta[q[::-1]])):
            table[at + 16 * face : at + 16 * face + 12] = rows
    return table


def point_table():
    basis, xi, eta = legendre_tables()
    return np.stack([np.concatenate([t[72 * h : 72 * h + 72] for t in (basis, xi, eta)]) for h in range(2)])


def half_face_rows(h):
    own = [(h, t) for t in range(1, 11)]
    along = range(1, 6) if h == 0 else range(6, 11)
    return own + [(f, t) for f in (2, 3) for t in along]


def pick_table():
    table = np.zeros((80, 128))
    for h in range(2):
        for g in range(2):
            for i, (f, t) in enumerate(half_face_rows(h)):
                table[40 * h + 20 * g + i, 64 * g + 16 * f + t] = 1.0
    return table


def place_table():
    table = np.zeros((2, 144, 40))
    for h in range(2):
        for g in range(2):
            for i, (f, t) in enumerate(half_face_rows(h)):
                table[h, 72 * g + face_points(f)[t] - 72 * h, 20 * g + i] = 1.0
    return table


def fourier_tables(planes, phys):
    m = np.arange(planes) // 2
    odd = np.arange(planes) % 2 == 1
    theta = (2.0 * np.pi / phys) * ((np.arange(phys)[None, :] * m[:, None]) % phys)
    weight = np.where(m == 0, 1.0, 2.0)[:, None]
    synth = np.where(odd[:, None], -weight * np.sin(theta), weight * np.cos(theta))
    analysis = np.where(odd[:, None], -np.sin(theta), np.cos(theta)) / phys
    return synth, analysis


def iota(shape, axis):
    return lax.broadcasted_iota(jnp.int32, shape, axis)


def to_element_rows():
    out, inp = iota((128, 128), 0), iota((128, 128), 1)
    return jnp.where(inp == (out % 16) * 8 + out // 16, 1.0, 0.0).astype(BF16)


def reverse_faces():
    out, inp = iota((128, 128), 0), iota((128, 128), 1)
    t = out % 16
    return jnp.where((t < 12) & (inp == out - t + 11 - t), 1.0, 0.0).astype(BF16)


def dot(a, b):
    return jnp.dot(a, b, preferred_element_type=F32)


def dot_nt(a, b):
    return lax.dot_general(a, b, NT, preferred_element_type=F32)


def dot_tn(a, b):
    return lax.dot_general(a, b, (((0,), (0,)), ((), ())), preferred_element_type=F32)


def prev_next(where_ref, blocks):
    me = where_ref[0]
    return me, jnp.where(me == 0, blocks - 1, me - 1), jnp.where(me == blocks - 1, 0, me + 1)


def pack_kernel(blocks, where_ref, partner_ref, metric_ref, v_ref, table_ref, modal_ref, own_ref, prev_ref, next_ref, rows_ref):
    order = to_element_rows()
    rows_ref[:, 96:128, :] = jnp.zeros((8, 32, 144), BF16)
    for b in range(6):
        block = dot(order, v_ref[128 * b : 128 * b + 128, :]).astype(BF16)
        for e in range(8):
            rows_ref[e, 16 * b : 16 * b + 16, :] = block[16 * e : 16 * e + 16]
    table = table_ref[...]
    for e in range(8):
        rows = rows_ref[e]
        out = dot_nt(table, rows)
        tail = out[0:16].astype(BF16)
        for z in range(2):
            modal_ref[z, e, 0:96, :] = rows[0:96, 0:128]
            modal_ref[z, e, 96:112, :] = tail
        for flip in range(2):
            xi = out[16 + 128 * flip : 80 + 128 * flip]
            eta = out[80 + 128 * flip : 144 + 128 * flip]
            for g in range(2):
                grad = xi * metric_ref[e, 2 * g] + eta * metric_ref[e, 2 * g + 1]
                own_ref[e, flip, 64 * g : 64 * g + 64, :] = grad.astype(BF16)
    me, before, after = prev_next(where_ref, blocks)
    for side, out_ref in ((before, prev_ref), (after, next_ref)):
        low, high = jnp.int32(7), jnp.int32(0)
        for e in range(8):
            for f in range(4):
                p = partner_ref[e, f]
                there = (p >= 0) & (lax.shift_right_arithmetic(p, 3) == side)
                low = jnp.where(there, jnp.minimum(low, e), low)
                high = jnp.where(there, jnp.maximum(high, e), high)
        out_ref[0] = own_ref[low, 0]
        out_ref[1] = own_ref[high, 0]


def average_kernel(blocks, where_ref, partner_ref, side_ref, flip_ref, own_ref, prev_ref, next_ref, pick_ref, modal_ref, send_ref, all_ref):
    me, before, after = prev_next(where_ref, blocks)
    reverse = reverse_faces()
    all_ref[0:128] = own_ref[...].reshape(128, 16, 128)
    for k, ref in ((8, prev_ref), (10, next_ref)):
        for i in range(2):
            at = 16 * (k + i)
            all_ref[at : at + 8] = ref[i].reshape(8, 16, 128)
            all_ref[at + 8 : at + 16] = dot(reverse, ref[i]).astype(BF16).reshape(8, 16, 128)
    least = []
    for side in (before, after):
        low = jnp.int32(1 << 30)
        for e in range(8):
            for f in range(4):
                p = partner_ref[e, f]
                there = (p >= 0) & (lax.shift_right_arithmetic(p, 3) == side)
                low = jnp.where(there, jnp.minimum(low, p), low)
        least.append(low)
    pick = pick_ref[...]
    for e in range(8):
        tiles = [None] * 8
        for f in range(4):
            p = partner_ref[e, f]
            home = lax.shift_right_arithmetic(p, 3)
            slot = jnp.where(
                home == me,
                lax.bitwise_and(p, 7),
                jnp.where(home == before, 8 + (p != least[0]).astype(jnp.int32), 10 + (p != least[1]).astype(jnp.int32)),
            )
            place = jnp.where(p >= 0, slot * 16 + flip_ref[e, f] * 8 + side_ref[e, f], 16 * e + f)
            for g in range(2):
                own = all_ref[16 * e + 4 * g + f].astype(F32)
                other = all_ref[place + 4 * g].astype(F32)
                tiles[4 * g + f] = (0.5 * (own + other)).astype(BF16)
        out = dot(pick, jnp.concatenate(tiles, axis=0))
        for h in range(2):
            send_ref[h, e, 112:152, :] = out[40 * h : 40 * h + 40].astype(BF16)


def regroup(blocks):
    rows = blocks[0].shape[0]
    lane = iota((rows, 128), 1) // 32
    out = []
    for c in range(3):
        groups = []
        for first in range(0, len(blocks), 4):
            group = None
            for k in range(4):
                shift = (32 * (k - c)) % 128
                piece = pltpu.roll(blocks[first + k], shift, 1) if shift else blocks[first + k]
                group = piece if group is None else jnp.where(lane == k, piece, group)
            groups.append(group)
        out.append(jnp.concatenate(groups, axis=1))
    return out


def main_kernel(where_ref, metric_ref, got_ref, table_ref, place_ref, synth_ref, analysis_ref, out_ref, field_ref, adv_ref):
    elem, half = where_ref[1], where_ref[2]
    m = [metric_ref[elem, k] for k in range(4)]
    table = table_ref[half]
    place = place_ref[half]
    tails = regroup([got_ref[p, 96:112, :].astype(F32) for p in range(16)])
    faces = regroup([got_ref[p, 112:152, :].astype(F32) for p in range(16)])
    on_face = dot(place, jnp.ones((40, 512), BF16)) > 0.5
    lane = iota((72, 128), 1)
    even = lane % 2 == 0
    for c in range(3):
        modes = jnp.concatenate([got_ref[p, 32 * c : 32 * c + 32, :] for p in range(16)], axis=0)
        d = dot_nt(table[:, 0:128], modes) + dot(table[:, 128:144], tails[c].astype(BF16))
        value = d[0:72].astype(BF16).astype(F32)
        xi, eta = d[72:144], d[144:216]
        turned = []
        for g in range(4):
            v = value[:, 128 * g : 128 * g + 128]
            k = ((lane + 128 * g) // 2).astype(F32) * (1.0 / 32.0)
            turned.append(jnp.where(even, -k * pltpu.roll(v, 127, 1), k * pltpu.roll(v, 1, 1)))
        field_ref[288 * c : 288 * c + 144, :] = jnp.concatenate([value, jnp.concatenate(turned, axis=1)], axis=0).astype(BF16)
        grads = jnp.concatenate([xi * m[0] + eta * m[1], xi * m[2] + eta * m[3]], axis=0)
        grads = jnp.where(on_face, dot(place, faces[c].astype(BF16)), grads)
        field_ref[288 * c + 144 : 288 * c + 288, :] = grads.astype(BF16)
    adv_ref[208:256, :] = jnp.zeros((48, 768), BF16)
    for j in range(0, 768, 256):
        phys = dot(field_ref[...], synth_ref[:, j : j + 256])
        terms = []
        for c in range(3):
            at = 288 * c
            terms.append(
                phys[0:72] * phys[at + 144 : at + 216]
                + phys[288:360] * phys[at + 216 : at + 288]
                + phys[576:648] * phys[at + 72 : at + 144]
            )
        terms.append(jnp.zeros((8, 256), F32))
        adv_ref[0:224, j : j + 256] = jnp.concatenate(terms, axis=0).astype(BF16)
    out = dot_nt(analysis_ref[...], adv_ref[...])
    out_ref[...] = out.astype(BF16).reshape(16, 32, 256)


def unpack_kernel(in_ref, out_ref):
    order = to_element_rows()
    rows, cols = iota((256, 144), 0), iota((256, 144), 1)
    for c in range(3):
        block = None
        for z in range(2):
            pick = jnp.where((rows - 72 * c == cols - 72 * z) & (cols // 72 == z), 1.0, 0.0).astype(BF16)
            part = dot(in_ref[8 * z : 8 * z + 8].reshape(256, 256), pick)
            block = part if block is None else block + part
        block = block.astype(BF16)
        for b in range(2):
            piece = jnp.concatenate([block[32 * e + 16 * b : 32 * e + 16 * b + 16] for e in range(8)], axis=0)
            back = dot_tn(order, piece)
            at = 256 * c + 128 * b
            out_ref[at : at + 128, :] = back.astype(BF16)


SMEM = pl.BlockSpec(memory_space=pltpu.SMEM)
VMEM = pl.BlockSpec(memory_space=pltpu.VMEM)


def call(kernel, in_specs, out_shapes, scratch=(), aliases=None):
    single = not isinstance(out_shapes, (list, tuple)) or hasattr(out_shapes, "shape")
    return pl.pallas_call(
        kernel,
        in_specs=in_specs,
        out_specs=VMEM if single else [VMEM] * len(out_shapes),
        out_shape=out_shapes,
        scratch_shapes=list(scratch),
        compiler_params=pltpu.CompilerParams(vmem_limit_bytes=40 * 1024 * 1024),
        input_output_aliases=aliases or {},
        interpret=INTERPRET,
    )


def shape(*dims):
    return jax.ShapeDtypeStruct(dims, BF16)


def on_device(velocity_modes, metric, face_partner, face_side, face_flip):
    blocks = lax.axis_size("elem")
    position = lax.axis_index("plane")
    where = jnp.stack([lax.axis_index("elem"), position % 8, position // 8]).astype(jnp.int32)
    up = [(i, (i + 1) % blocks) for i in range(blocks)]
    down = [(j, i) for i, j in up]
    synth, analysis = fourier_tables(512, 768)
    modal, own, to_prev, to_next = call(
        functools.partial(pack_kernel, blocks),
        [SMEM, SMEM, SMEM, VMEM, VMEM],
        [shape(2, 8, 152, 128), shape(8, 2, 128, 128), shape(2, 128, 128), shape(2, 128, 128)],
        [pltpu.VMEM((8, 128, 144), BF16)],
    )(where, face_partner, metric, velocity_modes.reshape(768, 144), bf16(trace_table()))
    from_prev = lax.ppermute(to_next, "elem", up)
    from_next = lax.ppermute(to_prev, "elem", down)
    sent = call(
        functools.partial(average_kernel, blocks),
        [SMEM, SMEM, SMEM, SMEM, VMEM, VMEM, VMEM, VMEM, VMEM],
        shape(2, 8, 152, 128),
        [pltpu.VMEM((192, 16, 128), BF16)],
        {8: 0},
    )(where, face_partner, face_side, face_flip, own, from_prev, from_next, bf16(pick_table()), modal)
    got = lax.all_to_all(sent.reshape(16, 152, 128), "plane", 0, 0, tiled=True)
    out = call(
        main_kernel,
        [SMEM, SMEM, VMEM, VMEM, VMEM, VMEM, VMEM],
        shape(16, 32, 256),
        [pltpu.VMEM((864, 512), BF16), pltpu.VMEM((256, 768), BF16)],
    )(where, metric, got, bf16(point_table()), bf16(place_table()), bf16(synth), bf16(analysis))
    out = lax.all_to_all(out, "plane", 0, 0, tiled=True)
    out = call(unpack_kernel, [VMEM], shape(768, 144))(out)
    return out.reshape(3, 32, 8, 144)


def solution(mesh):
    by_elem = P("elem", None)
    whole = P(None, "plane", "elem", None)
    return jax.shard_map(
        on_device,
        mesh=mesh,
        in_specs=(whole, by_elem, by_elem, by_elem, by_elem),
        out_specs=whole,
        check_vma=False,
    )
```

time: 112 us -> 69.2 us (0.62)
  the two profiles are of different devices: /device:TPU:18 before, /device:TPU:2 now
where the time goes in v1:
time: 69.2 us; the launch traced here: 68.8 us
  blocking collectives  35 us (51%)
  starting transfers between devices  21.5 us (31%)
  Pallas kernels  6.95 us (10%)
  local copies, waits for them, and re-layouts  3.55 us (5%)
  waiting for transfers between devices  1.71 us (2%)
    all_to_all x1, blocking collectives, on_device(): got = lax.all_to_all(sent.reshape(16, 152, 128), 'plane', 0, 0, tiled=True)  22.5 us
    ppermute x1, starting transfers between devices, on_device(): from_next = lax.ppermute(to_prev, 'elem', down)  19.5 us
    all_to_all x1, blocking collectives, on_device(): out = lax.all_to_all(out, 'plane', 0, 0, tiled=True)  12.5 us
    unnamed x26, local copies, waits for them, and re-layouts  3.55 us
    pallas_call x1, Pallas kernels, on_device(): call(main_kernel, [SMEM, SMEM, VMEM, VMEM, VMEM, VMEM, VMEM], shape(16, 3...  2.47 us
    ppermute x1, starting transfers between devices, on_device(): from_prev = lax.ppermute(to_next, 'elem', up)  1.92 us
    pallas_call x1, Pallas kernels, on_device(): out = call(unpack_kernel, [VMEM], shape(768, 144))(out)  1.77 us
    ppermute x1, waiting for transfers between devices, on_device(): from_next = lax.ppermute(to_prev, 'elem', down)  1.49 us
  transfers between devices with their start and end apart: 2, of which 2 were waited for; matrix products, arithmetic and copies ran while one was open for 0% of the time, Pallas kernels for 0%

profile of v1, /device:TPU:2, one launch (start us, length us, event | category | flops | bytes accessed | tf_op | source)
XLA Modules:
  0.0 68.8 jit_solution(3798307203115195274)
XLA Ops:
  0.0 0.0 copy-start.7
  0.0 0.7 copy-done.7
  0.7 0.0 copy-start.8
  0.7 0.1 copy.18.metric_ref
  0.8 0.6 copy-done.8
  1.4 0.1 copy.15.partner_ref
  1.4 0.1 pad_add_fusion.where_ref
  1.5 0.0 copy-start.2
  1.5 1.0 %copy-done.2 = bf16[3,32,8,144]{3,2,1,0:T(8,128)(2,1)S(1)} copy-done((bf16[3,32,8,144]{3,2,1,0:T(8,128)(2,1)S(1)}, bf16[3,32,8,144]{3,2,1,0:T(8,128)(2,1)}, u32[]{:S(2)}) %copy-start.2) | copy-done | bytes 221208
  2.5 0.0 copy-start.4
  2.5 0.9 %copy-done.4 = bf16[272,144]{1,0:T(8,128)(2,1)S(1)} copy-done((bf16[272,144]{1,0:T(8,128)(2,1)S(1)}, bf16[272,144]{1,0:T(8,128)(2,1)}, u32[]{:S(2)}) %copy-start.4) | copy-done | bytes 78360
  3.4 0.0 copy-start.6
  3.4 1.4 %shard_map.109 = (bf16[2,8,152,128]{3,2,1,0:T(8,128)(2,1)S(1)}, bf16[8,2,128,128]{3,2,1,0:T(8,128)(2,1)S(1)}, bf16[2,128,128]{2,1,0:T(8,128)(2,1)S(1)}, bf16[2,128,128]{2,1,0:T(8,128)(2,1)S(1)}) custom-call(s32[3]{0:T(128)S(1)} %pad_add_fusion.where_ref, s32[8,4]{1,0:T(8,128)S(1)} %copy.15.partner_ref, f32[8,4]{1,0:T(8,128)S(1)} %copy.18.metric_ref, ...), custom_call_target="tpu_custom_call" | custom-call | tf_op jit(solution)/shard_map/pallas_call | solution.py:296
  4.8 0.0 copy-start.9
  4.8 1.9 %collective-permute-start = (bf16[2,128,128]{2,1,0:T(8,128)(2,1)S(1)}, bf16[2,128,128]{2,1,0:T(8,128)(2,1)S(1)}, u32[]{:S(2)}, u32[]{:S(2)}) collective-permute-start(bf16[2,128,128]{2,1,0:T(8,128)(2,1)S(1)} %get-tuple-element.10), channel_id=1, source_target_pairs={{0,16},{16,32},{32,48},{48,64},{64,80},{80,96},{96,112},{112,128},... | collective-permute-start | bytes 196616 | tf_op jit(solution)/shard_map/ppermute | solution.py:302
  6.8 0.0 copy-start.10
  6.8 19.5 %collective-permute-start.1 = (bf16[2,128,128]{2,1,0:T(8,128)(2,1)S(1)}, bf16[2,128,128]{2,1,0:T(8,128)(2,1)S(1)}, u32[]{:S(2)}, u32[]{:S(2)}) collective-permute-start(bf16[2,128,128]{2,1,0:T(8,128)(2,1)S(1)} %get-tuple-element.11), channel_id=1, source_target_pairs={{16,0},{32,16},{48,32},{64,48},{80,64},{96,80},{112,96},{128,112},... | collective-permute-start | bytes 196616 | tf_op jit(solution)/shard_map/ppermute | solution.py:303
  26.3 0.0 copy-done.9
  26.3 0.1 copy.16.side_ref
  26.4 0.0 copy-done.10
  26.4 0.1 copy.17.flip_ref
  26.5 0.2 collective-permute-done.prev_ref
  26.7 1.5 %collective-permute-done.1.next_ref = bf16[2,128,128]{2,1,0:T(8,128)(2,1)S(1)} collective-permute-done((bf16[2,128,128]{2,1,0:T(8,128)(2,1)S(1)}, bf16[2,128,128]{2,1,0:T(8,128)(2,1)S(1)}, u32[]{:S(2)}, u32[]{:S(2)}) %collective-permute-start.1) | collective-permute-done | bytes 65568 | tf_op jit(solution)/shard_map/ppermute | solution.py:303
  28.2 0.0 copy-done.6
  28.2 0.0 copy-start.1
  28.2 1.3 %shard_map.110 = bf16[2,8,152,128]{3,2,1,0:T(8,128)(2,1)S(1)} custom-call(s32[3]{0:T(128)S(1)} %pad_add_fusion.where_ref, s32[8,4]{1,0:T(8,128)S(1)} %copy.15.partner_ref, s32[8,4]{1,0:T(8,128)S(1)} %copy.16.side_ref, s32[8,4]{1,0:T(8,128)S(1)} %copy.17.flip_ref, ...), custom_call_target="tpu_custom_call", output_to_operand_aliasing={{}: (8, {})} | custom-call | tf_op jit(solution)/shard_map/pallas_call | solution.py:304
  29.5 0.0 copy-start
  29.5 0.0 copy-start.3
  29.6 0.0 copy-start.5
  29.6 22.5 %all_to_all.10.got_ref = bf16[16,152,128]{2,1,0:T(8,128)(2,1)S(1)} all-to-all(bf16[16,152,128]{2,1,0:T(8,128)(2,1)S(1)} %bitcast.6), channel_id=1, replica_groups=mesh['elem'=64,'plane'=16] {'plane'}, dimensions={0} | all-to-all | bytes 1245184 | tf_op jit(solution)/shard_map/all_to_all | solution.py:311
  52.1 0.0 copy-done.1
  52.1 0.0 copy-done
  52.1 0.0 copy-done.3
  52.1 0.0 copy-done.5
  52.1 2.5 %shard_map.111 = bf16[16,32,256]{2,1,0:T(8,128)(2,1)S(1)} custom-call(s32[3]{0:T(128)S(1)} %pad_add_fusion.where_ref, f32[8,4]{1,0:T(8,128)S(1)} %copy.18.metric_ref, bf16[16,152,128]{2,1,0:T(8,128)(2,1)S(1)} %all_to_all.10.got_ref, bf16[2,216,144]{2,1,0:T(8,128)(2,1)S(1)} %copy-done.3, bf16[2,144,40]{2,1,0:T(8,128)(2,1)S(1)} %copy-done.5, ...), custom_call_target="tpu_custom_call" | custom-call | tf_op jit(solution)/shard_map/pallas_call | solution.py:312
  54.6 12.5 %all_to_all.11.in_ref = bf16[16,32,256]{2,1,0:T(8,128)(2,1)S(1)} all-to-all(bf16[16,32,256]{2,1,0:T(8,128)(2,1)S(1)} %shard_map.111), channel_id=1, replica_groups=mesh['elem'=64,'plane'=16] {'plane'}, dimensions={0} | all-to-all | bytes 524288 | tf_op jit(solution)/shard_map/all_to_all | solution.py:318
  67.1 1.8 %shard_map.112 = bf16[768,144]{1,0:T(8,128)(2,1)} custom-call(bf16[16,32,256]{2,1,0:T(8,128)(2,1)S(1)} %all_to_all.11.in_ref), custom_call_target="tpu_custom_call" | custom-call | tf_op jit(solution)/shard_map/pallas_call | solution.py:319
Async XLA Ops:
  0.0 0.7 copy-start.7
  0.7 0.7 copy-start.8
  1.5 1.0 %copy-start.2 = (bf16[3,32,8,144]{3,2,1,0:T(8,128)(2,1)S(1)}, bf16[3,32,8,144]{3,2,1,0:T(8,128)(2,1)}, u32[]{:S(2)}) copy-start(bf16[3,32,8,144]{3,2,1,0:T(8,128)(2,1)} %param.11) | copy-start | bytes 663556
  2.5 0.9 %copy-start.4 = (bf16[272,144]{1,0:T(8,128)(2,1)S(1)}, bf16[272,144]{1,0:T(8,128)(2,1)}, u32[]{:S(2)}) copy-start(bf16[272,144]{1,0:T(8,128)(2,1)} %constant.58.table_ref) | copy-start | bytes 235012
  3.4 24.8 %copy-start.6 = (bf16[80,128]{1,0:T(8,128)(2,1)S(1)}, bf16[80,128]{1,0:T(8,128)(2,1)}, u32[]{:S(2)}) copy-start(bf16[80,128]{1,0:T(8,128)(2,1)} %constant.59.pick_ref) | copy-start | bytes 61444
  4.8 21.5 %copy-start.9 = (s32[8,4]{0,1:T(4,128)S(1)}, s32[8,4]{0,1:T(4,128)}, u32[]{:S(2)}) copy-start(s32[8,4]{0,1:T(4,128)} %param.14) | copy-start | bytes 388
  4.8 21.9 %collective-permute-start = (bf16[2,128,128]{2,1,0:T(8,128)(2,1)S(1)}, bf16[2,128,128]{2,1,0:T(8,128)(2,1)S(1)}, u32[]{:S(2)}, u32[]{:S(2)}) collective-permute-start(bf16[2,128,128]{2,1,0:T(8,128)(2,1)S(1)} %get-tuple-element.10), channel_id=1, source_target_pairs={{0,16},{16,32},{32,48},{48,64},{64,80},{80,96},{96,112},{112,128},... | collective-permute-start | bytes 196616 | tf_op jit(solution)/shard_map/ppermute | solution.py:302
  6.8 19.6 %copy-start.10 = (s32[8,4]{0,1:T(4,128)S(1)}, s32[8,4]{0,1:T(4,128)}, u32[]{:S(2)}) copy-start(s32[8,4]{0,1:T(4,128)} %param.15) | copy-start | bytes 388
  6.8 21.4 %collective-permute-start.1 = (bf16[2,128,128]{2,1,0:T(8,128)(2,1)S(1)}, bf16[2,128,128]{2,1,0:T(8,128)(2,1)S(1)}, u32[]{:S(2)}, u32[]{:S(2)}) collective-permute-start(bf16[2,128,128]{2,1,0:T(8,128)(2,1)S(1)} %get-tuple-element.11), channel_id=1, source_target_pairs={{16,0},{32,16},{48,32},{64,48},{80,64},{96,80},{112,96},{128,112},... | collective-permute-start | bytes 196616 | tf_op jit(solution)/shard_map/ppermute | solution.py:303
  28.2 23.9 %copy-start.1 = (bf16[512,768]{1,0:T(8,128)(2,1)S(1)}, bf16[512,768]{1,0:T(8,128)(2,1)}, u32[]{:S(2)}) copy-start(bf16[512,768]{1,0:T(8,128)(2,1)} %constant.62.synth_ref) | copy-start | bytes 2359300
  29.5 22.6 %copy-start = (bf16[512,768]{1,0:T(8,128)(2,1)S(1)}, bf16[512,768]{1,0:T(8,128)(2,1)}, u32[]{:S(2)}) copy-start(bf16[512,768]{1,0:T(8,128)(2,1)} %constant.63.analysis_ref) | copy-start | bytes 2359300
  29.5 22.6 %copy-start.3 = (bf16[2,216,144]{2,1,0:T(8,128)(2,1)S(1)}, bf16[2,216,144]{2,1,0:T(8,128)(2,1)}, u32[]{:S(2)}) copy-start(bf16[2,216,144]{2,1,0:T(8,128)(2,1)} %constant.60.table_ref) | copy-start | bytes 373252
  29.6 22.6 %copy-start.5 = (bf16[2,144,40]{2,1,0:T(8,128)(2,1)S(1)}, bf16[2,144,40]{2,1,0:T(8,128)(2,1)}, u32[]{:S(2)}) copy-start(bf16[2,144,40]{2,1,0:T(8,128)(2,1)} %constant.61.place_ref) | copy-start | bytes 69124

commit v2 on v1

--- a/solution.py
+++ b/solution.py
@@ -7,6 +7,7 @@
 from jax.experimental import pallas as pl
 from jax.experimental.pallas import tpu as pltpu
 from jax.sharding import PartitionSpec as P
+
 
 F32, BF16 = jnp.float32, jnp.bfloat16
 NT = (((1,), (1,)), ((), ()))
@@ -137,7 +138,7 @@
             for g in range(2):
                 grad = xi * metric_ref[e, 2 * g] + eta * metric_ref[e, 2 * g + 1]
                 own_ref[e, flip, 64 * g : 64 * g + 64, :] = grad.astype(BF16)
-    me, before, after = prev_next(where_ref, blocks)
+    _, before, after = prev_next(where_ref, blocks)
     for side, out_ref in ((before, prev_ref), (after, next_ref)):
         low, high = jnp.int32(7), jnp.int32(0)
         for e in range(8):
@@ -150,7 +151,7 @@
         out_ref[1] = own_ref[high, 0]
 
 
-def average_kernel(blocks, where_ref, partner_ref, side_ref, flip_ref, own_ref, prev_ref, next_ref, pick_ref, modal_ref, send_ref, all_ref):
+def average_kernel(blocks, where_ref, partner_ref, side_ref, flip_ref, own_ref, prev_ref, next_ref, pick_ref, face_ref, all_ref):
     me, before, after = prev_next(where_ref, blocks)
     reverse = reverse_faces()
     all_ref[0:128] = own_ref[...].reshape(128, 16, 128)
@@ -186,7 +187,7 @@
                 tiles[4 * g + f] = (0.5 * (own + other)).astype(BF16)
         out = dot(pick, jnp.concatenate(tiles, axis=0))
         for h in range(2):
-            send_ref[h, e, 112:152, :] = out[40 * h : 40 * h + 40].astype(BF16)
+            face_ref[h, e] = out[40 * h : 40 * h + 40].astype(BF16)
 
 
 def regroup(blocks):
@@ -206,18 +207,18 @@
     return out
 
 
-def main_kernel(where_ref, metric_ref, got_ref, table_ref, place_ref, synth_ref, analysis_ref, out_ref, field_ref, adv_ref):
+def main_kernel(where_ref, metric_ref, modal_ref, face_ref, table_ref, place_ref, synth_ref, analysis_ref, out_ref, field_ref, adv_ref):
     elem, half = where_ref[1], where_ref[2]
     m = [metric_ref[elem, k] for k in range(4)]
     table = table_ref[half]
     place = place_ref[half]
-    tails = regroup([got_ref[p, 96:112, :].astype(F32) for p in range(16)])
-    faces = regroup([got_ref[p, 112:152, :].astype(F32) for p in range(16)])
+    tails = regroup([modal_ref[p, 96:112, :].astype(F32) for p in range(16)])
+    faces = regroup([face_ref[p].astype(F32) for p in range(16)])
     on_face = dot(place, jnp.ones((40, 512), BF16)) > 0.5
     lane = iota((72, 128), 1)
     even = lane % 2 == 0
     for c in range(3):
-        modes = jnp.concatenate([got_ref[p, 32 * c : 32 * c + 32, :] for p in range(16)], axis=0)
+        modes = jnp.concatenate([modal_ref[p, 32 * c : 32 * c + 32, :] for p in range(16)], axis=0)
         d = dot_nt(table[:, 0:128], modes) + dot(table[:, 128:144], tails[c].astype(BF16))
         value = d[0:72].astype(BF16).astype(F32)
         xi, eta = d[72:144], d[144:216]
@@ -268,7 +269,7 @@
 VMEM = pl.BlockSpec(memory_space=pltpu.VMEM)
 
 
-def call(kernel, in_specs, out_shapes, scratch=(), aliases=None):
+def call(kernel, in_specs, out_shapes, scratch=()):
     single = not isinstance(out_shapes, (list, tuple)) or hasattr(out_shapes, "shape")
     return pl.pallas_call(
         kernel,
@@ -277,7 +278,6 @@
         out_shape=out_shapes,
         scratch_shapes=list(scratch),
         compiler_params=pltpu.CompilerParams(vmem_limit_bytes=40 * 1024 * 1024),
-        input_output_aliases=aliases or {},
         interpret=INTERPRET,
     )
 
@@ -296,25 +296,25 @@
     modal, own, to_prev, to_next = call(
         functools.partial(pack_kernel, blocks),
         [SMEM, SMEM, SMEM, VMEM, VMEM],
-        [shape(2, 8, 152, 128), shape(8, 2, 128, 128), shape(2, 128, 128), shape(2, 128, 128)],
+        [shape(2, 8, 112, 128), shape(8, 2, 128, 128), shape(2, 128, 128), shape(2, 128, 128)],
         [pltpu.VMEM((8, 128, 144), BF16)],
     )(where, face_partner, metric, velocity_modes.reshape(768, 144), bf16(trace_table()))
     from_prev = lax.ppermute(to_next, "elem", up)
     from_next = lax.ppermute(to_prev, "elem", down)
-    sent = call(
+    modal = lax.all_to_all(modal.reshape(16, 112, 128), "plane", 0, 0, tiled=True)
+    faces = call(
         functools.partial(average_kernel, blocks),
-        [SMEM, SMEM, SMEM, SMEM, VMEM, VMEM, VMEM, VMEM, VMEM],
-        shape(2, 8, 152, 128),
+        [SMEM, SMEM, SMEM, SMEM, VMEM, VMEM, VMEM, VMEM],
+        shape(2, 8, 40, 128),
         [pltpu.VMEM((192, 16, 128), BF16)],
-        {8: 0},
-    )(where, face_partner, face_side, face_flip, own, from_prev, from_next, bf16(pick_table()), modal)
-    got = lax.all_to_all(sent.reshape(16, 152, 128), "plane", 0, 0, tiled=True)
+    )(where, face_partner, face_side, face_flip, own, from_prev, from_next, bf16(pick_table()))
+    faces = lax.all_to_all(faces.reshape(16, 40, 128), "plane", 0, 0, tiled=True)
     out = call(
         main_kernel,
-        [SMEM, SMEM, VMEM, VMEM, VMEM, VMEM, VMEM],
+        [SMEM, SMEM, VMEM, VMEM, VMEM, VMEM, VMEM, VMEM],
         shape(16, 32, 256),
         [pltpu.VMEM((864, 512), BF16), pltpu.VMEM((256, 768), BF16)],
-    )(where, metric, got, bf16(point_table()), bf16(place_table()), bf16(synth), bf16(analysis))
+    )(where, metric, modal, faces, bf16(point_table()), bf16(place_table()), bf16(synth), bf16(analysis))
     out = lax.all_to_all(out, "plane", 0, 0, tiled=True)
     out = call(unpack_kernel, [VMEM], shape(768, 144))(out)
     return out.reshape(3, 32, 8, 144)

time: 69.2 us -> 82.2 us (1.19)
  blocking collectives: 35 us -> 47.9 us
    all_to_all x1 -> x2, blocking collectives: 22.5 us -> 32.7 us  [the longest x1 17.4 us: on_device(): lax.all_to_all(faces.reshape(16, 40, 128), 'plane', 0, 0, tiled=True)]
    all_to_all x1, blocking collectives: 12.5 us -> 15.2 us  [on_device(): out = lax.all_to_all(out, 'plane', 0, 0, tiled=True)]
where the time goes in v2:
time: 82.2 us; the launch traced here: 81.8 us
  blocking collectives  47.9 us (58%)
  starting transfers between devices  21.5 us (26%)
  Pallas kernels  6.96 us (8%)
  local copies, waits for them, and re-layouts  3.54 us (4%)
  waiting for transfers between devices  1.71 us (2%)
    ppermute x1, starting transfers between devices, on_device(): from_next = lax.ppermute(to_prev, 'elem', down)  19.5 us
    all_to_all x1, blocking collectives, on_device(): lax.all_to_all(faces.reshape(16, 40, 128), 'plane', 0, 0, tiled=True)  17.4 us
    all_to_all x1, blocking collectives, on_device(): lax.all_to_all(modal.reshape(16, 112, 128), 'plane', 0, 0, tiled=True)  15.4 us
    all_to_all x1, blocking collectives, on_device(): out = lax.all_to_all(out, 'plane', 0, 0, tiled=True)  15.2 us
    unnamed x26, local copies, waits for them, and re-layouts  3.54 us
    pallas_call x1, Pallas kernels, on_device(): call(main_kernel, [SMEM, SMEM, VMEM, VMEM, VMEM, VMEM, VMEM, VMEM], shape...  2.48 us
    ppermute x1, starting transfers between devices, on_device(): from_prev = lax.ppermute(to_next, 'elem', up)  1.92 us
    pallas_call x1, Pallas kernels, on_device(): out = call(unpack_kernel, [VMEM], shape(768, 144))(out)  1.77 us
  transfers between devices with their start and end apart: 2, of which 2 were waited for; matrix products, arithmetic and copies ran while one was open for 0% of the time, Pallas kernels for 0%

profile of v2, /device:TPU:2, one launch (start us, length us, event | category | flops | bytes accessed | tf_op | source)
XLA Modules:
  0.0 81.8 jit_solution(8666421846425828881)
XLA Ops:
  0.0 0.0 copy-start.7
  0.0 0.7 copy-done.7
  0.7 0.0 copy-start.8
  0.7 0.1 copy.12.partner_ref
  0.8 0.6 copy-done.8
  1.4 0.1 copy.17.metric_ref
  1.4 0.1 pad_add_fusion.where_ref
  1.5 0.0 copy-start.2
  1.5 1.0 %copy-done.2 = bf16[3,32,8,144]{3,2,1,0:T(8,128)(2,1)S(1)} copy-done((bf16[3,32,8,144]{3,2,1,0:T(8,128)(2,1)S(1)}, bf16[3,32,8,144]{3,2,1,0:T(8,128)(2,1)}, u32[]{:S(2)}) %copy-start.2) | copy-done | bytes 221208
  2.5 0.0 copy-start.4
  2.5 0.9 %copy-done.4 = bf16[272,144]{1,0:T(8,128)(2,1)S(1)} copy-done((bf16[272,144]{1,0:T(8,128)(2,1)S(1)}, bf16[272,144]{1,0:T(8,128)(2,1)}, u32[]{:S(2)}) %copy-start.4) | copy-done | bytes 78360
  3.4 0.0 copy-start.6
  3.4 1.4 %shard_map.109 = (bf16[2,8,112,128]{3,2,1,0:T(8,128)(2,1)S(1)}, bf16[8,2,128,128]{3,2,1,0:T(8,128)(2,1)S(1)}, bf16[2,128,128]{2,1,0:T(8,128)(2,1)S(1)}, bf16[2,128,128]{2,1,0:T(8,128)(2,1)S(1)}) custom-call(s32[3]{0:T(128)S(1)} %pad_add_fusion.where_ref, s32[8,4]{1,0:T(8,128)S(1)} %copy.12.partner_ref, f32[8,4]{1,0:T(8,128)S(1)} %copy.17.metric_ref, ...), custom_call_target="tpu_custom_call" | custom-call | tf_op jit(solution)/shard_map/pallas_call | solution.py:296
  4.8 0.0 copy-start.9
  4.8 1.9 %collective-permute-start = (bf16[2,128,128]{2,1,0:T(8,128)(2,1)S(1)}, bf16[2,128,128]{2,1,0:T(8,128)(2,1)S(1)}, u32[]{:S(2)}, u32[]{:S(2)}) collective-permute-start(bf16[2,128,128]{2,1,0:T(8,128)(2,1)S(1)} %get-tuple-element.11), channel_id=1, source_target_pairs={{0,16},{16,32},{32,48},{48,64},{64,80},{80,96},{96,112},{112,128},... | collective-permute-start | bytes 196616 | tf_op jit(solution)/shard_map/ppermute | solution.py:302
  6.8 0.0 copy-start.10
  6.8 19.5 %collective-permute-start.1 = (bf16[2,128,128]{2,1,0:T(8,128)(2,1)S(1)}, bf16[2,128,128]{2,1,0:T(8,128)(2,1)S(1)}, u32[]{:S(2)}, u32[]{:S(2)}) collective-permute-start(bf16[2,128,128]{2,1,0:T(8,128)(2,1)S(1)} %get-tuple-element.12), channel_id=1, source_target_pairs={{16,0},{32,16},{48,32},{64,48},{80,64},{96,80},{112,96},{128,112},... | collective-permute-start | bytes 196616 | tf_op jit(solution)/shard_map/ppermute | solution.py:303
  26.3 0.0 copy-done.9
  26.3 0.1 copy.15.side_ref
  26.4 0.0 copy-done.10
  26.4 0.1 copy.16.flip_ref
  26.5 0.2 collective-permute-done.prev_ref
  26.7 1.5 %collective-permute-done.1.next_ref = bf16[2,128,128]{2,1,0:T(8,128)(2,1)S(1)} collective-permute-done((bf16[2,128,128]{2,1,0:T(8,128)(2,1)S(1)}, bf16[2,128,128]{2,1,0:T(8,128)(2,1)S(1)}, u32[]{:S(2)}, u32[]{:S(2)}) %collective-permute-start.1) | collective-permute-done | bytes 65568 | tf_op jit(solution)/shard_map/ppermute | solution.py:303
  28.2 0.0 copy-done.6
  28.2 0.0 copy-start.1
  28.2 1.3 %shard_map.110 = bf16[2,8,40,128]{3,2,1,0:T(8,128)(2,1)S(1)} custom-call(s32[3]{0:T(128)S(1)} %pad_add_fusion.where_ref, s32[8,4]{1,0:T(8,128)S(1)} %copy.12.partner_ref, s32[8,4]{1,0:T(8,128)S(1)} %copy.15.side_ref, s32[8,4]{1,0:T(8,128)S(1)} %copy.16.flip_ref, bf16[8,2,128,128]{3,2,1,0:T(8,128)(2,1)S(1)} %get-tuple-element.10.own_ref, ...), custom_call_target="tpu_custom_call" | custom-call | tf_op jit(solution)/shard_map/pallas_call | solution.py:305
  29.5 0.0 copy-start
  29.5 17.4 %all_to_all.15.face_ref = bf16[16,40,128]{2,1,0:T(8,128)(2,1)S(1)} all-to-all(bf16[16,40,128]{2,1,0:T(8,128)(2,1)S(1)} %bitcast.7), channel_id=1, replica_groups=mesh['elem'=64,'plane'=16] {'plane'}, dimensions={0} | all-to-all | bytes 327680 | tf_op jit(solution)/shard_map/all_to_all | solution.py:311
  46.9 0.0 copy-start.3
  46.9 0.0 copy-start.5
  46.9 15.4 %all_to_all.16.modal_ref = bf16[16,112,128]{2,1,0:T(8,128)(2,1)S(1)} all-to-all(bf16[16,112,128]{2,1,0:T(8,128)(2,1)S(1)} %bitcast.8), channel_id=1, replica_groups=mesh['elem'=64,'plane'=16] {'plane'}, dimensions={0} | all-to-all | bytes 917504 | tf_op jit(solution)/shard_map/all_to_all | solution.py:304
  62.3 0.0 copy-done.1
  62.3 0.0 copy-done
  62.3 0.0 copy-done.3
  62.3 0.0 copy-done.5
  62.3 2.5 %shard_map.111 = bf16[16,32,256]{2,1,0:T(8,128)(2,1)S(1)} custom-call(s32[3]{0:T(128)S(1)} %pad_add_fusion.where_ref, f32[8,4]{1,0:T(8,128)S(1)} %copy.17.metric_ref, bf16[16,112,128]{2,1,0:T(8,128)(2,1)S(1)} %all_to_all.16.modal_ref, bf16[16,40,128]{2,1,0:T(8,128)(2,1)S(1)} %all_to_all.15.face_ref, bf16[2,216,144]{2,1,0:T(8,128)(2,1)S(1)} %copy-done.3, ...), custom_call_target="tpu_custom_call" | custom-call | tf_op jit(solution)/shard_map/pallas_call | solution.py:312
  64.8 15.2 %all_to_all.17.in_ref = bf16[16,32,256]{2,1,0:T(8,128)(2,1)S(1)} all-to-all(bf16[16,32,256]{2,1,0:T(8,128)(2,1)S(1)} %shard_map.111), channel_id=1, replica_groups=mesh['elem'=64,'plane'=16] {'plane'}, dimensions={0} | all-to-all | bytes 524288 | tf_op jit(solution)/shard_map/all_to_all | solution.py:318
  80.0 1.8 %shard_map.112 = bf16[768,144]{1,0:T(8,128)(2,1)} custom-call(bf16[16,32,256]{2,1,0:T(8,128)(2,1)S(1)} %all_to_all.17.in_ref), custom_call_target="tpu_custom_call" | custom-call | tf_op jit(solution)/shard_map/pallas_call | solution.py:319
Async XLA Ops:
  0.0 0.7 copy-start.7
  0.7 0.7 copy-start.8
  1.5 1.0 %copy-start.2 = (bf16[3,32,8,144]{3,2,1,0:T(8,128)(2,1)S(1)}, bf16[3,32,8,144]{3,2,1,0:T(8,128)(2,1)}, u32[]{:S(2)}) copy-start(bf16[3,32,8,144]{3,2,1,0:T(8,128)(2,1)} %param.11) | copy-start | bytes 663556
  2.5 0.9 %copy-start.4 = (bf16[272,144]{1,0:T(8,128)(2,1)S(1)}, bf16[272,144]{1,0:T(8,128)(2,1)}, u32[]{:S(2)}) copy-start(bf16[272,144]{1,0:T(8,128)(2,1)} %constant.58.table_ref) | copy-start | bytes 235012
  3.4 24.8 %copy-start.6 = (bf16[80,128]{1,0:T(8,128)(2,1)S(1)}, bf16[80,128]{1,0:T(8,128)(2,1)}, u32[]{:S(2)}) copy-start(bf16[80,128]{1,0:T(8,128)(2,1)} %constant.59.pick_ref) | copy-start | bytes 61444
  4.8 21.5 %copy-start.9 = (s32[8,4]{0,1:T(4,128)S(1)}, s32[8,4]{0,1:T(4,128)}, u32[]{:S(2)}) copy-start(s32[8,4]{0,1:T(4,128)} %param.14) | copy-start | bytes 388
  4.8 21.9 %collective-permute-start = (bf16[2,128,128]{2,1,0:T(8,128)(2,1)S(1)}, bf16[2,128,128]{2,1,0:T(8,128)(2,1)S(1)}, u32[]{:S(2)}, u32[]{:S(2)}) collective-permute-start(bf16[2,128,128]{2,1,0:T(8,128)(2,1)S(1)} %get-tuple-element.11), channel_id=1, source_target_pairs={{0,16},{16,32},{32,48},{48,64},{64,80},{80,96},{96,112},{112,128},... | collective-permute-start | bytes 196616 | tf_op jit(solution)/shard_map/ppermute | solution.py:302
  6.8 19.6 %copy-start.10 = (s32[8,4]{0,1:T(4,128)S(1)}, s32[8,4]{0,1:T(4,128)}, u32[]{:S(2)}) copy-start(s32[8,4]{0,1:T(4,128)} %param.15) | copy-start | bytes 388
  6.8 21.4 %collective-permute-start.1 = (bf16[2,128,128]{2,1,0:T(8,128)(2,1)S(1)}, bf16[2,128,128]{2,1,0:T(8,128)(2,1)S(1)}, u32[]{:S(2)}, u32[]{:S(2)}) collective-permute-start(bf16[2,128,128]{2,1,0:T(8,128)(2,1)S(1)} %get-tuple-element.12), channel_id=1, source_target_pairs={{16,0},{32,16},{48,32},{64,48},{80,64},{96,80},{112,96},{128,112},... | collective-permute-start | bytes 196616 | tf_op jit(solution)/shard_map/ppermute | solution.py:303
  28.2 34.1 %copy-start.1 = (bf16[512,768]{1,0:T(8,128)(2,1)S(1)}, bf16[512,768]{1,0:T(8,128)(2,1)}, u32[]{:S(2)}) copy-start(bf16[512,768]{1,0:T(8,128)(2,1)} %constant.63.analysis_ref) | copy-start | bytes 2359300
  29.5 32.7 %copy-start = (bf16[512,768]{1,0:T(8,128)(2,1)S(1)}, bf16[512,768]{1,0:T(8,128)(2,1)}, u32[]{:S(2)}) copy-start(bf16[512,768]{1,0:T(8,128)(2,1)} %constant.62.synth_ref) | copy-start | bytes 2359300
  46.9 15.4 %copy-start.3 = (bf16[2,216,144]{2,1,0:T(8,128)(2,1)S(1)}, bf16[2,216,144]{2,1,0:T(8,128)(2,1)}, u32[]{:S(2)}) copy-start(bf16[2,216,144]{2,1,0:T(8,128)(2,1)} %constant.60.table_ref) | copy-start | bytes 373252
  46.9 15.4 %copy-start.5 = (bf16[2,144,40]{2,1,0:T(8,128)(2,1)S(1)}, bf16[2,144,40]{2,1,0:T(8,128)(2,1)}, u32[]{:S(2)}) copy-start(bf16[2,144,40]{2,1,0:T(8,128)(2,1)} %constant.61.place_ref) | copy-start | bytes 69124

commit v3 on v1

--- a/solution.py
+++ b/solution.py
@@ -90,12 +90,12 @@
 
 def to_element_rows():
     out, inp = iota((128, 128), 0), iota((128, 128), 1)
-    return jnp.where(inp == (out % 16) * 8 + out // 16, 1.0, 0.0).astype(BF16)
+    return jnp.where(inp == ((out & 15) << 3) + (out >> 4), 1.0, 0.0).astype(BF16)
 
 
 def reverse_faces():
     out, inp = iota((128, 128), 0), iota((128, 128), 1)
-    t = out % 16
+    t = out & 15
     return jnp.where((t < 12) & (inp == out - t + 11 - t), 1.0, 0.0).astype(BF16)
 
 
@@ -116,82 +116,106 @@
     return me, jnp.where(me == 0, blocks - 1, me - 1), jnp.where(me == blocks - 1, 0, me + 1)
 
 
-def pack_kernel(blocks, where_ref, partner_ref, metric_ref, v_ref, table_ref, modal_ref, own_ref, prev_ref, next_ref, rows_ref):
+def trace_kernel(blocks, where_ref, partner_hbm, metric_hbm, v_hbm, table_hbm, rows_ref, tail_ref, own_ref, prev_ref, next_ref, partner_ref, metric_ref, v_ref, table_ref, sems):
+    copies = [
+        pltpu.make_async_copy(src, dst, sems.at[i])
+        for i, (src, dst) in enumerate(((v_hbm, v_ref), (table_hbm, table_ref), (metric_hbm, metric_ref), (partner_hbm, partner_ref)))
+    ]
+    for copy in copies:
+        copy.start()
     order = to_element_rows()
     rows_ref[:, 96:128, :] = jnp.zeros((8, 32, 144), BF16)
+    for copy in copies:
+        copy.wait()
     for b in range(6):
         block = dot(order, v_ref[128 * b : 128 * b + 128, :]).astype(BF16)
         for e in range(8):
             rows_ref[e, 16 * b : 16 * b + 16, :] = block[16 * e : 16 * e + 16]
     table = table_ref[...]
     for e in range(8):
-        rows = rows_ref[e]
-        out = dot_nt(table, rows)
-        tail = out[0:16].astype(BF16)
-        for z in range(2):
-            modal_ref[z, e, 0:96, :] = rows[0:96, 0:128]
-            modal_ref[z, e, 96:112, :] = tail
+        out = dot_nt(table, rows_ref[e])
+        tail_ref[e] = out[0:16].astype(BF16)
         for flip in range(2):
             xi = out[16 + 128 * flip : 80 + 128 * flip]
             eta = out[80 + 128 * flip : 144 + 128 * flip]
             for g in range(2):
-                grad = xi * metric_ref[e, 2 * g] + eta * metric_ref[e, 2 * g + 1]
-                own_ref[e, flip, 64 * g : 64 * g + 64, :] = grad.astype(BF16)
-    me, before, after = prev_next(where_ref, blocks)
+                grad = xi * metric_ref[2 * g, e] + eta * metric_ref[2 * g + 1, e]
+                at = 16 * e + 8 * flip + 4 * g
+                own_ref[at : at + 4] = grad.astype(BF16).reshape(4, 16, 128)
+    _, before, after = prev_next(where_ref, blocks)
     for side, out_ref in ((before, prev_ref), (after, next_ref)):
         low, high = jnp.int32(7), jnp.int32(0)
         for e in range(8):
-            for f in range(4):
-                p = partner_ref[e, f]
-                there = (p >= 0) & (lax.shift_right_arithmetic(p, 3) == side)
-                low = jnp.where(there, jnp.minimum(low, e), low)
-                high = jnp.where(there, jnp.maximum(high, e), high)
-        out_ref[0] = own_ref[low, 0]
-        out_ref[1] = own_ref[high, 0]
-
-
-def average_kernel(blocks, where_ref, partner_ref, side_ref, flip_ref, own_ref, prev_ref, next_ref, pick_ref, modal_ref, send_ref, all_ref):
+            there = [(partner_ref[f, e] >= 0) & (lax.shift_right_arithmetic(partner_ref[f, e], 3) == side) for f in range(4)]
+            there = (there[0] | there[1]) | (there[2] | there[3])
+            low = jnp.where(there, jnp.minimum(low, e), low)
+            high = jnp.where(there, jnp.maximum(high, e), high)
+        out_ref[0] = own_ref[pl.ds(16 * low, 8)]
+        out_ref[1] = own_ref[pl.ds(16 * high, 8)]
+
+
+def average(own_ref, pick, element, places):
+    tiles = [None] * 8
+    for f in range(4):
+        for g in range(2):
+            own = own_ref[16 * element + 4 * g + f].astype(F32)
+            other = own_ref[places[f] + 4 * g].astype(F32)
+            tiles[4 * g + f] = (0.5 * (own + other)).astype(BF16)
+    return dot(pick, jnp.concatenate(tiles, axis=0))
+
+
+def pack_kernel(blocks, where_ref, partner_ref, side_ref, flip_ref, rows_ref, tail_ref, own_ref, pick_ref, send_ref, plan_ref, place_ref):
     me, before, after = prev_next(where_ref, blocks)
+    sides = (before, after)
+    low, high, least = [jnp.int32(7)] * 2, [jnp.int32(0)] * 2, [jnp.int32(1 << 30)] * 2
+    for e in range(8):
+        for f in range(4):
+            p = partner_ref[f, e]
+            for i in range(2):
+                there = (p >= 0) & (lax.shift_right_arithmetic(p, 3) == sides[i])
+                low[i] = jnp.where(there, jnp.minimum(low[i], e), low[i])
+                high[i] = jnp.where(there, jnp.maximum(high[i], e), high[i])
+                least[i] = jnp.where(there, jnp.minimum(least[i], p), least[i])
+    pick = pick_ref[...]
+    for e in range(8):
+        places = []
+        for f in range(4):
+            p = partner_ref[f, e]
+            home = lax.shift_right_arithmetic(p, 3)
+            turn = flip_ref[f, e] * 8 + side_ref[f, e]
+            near = lax.bitwise_and(p, 7) * 16 + turn
+            far = jnp.where(home == before, jnp.where(p == least[0], 128, 144), jnp.where(p == least[1], 160, 176)) + turn
+            place_ref[e, f] = jnp.where(p < 0, 16 * e + f, jnp.where(home == me, near, far))
+            places.append(jnp.where(home == me, near, 16 * e + f))
+        out = average(own_ref, pick, e, places)
+        for h in range(2):
+            send_ref[h, e, 0:96, :] = rows_ref[e, 0:96, 0:128]
+            send_ref[h, e, 96:112, :] = tail_ref[e]
+            send_ref[h, e, 112:152, :] = out[40 * h : 40 * h + 40].astype(BF16)
+    for r, e in enumerate((low[0], high[0], low[1], high[1])):
+        plan_ref[8 * r] = e
+        for f in range(4):
+            plan_ref[8 * r + 1 + f] = place_ref[e, f]
+
+
+def border_kernel(plan_ref, prev_ref, next_ref, pick_ref, own_in, send_in, own_ref, send_ref):
     reverse = reverse_faces()
-    all_ref[0:128] = own_ref[...].reshape(128, 16, 128)
     for k, ref in ((8, prev_ref), (10, next_ref)):
         for i in range(2):
             at = 16 * (k + i)
-            all_ref[at : at + 8] = ref[i].reshape(8, 16, 128)
-            all_ref[at + 8 : at + 16] = dot(reverse, ref[i]).astype(BF16).reshape(8, 16, 128)
-    least = []
-    for side in (before, after):
-        low = jnp.int32(1 << 30)
-        for e in range(8):
-            for f in range(4):
-                p = partner_ref[e, f]
-                there = (p >= 0) & (lax.shift_right_arithmetic(p, 3) == side)
-                low = jnp.where(there, jnp.minimum(low, p), low)
-        least.append(low)
+            own_ref[at : at + 8] = ref[i]
+            own_ref[at + 8 : at + 16] = dot(reverse, ref[i].reshape(128, 128)).astype(BF16).reshape(8, 16, 128)
     pick = pick_ref[...]
-    for e in range(8):
-        tiles = [None] * 8
-        for f in range(4):
-            p = partner_ref[e, f]
-            home = lax.shift_right_arithmetic(p, 3)
-            slot = jnp.where(
-                home == me,
-                lax.bitwise_and(p, 7),
-                jnp.where(home == before, 8 + (p != least[0]).astype(jnp.int32), 10 + (p != least[1]).astype(jnp.int32)),
-            )
-            place = jnp.where(p >= 0, slot * 16 + flip_ref[e, f] * 8 + side_ref[e, f], 16 * e + f)
-            for g in range(2):
-                own = all_ref[16 * e + 4 * g + f].astype(F32)
-                other = all_ref[place + 4 * g].astype(F32)
-                tiles[4 * g + f] = (0.5 * (own + other)).astype(BF16)
-        out = dot(pick, jnp.concatenate(tiles, axis=0))
+    for r in range(4):
+        e = plan_ref[8 * r]
+        out = average(own_ref, pick, e, [plan_ref[8 * r + 1 + f] for f in range(4)])
         for h in range(2):
             send_ref[h, e, 112:152, :] = out[40 * h : 40 * h + 40].astype(BF16)
 
 
 def regroup(blocks):
     rows = blocks[0].shape[0]
-    lane = iota((rows, 128), 1) // 32
+    lane = iota((rows, 128), 1) >> 5
     out = []
     for c in range(3):
         groups = []
@@ -208,14 +232,14 @@
 
 def main_kernel(where_ref, metric_ref, got_ref, table_ref, place_ref, synth_ref, analysis_ref, out_ref, field_ref, adv_ref):
     elem, half = where_ref[1], where_ref[2]
-    m = [metric_ref[elem, k] for k in range(4)]
+    m = [metric_ref[k, elem] for k in range(4)]
     table = table_ref[half]
     place = place_ref[half]
     tails = regroup([got_ref[p, 96:112, :].astype(F32) for p in range(16)])
     faces = regroup([got_ref[p, 112:152, :].astype(F32) for p in range(16)])
     on_face = dot(place, jnp.ones((40, 512), BF16)) > 0.5
     lane = iota((72, 128), 1)
-    even = lane % 2 == 0
+    even = (lane & 1) == 0
     for c in range(3):
         modes = jnp.concatenate([got_ref[p, 32 * c : 32 * c + 32, :] for p in range(16)], axis=0)
         d = dot_nt(table[:, 0:128], modes) + dot(table[:, 128:144], tails[c].astype(BF16))
@@ -224,7 +248,7 @@
         turned = []
         for g in range(4):
             v = value[:, 128 * g : 128 * g + 128]
-            k = ((lane + 128 * g) // 2).astype(F32) * (1.0 / 32.0)
+            k = ((lane + 128 * g) >> 1).astype(F32) * (1.0 / 32.0)
             turned.append(jnp.where(even, -k * pltpu.roll(v, 127, 1), k * pltpu.roll(v, 1, 1)))
         field_ref[288 * c : 288 * c + 144, :] = jnp.concatenate([value, jnp.concatenate(turned, axis=1)], axis=0).astype(BF16)
         grads = jnp.concatenate([xi * m[0] + eta * m[1], xi * m[2] + eta * m[3]], axis=0)
@@ -249,11 +273,12 @@
 
 def unpack_kernel(in_ref, out_ref):
     order = to_element_rows()
-    rows, cols = iota((256, 144), 0), iota((256, 144), 1)
+    lead, cols = iota((256, 144), 0) - iota((256, 144), 1), iota((256, 144), 1)
+    mine = (cols < 72, cols >= 72)
     for c in range(3):
         block = None
         for z in range(2):
-            pick = jnp.where((rows - 72 * c == cols - 72 * z) & (cols // 72 == z), 1.0, 0.0).astype(BF16)
+            pick = jnp.where((lead == 72 * (c - z)) & mine[z], 1.0, 0.0).astype(BF16)
             part = dot(in_ref[8 * z : 8 * z + 8].reshape(256, 256), pick)
             block = part if block is None else block + part
         block = block.astype(BF16)
@@ -266,20 +291,25 @@
 
 SMEM = pl.BlockSpec(memory_space=pltpu.SMEM)
 VMEM = pl.BlockSpec(memory_space=pltpu.VMEM)
-
-
-def call(kernel, in_specs, out_shapes, scratch=(), aliases=None):
+HBM = pl.BlockSpec(memory_space=pltpu.HBM)
+
+
+def call(kernel, in_specs, out_shapes, scratch=(), aliases=None, out_specs=None):
     single = not isinstance(out_shapes, (list, tuple)) or hasattr(out_shapes, "shape")
     return pl.pallas_call(
         kernel,
         in_specs=in_specs,
-        out_specs=VMEM if single else [VMEM] * len(out_shapes),
+        out_specs=out_specs or (VMEM if single else [VMEM] * len(out_shapes)),
         out_shape=out_shapes,
         scratch_shapes=list(scratch),
         compiler_params=pltpu.CompilerParams(vmem_limit_bytes=40 * 1024 * 1024),
         input_output_aliases=aliases or {},
         interpret=INTERPRET,
     )
+
+
+def in_hbm(x):
+    return x if INTERPRET else pltpu.with_memory_space_constraint(x, pltpu.HBM)
 
 
 def shape(*dims):
@@ -293,28 +323,36 @@
     up = [(i, (i + 1) % blocks) for i in range(blocks)]
     down = [(j, i) for i, j in up]
     synth, analysis = fourier_tables(512, 768)
-    modal, own, to_prev, to_next = call(
-        functools.partial(pack_kernel, blocks),
-        [SMEM, SMEM, SMEM, VMEM, VMEM],
-        [shape(2, 8, 152, 128), shape(8, 2, 128, 128), shape(2, 128, 128), shape(2, 128, 128)],
-        [pltpu.VMEM((8, 128, 144), BF16)],
-    )(where, face_partner, metric, velocity_modes.reshape(768, 144), bf16(trace_table()))
+    partner, side, flip, geometry = face_partner.T, face_side.T, face_flip.T, metric.T
+    pick = bf16(pick_table())
+    rows, tail, own, to_prev, to_next = call(
+        functools.partial(trace_kernel, blocks),
+        [SMEM, HBM, HBM, HBM, HBM],
+        [shape(8, 128, 144), shape(8, 16, 128), shape(192, 16, 128), shape(2, 8, 16, 128), shape(2, 8, 16, 128)],
+        [pltpu.SMEM((4, 8), jnp.int32), pltpu.SMEM((4, 8), F32), pltpu.VMEM((768, 144), BF16), pltpu.VMEM((272, 144), BF16), pltpu.SemaphoreType.DMA((4,))],
+    )(where, *map(in_hbm, (partner, geometry, velocity_modes.reshape(768, 144), bf16(trace_table()))))
     from_prev = lax.ppermute(to_next, "elem", up)
     from_next = lax.ppermute(to_prev, "elem", down)
-    sent = call(
-        functools.partial(average_kernel, blocks),
-        [SMEM, SMEM, SMEM, SMEM, VMEM, VMEM, VMEM, VMEM, VMEM],
-        shape(2, 8, 152, 128),
-        [pltpu.VMEM((192, 16, 128), BF16)],
-        {8: 0},
-    )(where, face_partner, face_side, face_flip, own, from_prev, from_next, bf16(pick_table()), modal)
-    got = lax.all_to_all(sent.reshape(16, 152, 128), "plane", 0, 0, tiled=True)
+    send, plan = call(
+        functools.partial(pack_kernel, blocks),
+        [SMEM, SMEM, SMEM, SMEM, VMEM, VMEM, VMEM, VMEM],
+        [shape(2, 8, 152, 128), jax.ShapeDtypeStruct((32,), jnp.int32)],
+        [pltpu.SMEM((8, 4), jnp.int32)],
+        out_specs=[VMEM, SMEM],
+    )(where, partner, side, flip, rows, tail, own, pick)
+    _, send = call(
+        border_kernel,
+        [SMEM, VMEM, VMEM, VMEM, VMEM, VMEM],
+        [shape(192, 16, 128), shape(2, 8, 152, 128)],
+        aliases={4: 0, 5: 1},
+    )(plan, from_prev, from_next, pick, own, send)
+    got = lax.all_to_all(send.reshape(16, 152, 128), "plane", 0, 0, tiled=True)
     out = call(
         main_kernel,
         [SMEM, SMEM, VMEM, VMEM, VMEM, VMEM, VMEM],
         shape(16, 32, 256),
         [pltpu.VMEM((864, 512), BF16), pltpu.VMEM((256, 768), BF16)],
-    )(where, metric, got, bf16(point_table()), bf16(place_table()), bf16(synth), bf16(analysis))
+    )(where, geometry, got, bf16(point_table()), bf16(place_table()), bf16(synth), bf16(analysis))
     out = lax.all_to_all(out, "plane", 0, 0, tiled=True)
     out = call(unpack_kernel, [VMEM], shape(768, 144))(out)
     return out.reshape(3, 32, 8, 144)

time: 69.2 us -> 66.8 us (0.965)
  local copies, waits for them, and re-layouts: 3.55 us -> 0.71 us
  Pallas kernels: 6.95 us -> 9.15 us
  waiting for transfers between devices: 1.71 us -> 0.01 us
    unnamed x26 -> x18, local copies, waits for them, and re-layouts: 3.55 us -> 0.71 us
    pallas_call x2 -> x3, Pallas kernels: 2.71 us -> 4.95 us  [the longest x1 2.3 us: on_device(): call(functools.partial(trace_kernel, blocks), [SMEM, HBM, HBM, HBM, HBM],...]
    ppermute x1, waiting for transfers between devices: 1.49 us -> 0.01 us  [on_device(): from_next = lax.ppermute(to_prev, 'elem', down)]
  transfers between devices with their start and end apart: 2 -> 2, of which waited for: 2 -> 0; matrix products, arithmetic and copies ran while one was open for 0% -> 0% of each run, Pallas kernels for 0% -> 3%
where the time goes in v3:
time: 66.8 us; the launch traced here: 66.5 us
  blocking collectives  35 us (52%)
  starting transfers between devices  21.5 us (32%)
  Pallas kernels  9.15 us (14%)
  local copies, waits for them, and re-layouts  0.71 us (1%)
    all_to_all x1, blocking collectives, on_device(): got = lax.all_to_all(send.reshape(16, 152, 128), 'plane', 0, 0, tiled=True)  22.6 us
    ppermute x1, starting transfers between devices, on_device(): from_next = lax.ppermute(to_prev, 'elem', down)  19.5 us
    all_to_all x1, blocking collectives, on_device(): out = lax.all_to_all(out, 'plane', 0, 0, tiled=True)  12.4 us
    pallas_call x1, Pallas kernels, on_device(): call(main_kernel, [SMEM, SMEM, VMEM, VMEM, VMEM, VMEM, VMEM], shape(16, 3...  2.44 us
    pallas_call x1, Pallas kernels, on_device(): call(functools.partial(trace_kernel, blocks), [SMEM, HBM, HBM, HBM, HBM],...  2.3 us
    ppermute x1, starting transfers between devices, on_device(): from_prev = lax.ppermute(to_next, 'elem', up)  1.92 us
    pallas_call x1, Pallas kernels, on_device(): out = call(unpack_kernel, [VMEM], shape(768, 144))(out)  1.76 us
    pallas_call x1, Pallas kernels, on_device(): call(functools.partial(pack_kernel, blocks), [SMEM, SMEM, SMEM, SMEM, VME...  1.73 us
  transfers between devices with their start and end apart: 2, of which 0 were waited for; matrix products, arithmetic and copies ran while one was open for 0% of the time, Pallas kernels for 3%

profile of v3, /device:TPU:2, one launch (start us, length us, event | category | flops | bytes accessed | tf_op | source)
XLA Modules:
  0.0 66.5 jit_solution(10562512360244236288)
XLA Ops:
  0.0 0.1 pad_add_fusion.where_ref
  0.1 0.0 copy-start.3
  0.1 2.3 %shard_map.109 = (bf16[8,128,144]{2,1,0:T(8,128)(2,1)S(1)}, bf16[8,16,128]{2,1,0:T(8,128)(2,1)S(1)}, bf16[192,16,128]{2,1,0:T(8,128)(2,1)S(1)}, bf16[2,8,16,128]...) custom-call(s32[3]{0:T(128)S(1)} %pad_add_fusion.where_ref, s32[4,8]{1,0:T(4,128)} %bitcast.11, f32[4,8]{1,0:T(4,128)} %bitcast.13, ...), custom_call_target="tpu_custom_call" | custom-call | tf_op jit(solution)/shard_map/pallas_call | solution.py:328
  2.4 0.0 copy-start.8
  2.4 1.9 %collective-permute-start = (bf16[2,8,16,128]{3,2,1,0:T(8,128)(2,1)S(1)}, bf16[2,8,16,128]{3,2,1,0:T(8,128)(2,1)S(1)}, u32[]{:S(2)}, u32[]{:S(2)}) collective-permute-start(bf16[2,8,16,128]{3,2,1,0:T(8,128)(2,1)S(1)} %get-tuple-element.17), channel_id=1, source_target_pairs={{0,16},{16,32},{32,48},{48,64},{64,80},{80,96},{96,112},{112,128},... | collective-permute-start | bytes 196616 | tf_op jit(solution)/shard_map/ppermute | solution.py:334
  4.3 19.5 %collective-permute-start.1 = (bf16[2,8,16,128]{3,2,1,0:T(8,128)(2,1)S(1)}, bf16[2,8,16,128]{3,2,1,0:T(8,128)(2,1)S(1)}, u32[]{:S(2)}, u32[]{:S(2)}) collective-permute-start(bf16[2,8,16,128]{3,2,1,0:T(8,128)(2,1)S(1)} %get-tuple-element.18), channel_id=1, source_target_pairs={{16,0},{32,16},{48,32},{64,48},{80,64},{96,80},{112,96},{128,112},... | collective-permute-start | bytes 196616 | tf_op jit(solution)/shard_map/ppermute | solution.py:335
  23.9 0.0 copy-start.7
  23.9 0.0 copy-start.5
  23.9 0.0 copy-done.3
  23.9 0.0 copy-done.8
  23.9 0.6 copy-done.7
  24.6 0.0 copy-done.5
  24.6 1.7 %shard_map.110 = (bf16[2,8,152,128]{3,2,1,0:T(8,128)(2,1)S(1)}, s32[32]{0:T(128)S(1)}) custom-call(s32[3]{0:T(128)S(1)} %pad_add_fusion.where_ref, s32[4,8]{1,0:T(4,128)S(1)} %bitcast.12, s32[4,8]{1,0:T(4,128)S(1)} %bitcast.15, s32[4,8]{1,0:T(4,128)S(1)} %bitcast.16, bf16[8,128,144]{2,1,0:T(8,128)(2,1)S(1)} %get-tuple-element.13.rows_ref, ...), custom_call_target="tpu_custom_call" | custom-call | tf_op jit(solution)/shard_map/pallas_call | solution.py:336
  26.3 0.0 collective-permute-done.prev_ref
  26.3 0.0 collective-permute-done.1.next_ref
  26.3 0.0 copy-start.1
  26.3 0.9 %shard_map.111 = (bf16[192,16,128]{2,1,0:T(8,128)(2,1)S(1)}, bf16[2,8,152,128]{3,2,1,0:T(8,128)(2,1)S(1)}) custom-call(s32[32]{0:T(128)S(1)} %get-tuple-element.16.plan_ref, bf16[2,8,16,128]{3,2,1,0:T(8,128)(2,1)S(1)} %collective-permute-done.prev_ref, ...), custom_call_target="tpu_custom_call", output_to_operand_aliasing={{0}: (4, {}), {1}: (5, {})} | custom-call | tf_op jit(solution)/shard_map/pallas_call | solution.py:343
  27.3 0.0 copy-start
  27.3 0.0 copy-start.2
  27.3 0.0 copy-start.4
  27.3 0.0 copy-start.6
  27.3 22.6 %all_to_all.10.got_ref = bf16[16,152,128]{2,1,0:T(8,128)(2,1)S(1)} all-to-all(bf16[16,152,128]{2,1,0:T(8,128)(2,1)S(1)} %bitcast.10), channel_id=1, replica_groups=mesh['elem'=64,'plane'=16] {'plane'}, dimensions={0} | all-to-all | bytes 1245184 | tf_op jit(solution)/shard_map/all_to_all | solution.py:349
  49.9 0.0 copy-done.1
  49.9 0.0 copy-done
  49.9 0.0 copy-done.2
  49.9 0.0 copy-done.4
  49.9 0.0 copy-done.6
  50.0 2.4 %shard_map.112 = bf16[16,32,256]{2,1,0:T(8,128)(2,1)S(1)} custom-call(s32[3]{0:T(128)S(1)} %pad_add_fusion.where_ref, f32[4,8]{1,0:T(4,128)S(1)} %bitcast.14, bf16[16,152,128]{2,1,0:T(8,128)(2,1)S(1)} %all_to_all.10.got_ref, bf16[2,216,144]{2,1,0:T(8,128)(2,1)S(1)} %copy-done.2, bf16[2,144,40]{2,1,0:T(8,128)(2,1)S(1)} %copy-done.4, ...), custom_call_target="tpu_custom_call" | custom-call | tf_op jit(solution)/shard_map/pallas_call | solution.py:350
  52.4 12.4 %all_to_all.11.in_ref = bf16[16,32,256]{2,1,0:T(8,128)(2,1)S(1)} all-to-all(bf16[16,32,256]{2,1,0:T(8,128)(2,1)S(1)} %shard_map.112), channel_id=1, replica_groups=mesh['elem'=64,'plane'=16] {'plane'}, dimensions={0} | all-to-all | bytes 524288 | tf_op jit(solution)/shard_map/all_to_all | solution.py:356
  64.8 1.8 %shard_map.113 = bf16[768,144]{1,0:T(8,128)(2,1)} custom-call(bf16[16,32,256]{2,1,0:T(8,128)(2,1)S(1)} %all_to_all.11.in_ref), custom_call_target="tpu_custom_call" | custom-call | tf_op jit(solution)/shard_map/pallas_call | solution.py:357
Async XLA Ops:
  0.1 23.8 %copy-start.3 = (bf16[80,128]{1,0:T(8,128)(2,1)S(1)}, bf16[80,128]{1,0:T(8,128)(2,1)}, u32[]{:S(2)}) copy-start(bf16[80,128]{1,0:T(8,128)(2,1)} %constant.59.pick_ref) | copy-start | bytes 61444
  2.4 21.5 %copy-start.8 = (s32[8,4]{0,1:T(4,128)S(1)}, s32[8,4]{0,1:T(4,128)}, u32[]{:S(2)}) copy-start(s32[8,4]{0,1:T(4,128)} %param.15) | copy-start | bytes 388
  2.4 23.9 %collective-permute-start = (bf16[2,8,16,128]{3,2,1,0:T(8,128)(2,1)S(1)}, bf16[2,8,16,128]{3,2,1,0:T(8,128)(2,1)S(1)}, u32[]{:S(2)}, u32[]{:S(2)}) collective-permute-start(bf16[2,8,16,128]{3,2,1,0:T(8,128)(2,1)S(1)} %get-tuple-element.17), channel_id=1, source_target_pairs={{0,16},{16,32},{32,48},{48,64},{64,80},{80,96},{96,112},{112,128},... | collective-permute-start | bytes 196616 | tf_op jit(solution)/shard_map/ppermute | solution.py:334
  4.3 22.0 %collective-permute-start.1 = (bf16[2,8,16,128]{3,2,1,0:T(8,128)(2,1)S(1)}, bf16[2,8,16,128]{3,2,1,0:T(8,128)(2,1)S(1)}, u32[]{:S(2)}, u32[]{:S(2)}) collective-permute-start(bf16[2,8,16,128]{3,2,1,0:T(8,128)(2,1)S(1)} %get-tuple-element.18), channel_id=1, source_target_pairs={{16,0},{32,16},{48,32},{64,48},{80,64},{96,80},{112,96},{128,112},... | collective-permute-start | bytes 196616 | tf_op jit(solution)/shard_map/ppermute | solution.py:335
  23.9 0.7 %copy-start.7 = (s32[8,4]{0,1:T(4,128)S(1)}, s32[8,4]{0,1:T(4,128)}, u32[]{:S(2)}) copy-start(s32[8,4]{0,1:T(4,128)} %param.14) | copy-start | bytes 388
  23.9 0.7 %copy-start.5 = (s32[8,4]{0,1:T(4,128)S(1)}, s32[8,4]{0,1:T(4,128)}, u32[]{:S(2)}) copy-start(s32[8,4]{0,1:T(4,128)} %param.13) | copy-start | bytes 388
  26.3 23.6 %copy-start.1 = (bf16[512,768]{1,0:T(8,128)(2,1)S(1)}, bf16[512,768]{1,0:T(8,128)(2,1)}, u32[]{:S(2)}) copy-start(bf16[512,768]{1,0:T(8,128)(2,1)} %constant.62.synth_ref) | copy-start | bytes 2359300
  27.3 22.7 %copy-start = (bf16[512,768]{1,0:T(8,128)(2,1)S(1)}, bf16[512,768]{1,0:T(8,128)(2,1)}, u32[]{:S(2)}) copy-start(bf16[512,768]{1,0:T(8,128)(2,1)} %constant.63.analysis_ref) | copy-start | bytes 2359300
  27.3 22.7 %copy-start.2 = (bf16[2,216,144]{2,1,0:T(8,128)(2,1)S(1)}, bf16[2,216,144]{2,1,0:T(8,128)(2,1)}, u32[]{:S(2)}) copy-start(bf16[2,216,144]{2,1,0:T(8,128)(2,1)} %constant.60.table_ref) | copy-start | bytes 373252
  27.3 22.6 %copy-start.4 = (bf16[2,144,40]{2,1,0:T(8,128)(2,1)S(1)}, bf16[2,144,40]{2,1,0:T(8,128)(2,1)}, u32[]{:S(2)}) copy-start(bf16[2,144,40]{2,1,0:T(8,128)(2,1)} %constant.61.place_ref) | copy-start | bytes 69124
  27.3 22.6 %copy-start.6 = (f32[8,4]{0,1:T(4,128)S(1)}, f32[8,4]{0,1:T(4,128)}, u32[]{:S(2)}) copy-start(f32[8,4]{0,1:T(4,128)} %param.12) | copy-start | bytes 388

commit v4 on v3

--- a/solution.py
+++ b/solution.py
@@ -111,47 +111,18 @@
     return lax.dot_general(a, b, (((0,), (0,)), ((), ())), preferred_element_type=F32)
 
 
-def prev_next(where_ref, blocks):
-    me = where_ref[0]
-    return me, jnp.where(me == 0, blocks - 1, me - 1), jnp.where(me == blocks - 1, 0, me + 1)
-
-
-def trace_kernel(blocks, where_ref, partner_hbm, metric_hbm, v_hbm, table_hbm, rows_ref, tail_ref, own_ref, prev_ref, next_ref, partner_ref, metric_ref, v_ref, table_ref, sems):
-    copies = [
-        pltpu.make_async_copy(src, dst, sems.at[i])
-        for i, (src, dst) in enumerate(((v_hbm, v_ref), (table_hbm, table_ref), (metric_hbm, metric_ref), (partner_hbm, partner_ref)))
-    ]
+def neighbours(blocks):
+    me = lax.axis_index("elem")
+    odd = lax.bitwise_and(me, 1)
+    other = lax.bitwise_and(me + 2 * odd - 1 + blocks, blocks - 1)
+    return me, (me + 1 - 2 * odd, other)
+
+
+def start_copies(pairs, sems):
+    copies = [pltpu.make_async_copy(src, dst, sems.at[i]) for i, (src, dst) in enumerate(pairs)]
     for copy in copies:
         copy.start()
-    order = to_element_rows()
-    rows_ref[:, 96:128, :] = jnp.zeros((8, 32, 144), BF16)
-    for copy in copies:
-        copy.wait()
-    for b in range(6):
-        block = dot(order, v_ref[128 * b : 128 * b + 128, :]).astype(BF16)
-        for e in range(8):
-            rows_ref[e, 16 * b : 16 * b + 16, :] = block[16 * e : 16 * e + 16]
-    table = table_ref[...]
-    for e in range(8):
-        out = dot_nt(table, rows_ref[e])
-        tail_ref[e] = out[0:16].astype(BF16)
-        for flip in range(2):
-            xi = out[16 + 128 * flip : 80 + 128 * flip]
-            eta = out[80 + 128 * flip : 144 + 128 * flip]
-            for g in range(2):
-                grad = xi * metric_ref[2 * g, e] + eta * metric_ref[2 * g + 1, e]
-                at = 16 * e + 8 * flip + 4 * g
-                own_ref[at : at + 4] = grad.astype(BF16).reshape(4, 16, 128)
-    _, before, after = prev_next(where_ref, blocks)
-    for side, out_ref in ((before, prev_ref), (after, next_ref)):
-        low, high = jnp.int32(7), jnp.int32(0)
-        for e in range(8):
-            there = [(partner_ref[f, e] >= 0) & (lax.shift_right_arithmetic(partner_ref[f, e], 3) == side) for f in range(4)]
-            there = (there[0] | there[1]) | (there[2] | there[3])
-            low = jnp.where(there, jnp.minimum(low, e), low)
-            high = jnp.where(there, jnp.maximum(high, e), high)
-        out_ref[0] = own_ref[pl.ds(16 * low, 8)]
-        out_ref[1] = own_ref[pl.ds(16 * high, 8)]
+    return copies
 
 
 def average(own_ref, pick, element, places):
@@ -164,19 +135,59 @@
     return dot(pick, jnp.concatenate(tiles, axis=0))
 
 
-def pack_kernel(blocks, where_ref, partner_ref, side_ref, flip_ref, rows_ref, tail_ref, own_ref, pick_ref, send_ref, plan_ref, place_ref):
-    me, before, after = prev_next(where_ref, blocks)
-    sides = (before, after)
+def pack_kernel(
+    blocks, partner_hbm, side_hbm, flip_hbm, metric_hbm, v_hbm, table_hbm, pick_hbm, send_ref, own_ref, swap_ref_0, swap_ref_1, plan_ref,
+    partner_ref, side_ref, flip_ref, metric_ref, v_ref, table_ref, pick_ref, rows_ref, place_ref, sems,
+):
+    copies = start_copies(
+        (
+            (v_hbm, v_ref),
+            (table_hbm, table_ref),
+            (partner_hbm, partner_ref),
+            (metric_hbm, metric_ref),
+            (side_hbm, side_ref),
+            (flip_hbm, flip_ref),
+            (pick_hbm, pick_ref),
+        ),
+        sems,
+    )
+    me, sides = neighbours(blocks)
+    order = to_element_rows()
+    rows_ref[:, 96:128, :] = jnp.zeros((8, 32, 144), BF16)
+    for copy in copies:
+        copy.wait()
     low, high, least = [jnp.int32(7)] * 2, [jnp.int32(0)] * 2, [jnp.int32(1 << 30)] * 2
     for e in range(8):
         for f in range(4):
             p = partner_ref[f, e]
             for i in range(2):
-                there = (p >= 0) & (lax.shift_right_arithmetic(p, 3) == sides[i])
+                there = lax.shift_right_arithmetic(p, 3) == sides[i]
                 low[i] = jnp.where(there, jnp.minimum(low[i], e), low[i])
-                high[i] = jnp.where(there, jnp.maximum(high[i], e), high[i])
+                high[i] = jnp.where(there, e, high[i])
                 least[i] = jnp.where(there, jnp.minimum(least[i], p), least[i])
+    table = table_ref[...]
     pick = pick_ref[...]
+    for b in range(6):
+        block = dot(order, v_ref[128 * b : 128 * b + 128, :]).astype(BF16)
+        for e in range(8):
+            rows_ref[e, 16 * b : 16 * b + 16, :] = block[16 * e : 16 * e + 16]
+    for e in range(8):
+        rows = rows_ref[e]
+        out = dot_nt(table, rows)
+        tail = out[0:16].astype(BF16)
+        for h in range(2):
+            send_ref[h, e, 0:96, :] = rows[0:96, 0:128]
+            send_ref[h, e, 96:112, :] = tail
+        for flip in range(2):
+            xi = out[16 + 128 * flip : 80 + 128 * flip]
+            eta = out[80 + 128 * flip : 144 + 128 * flip]
+            for g in range(2):
+                grad = xi * metric_ref[2 * g, e] + eta * metric_ref[2 * g + 1, e]
+                at = 16 * e + 8 * flip + 4 * g
+                own_ref[at : at + 4] = grad.astype(BF16).reshape(4, 16, 128)
+    for i, out_ref in enumerate((swap_ref_0, swap_ref_1)):
+        out_ref[0] = own_ref[pl.ds(16 * low[i], 8)]
+        out_ref[1] = own_ref[pl.ds(16 * high[i], 8)]
     for e in range(8):
         places = []
         for f in range(4):
@@ -184,13 +195,12 @@
             home = lax.shift_right_arithmetic(p, 3)
             turn = flip_ref[f, e] * 8 + side_ref[f, e]
             near = lax.bitwise_and(p, 7) * 16 + turn
-            far = jnp.where(home == before, jnp.where(p == least[0], 128, 144), jnp.where(p == least[1], 160, 176)) + turn
-            place_ref[e, f] = jnp.where(p < 0, 16 * e + f, jnp.where(home == me, near, far))
-            places.append(jnp.where(home == me, near, 16 * e + f))
+            far = jnp.where(home == sides[0], jnp.where(p == least[0], 128, 144), jnp.where(p == least[1], 160, 176)) + turn
+            inside = jnp.where(home == me, near, 16 * e + f)
+            place_ref[e, f] = jnp.where((p < 0) | (home == me), inside, far)
+            places.append(inside)
         out = average(own_ref, pick, e, places)
         for h in range(2):
-            send_ref[h, e, 0:96, :] = rows_ref[e, 0:96, 0:128]
-            send_ref[h, e, 96:112, :] = tail_ref[e]
             send_ref[h, e, 112:152, :] = out[40 * h : 40 * h + 40].astype(BF16)
     for r, e in enumerate((low[0], high[0], low[1], high[1])):
         plan_ref[8 * r] = e
@@ -198,9 +208,9 @@
             plan_ref[8 * r + 1 + f] = place_ref[e, f]
 
 
-def border_kernel(plan_ref, prev_ref, next_ref, pick_ref, own_in, send_in, own_ref, send_ref):
+def border_kernel(plan_ref, swap_ref_0, swap_ref_1, pick_ref, own_in, send_in, own_ref, send_ref):
     reverse = reverse_faces()
-    for k, ref in ((8, prev_ref), (10, next_ref)):
+    for k, ref in ((8, swap_ref_0), (10, swap_ref_1)):
         for i in range(2):
             at = 16 * (k + i)
             own_ref[at : at + 8] = ref[i]
@@ -230,9 +240,10 @@
     return out
 
 
-def main_kernel(where_ref, metric_ref, got_ref, table_ref, place_ref, synth_ref, analysis_ref, out_ref, field_ref, adv_ref):
-    elem, half = where_ref[1], where_ref[2]
-    m = [metric_ref[k, elem] for k in range(4)]
+def main_kernel(metric_hbm, got_ref, table_ref, place_ref, synth_ref, analysis_ref, out_ref, field_ref, adv_ref, metric_ref, sems):
+    (copy,) = start_copies(((metric_hbm, metric_ref),), sems)
+    position = lax.axis_index("plane")
+    elem, half = lax.bitwise_and(position, 7), lax.shift_right_logical(position, 3)
     table = table_ref[half]
     place = place_ref[half]
     tails = regroup([got_ref[p, 96:112, :].astype(F32) for p in range(16)])
@@ -240,6 +251,8 @@
     on_face = dot(place, jnp.ones((40, 512), BF16)) > 0.5
     lane = iota((72, 128), 1)
     even = (lane & 1) == 0
+    copy.wait()
+    m = [metric_ref[k, elem] for k in range(4)]
     for c in range(3):
         modes = jnp.concatenate([got_ref[p, 32 * c : 32 * c + 32, :] for p in range(16)], axis=0)
         d = dot_nt(table[:, 0:128], modes) + dot(table[:, 128:144], tails[c].astype(BF16))
@@ -271,10 +284,12 @@
     out_ref[...] = out.astype(BF16).reshape(16, 32, 256)
 
 
-def unpack_kernel(in_ref, out_ref):
-    order = to_element_rows()
+def unpack_kernel(in_ref, out_hbm, out_ref, sems):
+    out, inp = iota((128, 128), 0), iota((128, 128), 1)
+    order = jnp.where(inp == ((out & 7) << 4) + (out >> 3), 1.0, 0.0).astype(BF16)
     lead, cols = iota((256, 144), 0) - iota((256, 144), 1), iota((256, 144), 1)
     mine = (cols < 72, cols >= 72)
+    copies = []
     for c in range(3):
         block = None
         for z in range(2):
@@ -284,9 +299,12 @@
         block = block.astype(BF16)
         for b in range(2):
             piece = jnp.concatenate([block[32 * e + 16 * b : 32 * e + 16 * b + 16] for e in range(8)], axis=0)
-            back = dot_tn(order, piece)
-            at = 256 * c + 128 * b
-            out_ref[at : at + 128, :] = back.astype(BF16)
+            rows = pl.ds(256 * c + 128 * b, 128)
+            out_ref[rows, :] = dot(order, piece).astype(BF16)
+            copies.append(pltpu.make_async_copy(out_ref.at[rows], out_hbm.at[rows], sems.at[2 * c + b]))
+            copies[-1].start()
+    for copy in copies:
+        copy.wait()
 
 
 SMEM = pl.BlockSpec(memory_space=pltpu.SMEM)
@@ -318,43 +336,70 @@
 
 def on_device(velocity_modes, metric, face_partner, face_side, face_flip):
     blocks = lax.axis_size("elem")
-    position = lax.axis_index("plane")
-    where = jnp.stack([lax.axis_index("elem"), position % 8, position // 8]).astype(jnp.int32)
-    up = [(i, (i + 1) % blocks) for i in range(blocks)]
-    down = [(j, i) for i, j in up]
+    within = [(i, i ^ 1) for i in range(blocks)]
+    across = [((i + 1) % blocks, ((i ^ 1) + 1) % blocks) for i in range(blocks)]
     synth, analysis = fourier_tables(512, 768)
-    partner, side, flip, geometry = face_partner.T, face_side.T, face_flip.T, metric.T
-    pick = bf16(pick_table())
-    rows, tail, own, to_prev, to_next = call(
-        functools.partial(trace_kernel, blocks),
-        [SMEM, HBM, HBM, HBM, HBM],
-        [shape(8, 128, 144), shape(8, 16, 128), shape(192, 16, 128), shape(2, 8, 16, 128), shape(2, 8, 16, 128)],
-        [pltpu.SMEM((4, 8), jnp.int32), pltpu.SMEM((4, 8), F32), pltpu.VMEM((768, 144), BF16), pltpu.VMEM((272, 144), BF16), pltpu.SemaphoreType.DMA((4,))],
-    )(where, *map(in_hbm, (partner, geometry, velocity_modes.reshape(768, 144), bf16(trace_table()))))
-    from_prev = lax.ppermute(to_next, "elem", up)
-    from_next = lax.ppermute(to_prev, "elem", down)
-    send, plan = call(
+    pick, geometry = bf16(pick_table()), in_hbm(metric.T)
+    send, own, to_first, to_second, plan = call(
         functools.partial(pack_kernel, blocks),
-        [SMEM, SMEM, SMEM, SMEM, VMEM, VMEM, VMEM, VMEM],
-        [shape(2, 8, 152, 128), jax.ShapeDtypeStruct((32,), jnp.int32)],
-        [pltpu.SMEM((8, 4), jnp.int32)],
-        out_specs=[VMEM, SMEM],
-    )(where, partner, side, flip, rows, tail, own, pick)
+        [HBM] * 7,
+        [
+            shape(2, 8, 152, 128),
+            shape(192, 16, 128),
+            shape(2, 8, 16, 128),
+            shape(2, 8, 16, 128),
+            jax.ShapeDtypeStruct((32,), jnp.int32),
+        ],
+        [
+            pltpu.SMEM((4, 8), jnp.int32),
+            pltpu.SMEM((4, 8), jnp.int32),
+            pltpu.SMEM((4, 8), jnp.int32),
+            pltpu.SMEM((4, 8), F32),
+            pltpu.VMEM((768, 144), BF16),
+            pltpu.VMEM((272, 144), BF16),
+            pltpu.VMEM((80, 128), BF16),
+            pltpu.VMEM((8, 128, 144), BF16),
+            pltpu.SMEM((8, 4), jnp.int32),
+            pltpu.SemaphoreType.DMA((7,)),
+        ],
+        out_specs=[VMEM] * 4 + [SMEM],
+    )(
+        in_hbm(face_partner.T),
+        in_hbm(face_side.T),
+        in_hbm(face_flip.T),
+        geometry,
+        in_hbm(velocity_modes.reshape(768, 144)),
+        in_hbm(bf16(trace_table())),
+        in_hbm(pick),
+    )
+    from_first = lax.ppermute(to_first, "elem", within)
+    from_second = lax.ppermute(to_second, "elem", across)
     _, send = call(
         border_kernel,
         [SMEM, VMEM, VMEM, VMEM, VMEM, VMEM],
         [shape(192, 16, 128), shape(2, 8, 152, 128)],
         aliases={4: 0, 5: 1},
-    )(plan, from_prev, from_next, pick, own, send)
+    )(plan, from_first, from_second, pick, own, send)
     got = lax.all_to_all(send.reshape(16, 152, 128), "plane", 0, 0, tiled=True)
     out = call(
         main_kernel,
-        [SMEM, SMEM, VMEM, VMEM, VMEM, VMEM, VMEM],
+        [HBM, VMEM, VMEM, VMEM, VMEM, VMEM],
         shape(16, 32, 256),
-        [pltpu.VMEM((864, 512), BF16), pltpu.VMEM((256, 768), BF16)],
-    )(where, geometry, got, bf16(point_table()), bf16(place_table()), bf16(synth), bf16(analysis))
+        [
+            pltpu.VMEM((864, 512), BF16),
+            pltpu.VMEM((256, 768), BF16),
+            pltpu.SMEM((4, 8), F32),
+            pltpu.SemaphoreType.DMA((1,)),
+        ],
+    )(geometry, got, bf16(point_table()), bf16(place_table()), bf16(synth), bf16(analysis))
     out = lax.all_to_all(out, "plane", 0, 0, tiled=True)
-    out = call(unpack_kernel, [VMEM], shape(768, 144))(out)
+    out = call(
+        unpack_kernel,
+        [VMEM],
+        shape(768, 144),
+        [pltpu.VMEM((768, 144), BF16), pltpu.SemaphoreType.DMA((6,))],
+        out_specs=HBM,
+    )(out)
     return out.reshape(3, 32, 8, 144)
 
 

time: 66.8 us -> 67.6 us (1.012)
  waiting for transfers between devices: 0.01 us -> 2.13 us
  Pallas kernels: 9.15 us -> 8.13 us
  local copies, waits for them, and re-layouts: 0.71 us -> 0.03 us
    ppermute x2, waiting for transfers between devices: 0.01 us -> 2.13 us  [the longest x1 2.13 us: on_device(): from_second = lax.ppermute(to_second, 'elem', across)]
    pallas_call x4 -> x3, Pallas kernels: 8.23 us -> 7.21 us  [the longest x1 2.91 us: on_device(): call(functools.partial(pack_kernel, blocks), [HBM] * 7, [shape(2, 8, 152,...]
    unnamed x18 -> x10, local copies, waits for them, and re-layouts: 0.71 us -> 0.03 us
  transfers between devices with their start and end apart: 2 -> 2, of which waited for: 0 -> 1; matrix products, arithmetic and copies ran while one was open for 0% -> 0% of each run, Pallas kernels for 3% -> 0%
where the time goes in v4:
time: 67.6 us; the launch traced here: 67.3 us
  blocking collectives  34.8 us (51%)
  starting transfers between devices  22.1 us (33%)
  Pallas kernels  8.13 us (12%)
  waiting for transfers between devices  2.13 us (3%)
    all_to_all x1, blocking collectives, on_device(): got = lax.all_to_all(send.reshape(16, 152, 128), 'plane', 0, 0, tiled=True)  22.2 us
    ppermute x1, starting transfers between devices, on_device(): from_second = lax.ppermute(to_second, 'elem', across)  20.2 us
    all_to_all x1, blocking collectives, on_device(): out = lax.all_to_all(out, 'plane', 0, 0, tiled=True)  12.6 us
    pallas_call x1, Pallas kernels, on_device(): call(functools.partial(pack_kernel, blocks), [HBM] * 7, [shape(2, 8, 152,...  2.91 us
    pallas_call x1, Pallas kernels, on_device(): call(main_kernel, [HBM, VMEM, VMEM, VMEM, VMEM, VMEM], shape(16, 32, 256)...  2.59 us
    ppermute x1, waiting for transfers between devices, on_device(): from_second = lax.ppermute(to_second, 'elem', across)  2.13 us
    ppermute x1, starting transfers between devices, on_device(): from_first = lax.ppermute(to_first, 'elem', within)  1.92 us
    pallas_call x1, Pallas kernels, on_device(): call(unpack_kernel, [VMEM], shape(768, 144), [pltpu.VMEM((768, 144), BF16...  1.71 us
  transfers between devices with their start and end apart: 2, of which 1 were waited for; matrix products, arithmetic and copies ran while one was open for 0% of the time, Pallas kernels for 0%

profile of v4, /device:TPU:2, one launch (start us, length us, event | category | flops | bytes accessed | tf_op | source)
XLA Modules:
  0.0 67.3 jit_solution(12247921522174099925)
XLA Ops:
  0.0 0.0 copy-start.3
  0.0 2.9 %shard_map.109 = (bf16[2,8,152,128]{3,2,1,0:T(8,128)(2,1)S(1)}, bf16[192,16,128]{2,1,0:T(8,128)(2,1)S(1)}, bf16[2,8,16,128]{3,2,1,0:T(8,128)(2,1)S(1)}, bf16[2,8,16,128]{3,2,1,0:T(8,128)(2,1)S(1)}, s32[32]{0:T(128)S(1)}) custom-call(s32[4,8]{1,0:T(4,128)} %bitcast.11, s32[4,8]{1,0:T(4,128)} %bitcast.12, s32[4,8]{1,0:T(4,128)} %bitcast.13, f32[4,8]{1,0:T(4,128)} %bitcast.9, ...), custom_call_target="tpu_custom_call" | custom-call | tf_op jit(solution)/shard_map/pallas_call | solution.py:343
  2.9 1.9 %collective-permute-start = (bf16[2,8,16,128]{3,2,1,0:T(8,128)(2,1)S(1)}, bf16[2,8,16,128]{3,2,1,0:T(8,128)(2,1)S(1)}, u32[]{:S(2)}, u32[]{:S(2)}) collective-permute-start(bf16[2,8,16,128]{3,2,1,0:T(8,128)(2,1)S(1)} %get-tuple-element.12), channel_id=1, source_target_pairs={{0,16},{16,0},{32,48},{48,32},{64,80},{80,64},{96,112},{112,96},{1... | collective-permute-start | bytes 196616 | tf_op jit(solution)/shard_map/ppermute | solution.py:375
  4.8 20.2 %collective-permute-start.1 = (bf16[2,8,16,128]{3,2,1,0:T(8,128)(2,1)S(1)}, bf16[2,8,16,128]{3,2,1,0:T(8,128)(2,1)S(1)}, u32[]{:S(2)}, u32[]{:S(2)}) collective-permute-start(bf16[2,8,16,128]{3,2,1,0:T(8,128)(2,1)S(1)} %get-tuple-element.13), channel_id=1, source_target_pairs={{16,32},{32,16},{48,64},{64,48},{80,96},{96,80},{112,128},{128,112... | collective-permute-start | bytes 196616 | tf_op jit(solution)/shard_map/ppermute | solution.py:376
  25.1 0.0 collective-permute-done.swap_ref_0
  25.1 2.1 %collective-permute-done.1.swap_ref_1 = bf16[2,8,16,128]{3,2,1,0:T(8,128)(2,1)S(1)} collective-permute-done((bf16[2,8,16,128]{3,2,1,0:T(8,128)(2,1)S(1)}, bf16[2,8,16,128]{3,2,1,0:T(8,128)(2,1)S(1)}, u32[]{:S(2)}, u32[]{:S(2)}) %collective-permute-start.1) | collective-permute-done | bytes 65568 | tf_op jit(solution)/shard_map/ppermute | solution.py:376
  27.2 0.0 copy-done.3
  27.2 0.0 copy-start.1
  27.2 0.9 %shard_map.110 = (bf16[192,16,128]{2,1,0:T(8,128)(2,1)S(1)}, bf16[2,8,152,128]{3,2,1,0:T(8,128)(2,1)S(1)}) custom-call(s32[32]{0:T(128)S(1)} %get-tuple-element.11.plan_ref, bf16[2,8,16,128]{3,2,1,0:T(8,128)(2,1)S(1)} %collective-permute-done.swap_ref_0, ...), custom_call_target="tpu_custom_call", output_to_operand_aliasing={{0}: (4, {}), {1}: (5, {})} | custom-call | tf_op jit(solution)/shard_map/pallas_call | solution.py:377
  28.1 0.0 copy-start
  28.1 0.0 copy-start.2
  28.1 0.0 copy-start.4
  28.2 22.2 %all_to_all.10.got_ref = bf16[16,152,128]{2,1,0:T(8,128)(2,1)S(1)} all-to-all(bf16[16,152,128]{2,1,0:T(8,128)(2,1)S(1)} %bitcast.7), channel_id=1, replica_groups=mesh['elem'=64,'plane'=16] {'plane'}, dimensions={0} | all-to-all | bytes 1245184 | tf_op jit(solution)/shard_map/all_to_all | solution.py:383
  50.4 0.0 copy-done.1
  50.4 0.0 copy-done
  50.4 0.0 copy-done.2
  50.4 0.0 copy-done.4
  50.4 2.6 %shard_map.111 = bf16[16,32,256]{2,1,0:T(8,128)(2,1)S(1)} custom-call(f32[4,8]{1,0:T(4,128)} %bitcast.10, bf16[16,152,128]{2,1,0:T(8,128)(2,1)S(1)} %all_to_all.10.got_ref, bf16[2,216,144]{2,1,0:T(8,128)(2,1)S(1)} %copy-done.2, bf16[2,144,40]{2,1,0:T(8,128)(2,1)S(1)} %copy-done.4, bf16[512,768]{1,0:T(8,128)(2,1)S(1)} %copy-done.1, bf16[512,768]{1,0:T(8,128)(2,1)S(1)} %copy-done), custom_call_target="tpu_custom_call" | custom-call | tf_op jit(solution)/shard_map/pallas_call | solution.py:384
  53.0 12.6 %all_to_all.11.in_ref = bf16[16,32,256]{2,1,0:T(8,128)(2,1)S(1)} all-to-all(bf16[16,32,256]{2,1,0:T(8,128)(2,1)S(1)} %shard_map.111), channel_id=1, replica_groups=mesh['elem'=64,'plane'=16] {'plane'}, dimensions={0} | all-to-all | bytes 524288 | tf_op jit(solution)/shard_map/all_to_all | solution.py:395
  65.6 1.7 %shard_map.112 = bf16[768,144]{1,0:T(8,128)(2,1)} custom-call(bf16[16,32,256]{2,1,0:T(8,128)(2,1)S(1)} %all_to_all.11.in_ref), custom_call_target="tpu_custom_call" | custom-call | tf_op jit(solution)/shard_map/pallas_call | solution.py:396
Async XLA Ops:
  0.0 27.2 %copy-start.3 = (bf16[80,128]{1,0:T(8,128)(2,1)S(1)}, bf16[80,128]{1,0:T(8,128)(2,1)}, u32[]{:S(2)}) copy-start(bf16[80,128]{1,0:T(8,128)(2,1)} %constant.24.pick_hbm.pick_ref) | copy-start | bytes 61444
  2.9 22.1 %collective-permute-start = (bf16[2,8,16,128]{3,2,1,0:T(8,128)(2,1)S(1)}, bf16[2,8,16,128]{3,2,1,0:T(8,128)(2,1)S(1)}, u32[]{:S(2)}, u32[]{:S(2)}) collective-permute-start(bf16[2,8,16,128]{3,2,1,0:T(8,128)(2,1)S(1)} %get-tuple-element.12), channel_id=1, source_target_pairs={{0,16},{16,0},{32,48},{48,32},{64,80},{80,64},{96,112},{112,96},{1... | collective-permute-start | bytes 196616 | tf_op jit(solution)/shard_map/ppermute | solution.py:375
  4.8 22.3 %collective-permute-start.1 = (bf16[2,8,16,128]{3,2,1,0:T(8,128)(2,1)S(1)}, bf16[2,8,16,128]{3,2,1,0:T(8,128)(2,1)S(1)}, u32[]{:S(2)}, u32[]{:S(2)}) collective-permute-start(bf16[2,8,16,128]{3,2,1,0:T(8,128)(2,1)S(1)} %get-tuple-element.13), channel_id=1, source_target_pairs={{16,32},{32,16},{48,64},{64,48},{80,96},{96,80},{112,128},{128,112... | collective-permute-start | bytes 196616 | tf_op jit(solution)/shard_map/ppermute | solution.py:376
  27.2 23.2 %copy-start.1 = (bf16[512,768]{1,0:T(8,128)(2,1)S(1)}, bf16[512,768]{1,0:T(8,128)(2,1)}, u32[]{:S(2)}) copy-start(bf16[512,768]{1,0:T(8,128)(2,1)} %constant.27.synth_ref) | copy-start | bytes 2359300
  28.1 22.3 %copy-start = (bf16[512,768]{1,0:T(8,128)(2,1)S(1)}, bf16[512,768]{1,0:T(8,128)(2,1)}, u32[]{:S(2)}) copy-start(bf16[512,768]{1,0:T(8,128)(2,1)} %constant.28.analysis_ref) | copy-start | bytes 2359300
  28.1 22.3 %copy-start.2 = (bf16[2,216,144]{2,1,0:T(8,128)(2,1)S(1)}, bf16[2,216,144]{2,1,0:T(8,128)(2,1)}, u32[]{:S(2)}) copy-start(bf16[2,216,144]{2,1,0:T(8,128)(2,1)} %constant.25.table_ref) | copy-start | bytes 373252
  28.1 22.3 %copy-start.4 = (bf16[2,144,40]{2,1,0:T(8,128)(2,1)S(1)}, bf16[2,144,40]{2,1,0:T(8,128)(2,1)}, u32[]{:S(2)}) copy-start(bf16[2,144,40]{2,1,0:T(8,128)(2,1)} %constant.26.place_ref) | copy-start | bytes 69124

commit v5 on v4

--- a/solution.py
+++ b/solution.py
@@ -113,9 +113,7 @@
 
 def neighbours(blocks):
     me = lax.axis_index("elem")
-    odd = lax.bitwise_and(me, 1)
-    other = lax.bitwise_and(me + 2 * odd - 1 + blocks, blocks - 1)
-    return me, (me + 1 - 2 * odd, other)
+    return me, (lax.bitwise_and(me + blocks - 1, blocks - 1), lax.bitwise_and(me + 1, blocks - 1))
 
 
 def start_copies(pairs, sems):
@@ -135,8 +133,12 @@
     return dot(pick, jnp.concatenate(tiles, axis=0))
 
 
+def everywhere(reduce, x):
+    return reduce(reduce(x, axis=1, keepdims=True), axis=0, keepdims=True)
+
+
 def pack_kernel(
-    blocks, partner_hbm, side_hbm, flip_hbm, metric_hbm, v_hbm, table_hbm, pick_hbm, send_ref, own_ref, swap_ref_0, swap_ref_1, plan_ref,
+    blocks, partner_hbm, side_hbm, flip_hbm, metric_hbm, v_hbm, table_hbm, pick_hbm, send_ref, own_ref, prev_ref, next_ref, plan_ref,
     partner_ref, side_ref, flip_ref, metric_ref, v_ref, table_ref, pick_ref, rows_ref, place_ref, sems,
 ):
     copies = start_copies(
@@ -156,15 +158,25 @@
     rows_ref[:, 96:128, :] = jnp.zeros((8, 32, 144), BF16)
     for copy in copies:
         copy.wait()
-    low, high, least = [jnp.int32(7)] * 2, [jnp.int32(0)] * 2, [jnp.int32(1 << 30)] * 2
-    for e in range(8):
-        for f in range(4):
-            p = partner_ref[f, e]
-            for i in range(2):
-                there = lax.shift_right_arithmetic(p, 3) == sides[i]
-                low[i] = jnp.where(there, jnp.minimum(low[i], e), low[i])
-                high[i] = jnp.where(there, e, high[i])
-                least[i] = jnp.where(there, jnp.minimum(least[i], p), least[i])
+    p = partner_ref[...]
+    home = p >> 3
+    e, f = iota((4, 8), 1).astype(F32), iota((4, 8), 0).astype(F32)
+    number = p.astype(F32)
+    turn = (flip_ref[...] * 8 + side_ref[...]).astype(F32)
+    there = [home == side for side in sides]
+    low = [everywhere(jnp.min, jnp.where(t, e, 7.0)) for t in there]
+    high = [everywhere(jnp.max, jnp.where(t, e, 0.0)) for t in there]
+    least = [everywhere(jnp.min, jnp.where(t, number, 1e9)) for t in there]
+    near = ((p & 7) << 4).astype(F32) + turn
+    inside = jnp.where(home == me, near, 16.0 * e + f)
+    first = jnp.where(number == least[0], 128.0, 144.0) + turn
+    second = jnp.where(number == least[1], 160.0, 176.0) + turn
+    plan_ref[0:4, 0:8] = inside.astype(jnp.int32)
+    plan_ref[4:8, 0:8] = jnp.where(there[0], first, jnp.where(there[1], second, inside)).astype(jnp.int32)
+    column = iota((1, 8), 1)
+    ends = jnp.where(column == 0, low[0], jnp.where(column == 1, high[0], jnp.where(column == 2, low[1], high[1])))
+    plan_ref[8:9, 0:8] = ends.astype(jnp.int32)
+    (plan_copy,) = start_copies(((plan_ref, place_ref),), sems)
     table = table_ref[...]
     pick = pick_ref[...]
     for b in range(6):
@@ -185,40 +197,27 @@
                 grad = xi * metric_ref[2 * g, e] + eta * metric_ref[2 * g + 1, e]
                 at = 16 * e + 8 * flip + 4 * g
                 own_ref[at : at + 4] = grad.astype(BF16).reshape(4, 16, 128)
-    for i, out_ref in enumerate((swap_ref_0, swap_ref_1)):
-        out_ref[0] = own_ref[pl.ds(16 * low[i], 8)]
-        out_ref[1] = own_ref[pl.ds(16 * high[i], 8)]
+    plan_copy.wait()
+    for i, out_ref in enumerate((prev_ref, next_ref)):
+        for k in range(2):
+            out_ref[k] = own_ref[pl.ds(16 * place_ref[8, 2 * i + k], 8)]
     for e in range(8):
-        places = []
-        for f in range(4):
-            p = partner_ref[f, e]
-            home = lax.shift_right_arithmetic(p, 3)
-            turn = flip_ref[f, e] * 8 + side_ref[f, e]
-            near = lax.bitwise_and(p, 7) * 16 + turn
-            far = jnp.where(home == sides[0], jnp.where(p == least[0], 128, 144), jnp.where(p == least[1], 160, 176)) + turn
-            inside = jnp.where(home == me, near, 16 * e + f)
-            place_ref[e, f] = jnp.where((p < 0) | (home == me), inside, far)
-            places.append(inside)
-        out = average(own_ref, pick, e, places)
+        out = average(own_ref, pick, e, [place_ref[f, e] for f in range(4)])
         for h in range(2):
             send_ref[h, e, 112:152, :] = out[40 * h : 40 * h + 40].astype(BF16)
-    for r, e in enumerate((low[0], high[0], low[1], high[1])):
-        plan_ref[8 * r] = e
-        for f in range(4):
-            plan_ref[8 * r + 1 + f] = place_ref[e, f]
-
-
-def border_kernel(plan_ref, swap_ref_0, swap_ref_1, pick_ref, own_in, send_in, own_ref, send_ref):
+
+
+def border_kernel(plan_ref, prev_ref, next_ref, pick_ref, own_in, send_in, own_ref, send_ref):
     reverse = reverse_faces()
-    for k, ref in ((8, swap_ref_0), (10, swap_ref_1)):
+    for k, ref in ((8, prev_ref), (10, next_ref)):
         for i in range(2):
             at = 16 * (k + i)
             own_ref[at : at + 8] = ref[i]
             own_ref[at + 8 : at + 16] = dot(reverse, ref[i].reshape(128, 128)).astype(BF16).reshape(8, 16, 128)
     pick = pick_ref[...]
     for r in range(4):
-        e = plan_ref[8 * r]
-        out = average(own_ref, pick, e, [plan_ref[8 * r + 1 + f] for f in range(4)])
+        e = plan_ref[8, r]
+        out = average(own_ref, pick, e, [plan_ref[4 + f, e] for f in range(4)])
         for h in range(2):
             send_ref[h, e, 112:152, :] = out[40 * h : 40 * h + 40].astype(BF16)
 
@@ -248,7 +247,7 @@
     place = place_ref[half]
     tails = regroup([got_ref[p, 96:112, :].astype(F32) for p in range(16)])
     faces = regroup([got_ref[p, 112:152, :].astype(F32) for p in range(16)])
-    on_face = dot(place, jnp.ones((40, 512), BF16)) > 0.5
+    on_face = dot(place, jnp.ones((40, 128), BF16)) > 0.5
     lane = iota((72, 128), 1)
     even = (lane & 1) == 0
     copy.wait()
@@ -265,7 +264,10 @@
             turned.append(jnp.where(even, -k * pltpu.roll(v, 127, 1), k * pltpu.roll(v, 1, 1)))
         field_ref[288 * c : 288 * c + 144, :] = jnp.concatenate([value, jnp.concatenate(turned, axis=1)], axis=0).astype(BF16)
         grads = jnp.concatenate([xi * m[0] + eta * m[1], xi * m[2] + eta * m[3]], axis=0)
-        grads = jnp.where(on_face, dot(place, faces[c].astype(BF16)), grads)
+        at_faces = dot(place, faces[c].astype(BF16))
+        grads = jnp.concatenate(
+            [jnp.where(on_face, at_faces[:, at : at + 128], grads[:, at : at + 128]) for at in range(0, 512, 128)], axis=1
+        )
         field_ref[288 * c + 144 : 288 * c + 288, :] = grads.astype(BF16)
     adv_ref[208:256, :] = jnp.zeros((48, 768), BF16)
     for j in range(0, 768, 256):
@@ -287,20 +289,29 @@
 def unpack_kernel(in_ref, out_hbm, out_ref, sems):
     out, inp = iota((128, 128), 0), iota((128, 128), 1)
     order = jnp.where(inp == ((out & 7) << 4) + (out >> 3), 1.0, 0.0).astype(BF16)
-    lead, cols = iota((256, 144), 0) - iota((256, 144), 1), iota((256, 144), 1)
-    mine = (cols < 72, cols >= 72)
+    lane = iota((128, 128), 1)
+    left = lane < 72
     copies = []
-    for c in range(3):
-        block = None
+    for b in range(2):
+        halves = []
         for z in range(2):
-            pick = jnp.where((lead == 72 * (c - z)) & mine[z], 1.0, 0.0).astype(BF16)
-            part = dot(in_ref[8 * z : 8 * z + 8].reshape(256, 256), pick)
-            block = part if block is None else block + part
-        block = block.astype(BF16)
-        for b in range(2):
-            piece = jnp.concatenate([block[32 * e + 16 * b : 32 * e + 16 * b + 16] for e in range(8)], axis=0)
+            piece = jnp.concatenate([in_ref[8 * z + e, 16 * b : 16 * b + 16, :] for e in range(8)], axis=0)
+            halves.append(dot(order, piece))
+        a0, a1 = halves[0][:, 0:128], halves[0][:, 128:256]
+        b0, b1 = halves[1][:, 0:128], halves[1][:, 128:256]
+        for c in range(3):
+            if c == 0:
+                upper = pltpu.roll(b0, 72, 1)
+                first, second = jnp.where(left, a0, upper), upper
+            elif c == 1:
+                lower = jnp.where(lane < 56, pltpu.roll(a0, 56, 1), pltpu.roll(a1, 56, 1))
+                first, second = jnp.where(left, lower, b0), b1
+            else:
+                upper = pltpu.roll(b1, 56, 1)
+                first, second = jnp.where(left, pltpu.roll(a1, 112, 1), upper), upper
             rows = pl.ds(256 * c + 128 * b, 128)
-            out_ref[rows, :] = dot(order, piece).astype(BF16)
+            out_ref[rows, 0:128] = first.astype(BF16)
+            out_ref[rows, 128:144] = second[:, 0:16].astype(BF16)
             copies.append(pltpu.make_async_copy(out_ref.at[rows], out_hbm.at[rows], sems.at[2 * c + b]))
             copies[-1].start()
     for copy in copies:
@@ -336,11 +347,11 @@
 
 def on_device(velocity_modes, metric, face_partner, face_side, face_flip):
     blocks = lax.axis_size("elem")
-    within = [(i, i ^ 1) for i in range(blocks)]
-    across = [((i + 1) % blocks, ((i ^ 1) + 1) % blocks) for i in range(blocks)]
+    up = [(i, (i + 1) % blocks) for i in range(blocks)]
+    down = [(j, i) for i, j in up]
     synth, analysis = fourier_tables(512, 768)
     pick, geometry = bf16(pick_table()), in_hbm(metric.T)
-    send, own, to_first, to_second, plan = call(
+    send, own, to_prev, to_next, plan = call(
         functools.partial(pack_kernel, blocks),
         [HBM] * 7,
         [
@@ -348,21 +359,21 @@
             shape(192, 16, 128),
             shape(2, 8, 16, 128),
             shape(2, 8, 16, 128),
-            jax.ShapeDtypeStruct((32,), jnp.int32),
+            jax.ShapeDtypeStruct((16, 128), jnp.int32),
         ],
         [
-            pltpu.SMEM((4, 8), jnp.int32),
-            pltpu.SMEM((4, 8), jnp.int32),
-            pltpu.SMEM((4, 8), jnp.int32),
+            pltpu.VMEM((4, 8), jnp.int32),
+            pltpu.VMEM((4, 8), jnp.int32),
+            pltpu.VMEM((4, 8), jnp.int32),
             pltpu.SMEM((4, 8), F32),
             pltpu.VMEM((768, 144), BF16),
             pltpu.VMEM((272, 144), BF16),
             pltpu.VMEM((80, 128), BF16),
             pltpu.VMEM((8, 128, 144), BF16),
-            pltpu.SMEM((8, 4), jnp.int32),
+            pltpu.SMEM((16, 128), jnp.int32),
             pltpu.SemaphoreType.DMA((7,)),
         ],
-        out_specs=[VMEM] * 4 + [SMEM],
+        out_specs=[VMEM] * 5,
     )(
         in_hbm(face_partner.T),
         in_hbm(face_side.T),
@@ -372,14 +383,14 @@
         in_hbm(bf16(trace_table())),
         in_hbm(pick),
     )
-    from_first = lax.ppermute(to_first, "elem", within)
-    from_second = lax.ppermute(to_second, "elem", across)
+    from_prev = lax.ppermute(to_next, "elem", up)
+    from_next = lax.ppermute(to_prev, "elem", down)
     _, send = call(
         border_kernel,
         [SMEM, VMEM, VMEM, VMEM, VMEM, VMEM],
         [shape(192, 16, 128), shape(2, 8, 152, 128)],
         aliases={4: 0, 5: 1},
-    )(plan, from_first, from_second, pick, own, send)
+    )(plan, from_prev, from_next, pick, own, send)
     got = lax.all_to_all(send.reshape(16, 152, 128), "plane", 0, 0, tiled=True)
     out = call(
         main_kernel,

time: 67.6 us -> 66.1 us (0.978)
  Pallas kernels: 8.13 us -> 7.35 us
  transfers between devices with their start and end apart: 2 -> 2, of which waited for: 1 -> 2; matrix products, arithmetic and copies ran while one was open for 0% -> 0% of each run, Pallas kernels for 0% -> 0%
where the time goes in v5:
time: 66.1 us; the launch traced here: 65.8 us
  blocking collectives  35 us (53%)
  starting transfers between devices  21.5 us (33%)
  Pallas kernels  7.35 us (11%)
  waiting for transfers between devices  1.88 us (3%)
    all_to_all x1, blocking collectives, on_device(): got = lax.all_to_all(send.reshape(16, 152, 128), 'plane', 0, 0, tiled=True)  22.5 us
    ppermute x1, starting transfers between devices, on_device(): from_next = lax.ppermute(to_prev, 'elem', down)  19.5 us
    all_to_all x1, blocking collectives, on_device(): out = lax.all_to_all(out, 'plane', 0, 0, tiled=True)  12.5 us
    pallas_call x1, Pallas kernels, on_device(): call(functools.partial(pack_kernel, blocks), [HBM] * 7, [shape(2, 8, 152,...  2.67 us
    pallas_call x1, Pallas kernels, on_device(): call(main_kernel, [HBM, VMEM, VMEM, VMEM, VMEM, VMEM], shape(16, 32, 256)...  2.59 us
    ppermute x1, starting transfers between devices, on_device(): from_prev = lax.ppermute(to_next, 'elem', up)  1.92 us
    ppermute x1, waiting for transfers between devices, on_device(): from_next = lax.ppermute(to_prev, 'elem', down)  1.49 us
  transfers between devices with their start and end apart: 2, of which 2 were waited for; matrix products, arithmetic and copies ran while one was open for 0% of the time, Pallas kernels for 0%

profile of v5, /device:TPU:2, one launch (start us, length us, event | category | flops | bytes accessed | tf_op | source)
XLA Modules:
  0.0 65.8 jit_solution(17144481061315930497)
XLA Ops:
  0.0 0.0 copy-start.3
  0.0 2.7 %shard_map.109 = (bf16[2,8,152,128]{3,2,1,0:T(8,128)(2,1)S(1)}, bf16[192,16,128]{2,1,0:T(8,128)(2,1)S(1)}, bf16[2,8,16,128]{3,2,1,0:T(8,128)(2,1)S(1)}, bf16[2,8,16,128]{3,2,1,0:T(8,128)(2,1)S(1)}, s32[16,128]{1,0:T(8,128)S(1)}) custom-call(s32[4,8]{1,0:T(4,128)} %bitcast.11, s32[4,8]{1,0:T(4,128)} %bitcast.12, s32[4,8]{1,0:T(4,128)} %bitcast.13, ...), custom_call_target="tpu_custom_call" | custom-call | tf_op jit(solution)/shard_map/pallas_call | solution.py:354
  2.7 1.9 %collective-permute-start = (bf16[2,8,16,128]{3,2,1,0:T(8,128)(2,1)S(1)}, bf16[2,8,16,128]{3,2,1,0:T(8,128)(2,1)S(1)}, u32[]{:S(2)}, u32[]{:S(2)}) collective-permute-start(bf16[2,8,16,128]{3,2,1,0:T(8,128)(2,1)S(1)} %get-tuple-element.12), channel_id=1, source_target_pairs={{0,16},{16,32},{32,48},{48,64},{64,80},{80,96},{96,112},{112,128},... | collective-permute-start | bytes 196616 | tf_op jit(solution)/shard_map/ppermute | solution.py:386
  4.6 19.5 %collective-permute-start.1 = (bf16[2,8,16,128]{3,2,1,0:T(8,128)(2,1)S(1)}, bf16[2,8,16,128]{3,2,1,0:T(8,128)(2,1)S(1)}, u32[]{:S(2)}, u32[]{:S(2)}) collective-permute-start(bf16[2,8,16,128]{3,2,1,0:T(8,128)(2,1)S(1)} %get-tuple-element.13), channel_id=1, source_target_pairs={{16,0},{32,16},{48,32},{64,48},{80,64},{96,80},{112,96},{128,112},... | collective-permute-start | bytes 196616 | tf_op jit(solution)/shard_map/ppermute | solution.py:387
  24.2 0.4 collective-permute-done.prev_ref
  24.5 1.5 %collective-permute-done.1.next_ref = bf16[2,8,16,128]{3,2,1,0:T(8,128)(2,1)S(1)} collective-permute-done((bf16[2,8,16,128]{3,2,1,0:T(8,128)(2,1)S(1)}, bf16[2,8,16,128]{3,2,1,0:T(8,128)(2,1)S(1)}, u32[]{:S(2)}, u32[]{:S(2)}) %collective-permute-start.1) | collective-permute-done | bytes 65568 | tf_op jit(solution)/shard_map/ppermute | solution.py:387
  26.0 0.0 copy-done.3
  26.0 0.0 copy-start.1
  26.0 1.0 %shard_map.110 = (bf16[192,16,128]{2,1,0:T(8,128)(2,1)S(1)}, bf16[2,8,152,128]{3,2,1,0:T(8,128)(2,1)S(1)}) custom-call(s32[16,128]{1,0:T(8,128)S(1)} %get-tuple-element.11.plan_ref, bf16[2,8,16,128]{3,2,1,0:T(8,128)(2,1)S(1)} %collective-permute-done.prev_ref, ...), custom_call_target="tpu_custom_call", output_to_operand_aliasing={{0}: (4, {}), {1}: (5, {})} | custom-call | tf_op jit(solution)/shard_map/pallas_call | solution.py:388
  27.1 0.0 copy-start
  27.1 0.0 copy-start.2
  27.1 0.0 copy-start.4
  27.1 22.5 %all_to_all.10.got_ref = bf16[16,152,128]{2,1,0:T(8,128)(2,1)S(1)} all-to-all(bf16[16,152,128]{2,1,0:T(8,128)(2,1)S(1)} %bitcast.7), channel_id=1, replica_groups=mesh['elem'=64,'plane'=16] {'plane'}, dimensions={0} | all-to-all | bytes 1245184 | tf_op jit(solution)/shard_map/all_to_all | solution.py:394
  49.7 0.0 copy-done.1
  49.7 0.0 copy-done
  49.7 0.0 copy-done.2
  49.7 0.0 copy-done.4
  49.7 2.6 %shard_map.111 = bf16[16,32,256]{2,1,0:T(8,128)(2,1)S(1)} custom-call(f32[4,8]{1,0:T(4,128)} %bitcast.10, bf16[16,152,128]{2,1,0:T(8,128)(2,1)S(1)} %all_to_all.10.got_ref, bf16[2,216,144]{2,1,0:T(8,128)(2,1)S(1)} %copy-done.2, bf16[2,144,40]{2,1,0:T(8,128)(2,1)S(1)} %copy-done.4, bf16[512,768]{1,0:T(8,128)(2,1)S(1)} %copy-done.1, bf16[512,768]{1,0:T(8,128)(2,1)S(1)} %copy-done), custom_call_target="tpu_custom_call" | custom-call | tf_op jit(solution)/shard_map/pallas_call | solution.py:395
  52.3 12.5 %all_to_all.11.in_ref = bf16[16,32,256]{2,1,0:T(8,128)(2,1)S(1)} all-to-all(bf16[16,32,256]{2,1,0:T(8,128)(2,1)S(1)} %shard_map.111), channel_id=1, replica_groups=mesh['elem'=64,'plane'=16] {'plane'}, dimensions={0} | all-to-all | bytes 524288 | tf_op jit(solution)/shard_map/all_to_all | solution.py:406
  64.8 1.0 %shard_map.112 = bf16[768,144]{1,0:T(8,128)(2,1)} custom-call(bf16[16,32,256]{2,1,0:T(8,128)(2,1)S(1)} %all_to_all.11.in_ref), custom_call_target="tpu_custom_call" | custom-call | tf_op jit(solution)/shard_map/pallas_call | solution.py:407
Async XLA Ops:
  0.0 26.0 %copy-start.3 = (bf16[80,128]{1,0:T(8,128)(2,1)S(1)}, bf16[80,128]{1,0:T(8,128)(2,1)}, u32[]{:S(2)}) copy-start(bf16[80,128]{1,0:T(8,128)(2,1)} %constant.24.pick_hbm.pick_ref) | copy-start | bytes 61444
  2.7 21.9 %collective-permute-start = (bf16[2,8,16,128]{3,2,1,0:T(8,128)(2,1)S(1)}, bf16[2,8,16,128]{3,2,1,0:T(8,128)(2,1)S(1)}, u32[]{:S(2)}, u32[]{:S(2)}) collective-permute-start(bf16[2,8,16,128]{3,2,1,0:T(8,128)(2,1)S(1)} %get-tuple-element.12), channel_id=1, source_target_pairs={{0,16},{16,32},{32,48},{48,64},{64,80},{80,96},{96,112},{112,128},... | collective-permute-start | bytes 196616 | tf_op jit(solution)/shard_map/ppermute | solution.py:386
  4.6 21.4 %collective-permute-start.1 = (bf16[2,8,16,128]{3,2,1,0:T(8,128)(2,1)S(1)}, bf16[2,8,16,128]{3,2,1,0:T(8,128)(2,1)S(1)}, u32[]{:S(2)}, u32[]{:S(2)}) collective-permute-start(bf16[2,8,16,128]{3,2,1,0:T(8,128)(2,1)S(1)} %get-tuple-element.13), channel_id=1, source_target_pairs={{16,0},{32,16},{48,32},{64,48},{80,64},{96,80},{112,96},{128,112},... | collective-permute-start | bytes 196616 | tf_op jit(solution)/shard_map/ppermute | solution.py:387
  26.0 23.6 %copy-start.1 = (bf16[512,768]{1,0:T(8,128)(2,1)S(1)}, bf16[512,768]{1,0:T(8,128)(2,1)}, u32[]{:S(2)}) copy-start(bf16[512,768]{1,0:T(8,128)(2,1)} %constant.27.synth_ref) | copy-start | bytes 2359300
  27.1 22.6 %copy-start = (bf16[512,768]{1,0:T(8,128)(2,1)S(1)}, bf16[512,768]{1,0:T(8,128)(2,1)}, u32[]{:S(2)}) copy-start(bf16[512,768]{1,0:T(8,128)(2,1)} %constant.28.analysis_ref) | copy-start | bytes 2359300
  27.1 22.6 %copy-start.2 = (bf16[2,216,144]{2,1,0:T(8,128)(2,1)S(1)}, bf16[2,216,144]{2,1,0:T(8,128)(2,1)}, u32[]{:S(2)}) copy-start(bf16[2,216,144]{2,1,0:T(8,128)(2,1)} %constant.25.table_ref) | copy-start | bytes 373252
  27.1 22.6 %copy-start.4 = (bf16[2,144,40]{2,1,0:T(8,128)(2,1)S(1)}, bf16[2,144,40]{2,1,0:T(8,128)(2,1)}, u32[]{:S(2)}) copy-start(bf16[2,144,40]{2,1,0:T(8,128)(2,1)} %constant.26.place_ref) | copy-start | bytes 69124

commit v6 on v5

--- a/solution.py
+++ b/solution.py
@@ -139,24 +139,31 @@
 
 def pack_kernel(
     blocks, partner_hbm, side_hbm, flip_hbm, metric_hbm, v_hbm, table_hbm, pick_hbm, send_ref, own_ref, prev_ref, next_ref, plan_ref,
-    partner_ref, side_ref, flip_ref, metric_ref, v_ref, table_ref, pick_ref, rows_ref, place_ref, sems,
+    partner_ref, side_ref, flip_ref, metric_ref, v_ref, table_ref, pick_ref, rows_ref, tail_ref, place_ref, sems,
 ):
+    parts = [pl.ds(256 * i, 256) for i in range(3)]
     copies = start_copies(
-        (
-            (v_hbm, v_ref),
+        [(v_hbm.at[part], v_ref.at[part]) for part in parts]
+        + [
             (table_hbm, table_ref),
             (partner_hbm, partner_ref),
             (metric_hbm, metric_ref),
             (side_hbm, side_ref),
             (flip_hbm, flip_ref),
             (pick_hbm, pick_ref),
-        ),
+        ],
         sems,
     )
     me, sides = neighbours(blocks)
     order = to_element_rows()
     rows_ref[:, 96:128, :] = jnp.zeros((8, 32, 144), BF16)
-    for copy in copies:
+    for b in range(6):
+        if b % 2 == 0:
+            copies[b // 2].wait()
+        block = dot(order, v_ref[128 * b : 128 * b + 128, :]).astype(BF16)
+        for e in range(8):
+            rows_ref[e, 16 * b : 16 * b + 16, :] = block[16 * e : 16 * e + 16]
+    for copy in copies[3:]:
         copy.wait()
     p = partner_ref[...]
     home = p >> 3
@@ -179,17 +186,12 @@
     (plan_copy,) = start_copies(((plan_ref, place_ref),), sems)
     table = table_ref[...]
     pick = pick_ref[...]
-    for b in range(6):
-        block = dot(order, v_ref[128 * b : 128 * b + 128, :]).astype(BF16)
-        for e in range(8):
-            rows_ref[e, 16 * b : 16 * b + 16, :] = block[16 * e : 16 * e + 16]
     for e in range(8):
         rows = rows_ref[e]
         out = dot_nt(table, rows)
-        tail = out[0:16].astype(BF16)
+        tail_ref[e] = out[0:16]
         for h in range(2):
             send_ref[h, e, 0:96, :] = rows[0:96, 0:128]
-            send_ref[h, e, 96:112, :] = tail
         for flip in range(2):
             xi = out[16 + 128 * flip : 80 + 128 * flip]
             eta = out[80 + 128 * flip : 144 + 128 * flip]
@@ -198,16 +200,21 @@
                 at = 16 * e + 8 * flip + 4 * g
                 own_ref[at : at + 4] = grad.astype(BF16).reshape(4, 16, 128)
     plan_copy.wait()
+    taken = iota((40, 128), 1) < 96
     for i, out_ref in enumerate((prev_ref, next_ref)):
         for k in range(2):
             out_ref[k] = own_ref[pl.ds(16 * place_ref[8, 2 * i + k], 8)]
     for e in range(8):
         out = average(own_ref, pick, e, [place_ref[f, e] for f in range(4)])
+        upper = tail_ref[e, 8:16]
+        spare = jnp.concatenate([pltpu.roll(upper, 96 - 32 * c, 1) for c in range(3)] + [jnp.zeros((16, 128), F32)], axis=0)
         for h in range(2):
-            send_ref[h, e, 112:152, :] = out[40 * h : 40 * h + 40].astype(BF16)
-
-
-def border_kernel(plan_ref, prev_ref, next_ref, pick_ref, own_in, send_in, own_ref, send_ref):
+            face = jnp.where(taken, out[40 * h : 40 * h + 40], spare)
+            send_ref[h, e, 96:144, :] = jnp.concatenate([tail_ref[e, 0:8], face], axis=0).astype(BF16)
+
+
+def border_kernel(plan_ref, prev_ref, next_ref, pick_ref, own_in, send_in, own_ref, send_ref, place_ref, sems):
+    (plan_copy,) = start_copies(((plan_ref, place_ref),), sems)
     reverse = reverse_faces()
     for k, ref in ((8, prev_ref), (10, next_ref)):
         for i in range(2):
@@ -215,23 +222,28 @@
             own_ref[at : at + 8] = ref[i]
             own_ref[at + 8 : at + 16] = dot(reverse, ref[i].reshape(128, 128)).astype(BF16).reshape(8, 16, 128)
     pick = pick_ref[...]
+    row, lane = iota((48, 128), 0), iota((48, 128), 1)
+    kept = (row < 8) | (lane >= 96)
+    plan_copy.wait()
     for r in range(4):
-        e = plan_ref[8, r]
-        out = average(own_ref, pick, e, [plan_ref[4 + f, e] for f in range(4)])
+        e = place_ref[8, r]
+        out = average(own_ref, pick, e, [place_ref[4 + f, e] for f in range(4)])
         for h in range(2):
-            send_ref[h, e, 112:152, :] = out[40 * h : 40 * h + 40].astype(BF16)
-
-
-def regroup(blocks):
+            old = send_ref[h, e, 96:144, :].astype(F32)
+            face = jnp.concatenate([jnp.zeros((8, 128), F32), out[40 * h : 40 * h + 40]], axis=0)
+            send_ref[h, e, 96:144, :] = jnp.where(kept, old, face).astype(BF16)
+
+
+def regroup(blocks, lanes=(0, 32, 64)):
     rows = blocks[0].shape[0]
     lane = iota((rows, 128), 1) >> 5
     out = []
-    for c in range(3):
+    for start in lanes:
         groups = []
         for first in range(0, len(blocks), 4):
             group = None
             for k in range(4):
-                shift = (32 * (k - c)) % 128
+                shift = (32 * k - start) % 128
                 piece = pltpu.roll(blocks[first + k], shift, 1) if shift else blocks[first + k]
                 group = piece if group is None else jnp.where(lane == k, piece, group)
             groups.append(group)
@@ -245,8 +257,11 @@
     elem, half = lax.bitwise_and(position, 7), lax.shift_right_logical(position, 3)
     table = table_ref[half]
     place = place_ref[half]
-    tails = regroup([got_ref[p, 96:112, :].astype(F32) for p in range(16)])
-    faces = regroup([got_ref[p, 112:152, :].astype(F32) for p in range(16)])
+    blocks = [got_ref[p, 96:144, :].astype(F32) for p in range(16)]
+    lower = regroup([block[0:8] for block in blocks])
+    upper = [regroup([block[8 * c + 8 : 8 * c + 16] for block in blocks], (96,))[0] for c in range(3)]
+    tails = [jnp.concatenate([lower[c], upper[c]], axis=0) for c in range(3)]
+    faces = regroup([block[8:48] for block in blocks])
     on_face = dot(place, jnp.ones((40, 128), BF16)) > 0.5
     lane = iota((72, 128), 1)
     even = (lane & 1) == 0
@@ -283,7 +298,12 @@
         terms.append(jnp.zeros((8, 256), F32))
         adv_ref[0:224, j : j + 256] = jnp.concatenate(terms, axis=0).astype(BF16)
     out = dot_nt(analysis_ref[...], adv_ref[...])
-    out_ref[...] = out.astype(BF16).reshape(16, 32, 256)
+    left = iota((8, 128), 1) < 88
+    for p in range(16):
+        out_ref[p, 0:32, :] = out[32 * p : 32 * p + 32, 0:128].astype(BF16)
+        rest = [out[32 * p + 8 * i : 32 * p + 8 * i + 8, 128:256] for i in range(4)]
+        packed = [jnp.where(left, rest[i], pltpu.roll(rest[3], 88 - 40 * i, 1)) for i in range(3)]
+        out_ref[p, 32:56, :] = jnp.concatenate(packed, axis=0).astype(BF16)
 
 
 def unpack_kernel(in_ref, out_hbm, out_ref, sems):
@@ -291,14 +311,21 @@
     order = jnp.where(inp == ((out & 7) << 4) + (out >> 3), 1.0, 0.0).astype(BF16)
     lane = iota((128, 128), 1)
     left = lane < 72
+    column = iota((8, 128), 1)
+    rests = []
+    for p in range(16):
+        packed = in_ref[p, 32:56, :].astype(F32)
+        h = [packed[8 * i : 8 * i + 8] for i in range(3)]
+        last = jnp.where(column < 40, pltpu.roll(h[0], 40, 1), jnp.where(column < 80, pltpu.roll(h[1], 80, 1), pltpu.roll(h[2], 120, 1)))
+        rests.append([jnp.concatenate(pair, axis=0).astype(BF16) for pair in ((h[0], h[1]), (h[2], last))])
     copies = []
     for b in range(2):
         halves = []
         for z in range(2):
-            piece = jnp.concatenate([in_ref[8 * z + e, 16 * b : 16 * b + 16, :] for e in range(8)], axis=0)
-            halves.append(dot(order, piece))
-        a0, a1 = halves[0][:, 0:128], halves[0][:, 128:256]
-        b0, b1 = halves[1][:, 0:128], halves[1][:, 128:256]
+            main = jnp.concatenate([in_ref[8 * z + e, 16 * b : 16 * b + 16, :] for e in range(8)], axis=0)
+            rest = jnp.concatenate([rests[8 * z + e][b] for e in range(8)], axis=0)
+            halves.append((dot(order, main), dot(order, rest)))
+        (a0, a1), (b0, b1) = halves
         for c in range(3):
             if c == 0:
                 upper = pltpu.roll(b0, 72, 1)
@@ -355,7 +382,7 @@
         functools.partial(pack_kernel, blocks),
         [HBM] * 7,
         [
-            shape(2, 8, 152, 128),
+            shape(2, 8, 144, 128),
             shape(192, 16, 128),
             shape(2, 8, 16, 128),
             shape(2, 8, 16, 128),
@@ -370,8 +397,9 @@
             pltpu.VMEM((272, 144), BF16),
             pltpu.VMEM((80, 128), BF16),
             pltpu.VMEM((8, 128, 144), BF16),
+            pltpu.VMEM((8, 16, 128), F32),
             pltpu.SMEM((16, 128), jnp.int32),
-            pltpu.SemaphoreType.DMA((7,)),
+            pltpu.SemaphoreType.DMA((9,)),
         ],
         out_specs=[VMEM] * 5,
     )(
@@ -387,15 +415,16 @@
     from_next = lax.ppermute(to_prev, "elem", down)
     _, send = call(
         border_kernel,
-        [SMEM, VMEM, VMEM, VMEM, VMEM, VMEM],
-        [shape(192, 16, 128), shape(2, 8, 152, 128)],
+        [VMEM] * 6,
+        [shape(192, 16, 128), shape(2, 8, 144, 128)],
+        [pltpu.SMEM((16, 128), jnp.int32), pltpu.SemaphoreType.DMA((1,))],
         aliases={4: 0, 5: 1},
     )(plan, from_prev, from_next, pick, own, send)
-    got = lax.all_to_all(send.reshape(16, 152, 128), "plane", 0, 0, tiled=True)
+    got = lax.all_to_all(send.reshape(16, 144, 128), "plane", 0, 0, tiled=True)
     out = call(
         main_kernel,
         [HBM, VMEM, VMEM, VMEM, VMEM, VMEM],
-        shape(16, 32, 256),
+        shape(16, 56, 128),
         [
             pltpu.VMEM((864, 512), BF16),
             pltpu.VMEM((256, 768), BF16),

time: 66.1 us -> 65.8 us (level)
  no operation moved by 1% of the time
where the time goes in v6:
time: 65.8 us; the launch traced here: 65.5 us
  blocking collectives  34.6 us (53%)
  starting transfers between devices  21.5 us (33%)
  Pallas kernels  7.46 us (11%)
  waiting for transfers between devices  1.88 us (3%)
    all_to_all x1, blocking collectives, on_device(): got = lax.all_to_all(send.reshape(16, 144, 128), 'plane', 0, 0, tiled=True)  22.3 us
    ppermute x1, starting transfers between devices, on_device(): from_next = lax.ppermute(to_prev, 'elem', down)  19.5 us
    all_to_all x1, blocking collectives, on_device(): out = lax.all_to_all(out, 'plane', 0, 0, tiled=True)  12.4 us
    pallas_call x1, Pallas kernels, on_device(): call(functools.partial(pack_kernel, blocks), [HBM] * 7, [shape(2, 8, 144,...  2.86 us
    pallas_call x1, Pallas kernels, on_device(): call(main_kernel, [HBM, VMEM, VMEM, VMEM, VMEM, VMEM], shape(16, 56, 128)...  2.66 us
    ppermute x1, starting transfers between devices, on_device(): from_prev = lax.ppermute(to_next, 'elem', up)  1.92 us
    ppermute x1, waiting for transfers between devices, on_device(): from_next = lax.ppermute(to_prev, 'elem', down)  1.5 us
  transfers between devices with their start and end apart: 2, of which 2 were waited for; matrix products, arithmetic and copies ran while one was open for 0% of the time, Pallas kernels for 0%

profile of v6, /device:TPU:2, one launch (start us, length us, event | category | flops | bytes accessed | tf_op | source)
XLA Modules:
  0.0 65.5 jit_solution(13144633851855993773)
XLA Ops:
  0.0 0.0 copy-start.3
  0.0 2.9 %shard_map.109 = (bf16[2,8,144,128]{3,2,1,0:T(8,128)(2,1)S(1)}, bf16[192,16,128]{2,1,0:T(8,128)(2,1)S(1)}, bf16[2,8,16,128]{3,2,1,0:T(8,128)(2,1)S(1)}, bf16[2,8,16,128]{3,2,1,0:T(8,128)(2,1)S(1)}, s32[16,128]{1,0:T(8,128)S(1)}) custom-call(s32[4,8]{1,0:T(4,128)} %bitcast.11, s32[4,8]{1,0:T(4,128)} %bitcast.12, s32[4,8]{1,0:T(4,128)} %bitcast.13, ...), custom_call_target="tpu_custom_call" | custom-call | tf_op jit(solution)/shard_map/pallas_call | solution.py:381
  2.9 1.9 %collective-permute-start = (bf16[2,8,16,128]{3,2,1,0:T(8,128)(2,1)S(1)}, bf16[2,8,16,128]{3,2,1,0:T(8,128)(2,1)S(1)}, u32[]{:S(2)}, u32[]{:S(2)}) collective-permute-start(bf16[2,8,16,128]{3,2,1,0:T(8,128)(2,1)S(1)} %get-tuple-element.12), channel_id=1, source_target_pairs={{0,16},{16,32},{32,48},{48,64},{64,80},{80,96},{96,112},{112,128},... | collective-permute-start | bytes 196616 | tf_op jit(solution)/shard_map/ppermute | solution.py:414
  4.8 19.5 %collective-permute-start.1 = (bf16[2,8,16,128]{3,2,1,0:T(8,128)(2,1)S(1)}, bf16[2,8,16,128]{3,2,1,0:T(8,128)(2,1)S(1)}, u32[]{:S(2)}, u32[]{:S(2)}) collective-permute-start(bf16[2,8,16,128]{3,2,1,0:T(8,128)(2,1)S(1)} %get-tuple-element.13), channel_id=1, source_target_pairs={{16,0},{32,16},{48,32},{64,48},{80,64},{96,80},{112,96},{128,112},... | collective-permute-start | bytes 196616 | tf_op jit(solution)/shard_map/ppermute | solution.py:415
  24.3 0.4 collective-permute-done.prev_ref
  24.7 1.5 %collective-permute-done.1.next_ref = bf16[2,8,16,128]{3,2,1,0:T(8,128)(2,1)S(1)} collective-permute-done((bf16[2,8,16,128]{3,2,1,0:T(8,128)(2,1)S(1)}, bf16[2,8,16,128]{3,2,1,0:T(8,128)(2,1)S(1)}, u32[]{:S(2)}, u32[]{:S(2)}) %collective-permute-start.1) | collective-permute-done | bytes 65568 | tf_op jit(solution)/shard_map/ppermute | solution.py:415
  26.2 0.0 copy-done.3
  26.2 0.0 copy-start.1
  26.2 0.9 %shard_map.110 = (bf16[192,16,128]{2,1,0:T(8,128)(2,1)S(1)}, bf16[2,8,144,128]{3,2,1,0:T(8,128)(2,1)S(1)}) custom-call(s32[16,128]{1,0:T(8,128)S(1)} %get-tuple-element.11.plan_ref, bf16[2,8,16,128]{3,2,1,0:T(8,128)(2,1)S(1)} %collective-permute-done.prev_ref, ...), custom_call_target="tpu_custom_call", output_to_operand_aliasing={{0}: (4, {}), {1}: (5, {})} | custom-call | tf_op jit(solution)/shard_map/pallas_call | solution.py:416
  27.1 0.0 copy-start
  27.2 0.0 copy-start.2
  27.2 0.0 copy-start.4
  27.2 22.3 %all_to_all.10.got_ref = bf16[16,144,128]{2,1,0:T(8,128)(2,1)S(1)} all-to-all(bf16[16,144,128]{2,1,0:T(8,128)(2,1)S(1)} %bitcast.7), channel_id=1, replica_groups=mesh['elem'=64,'plane'=16] {'plane'}, dimensions={0} | all-to-all | bytes 1179648 | tf_op jit(solution)/shard_map/all_to_all | solution.py:423
  49.4 0.0 copy-done.1
  49.4 0.0 copy-done
  49.4 0.0 copy-done.2
  49.5 0.0 copy-done.4
  49.5 2.7 %shard_map.111 = bf16[16,56,128]{2,1,0:T(8,128)(2,1)S(1)} custom-call(f32[4,8]{1,0:T(4,128)} %bitcast.10, bf16[16,144,128]{2,1,0:T(8,128)(2,1)S(1)} %all_to_all.10.got_ref, bf16[2,216,144]{2,1,0:T(8,128)(2,1)S(1)} %copy-done.2, bf16[2,144,40]{2,1,0:T(8,128)(2,1)S(1)} %copy-done.4, bf16[512,768]{1,0:T(8,128)(2,1)S(1)} %copy-done.1, bf16[512,768]{1,0:T(8,128)(2,1)S(1)} %copy-done), custom_call_target="tpu_custom_call" | custom-call | tf_op jit(solution)/shard_map/pallas_call | solution.py:424
  52.1 12.4 %all_to_all.11.in_ref = bf16[16,56,128]{2,1,0:T(8,128)(2,1)S(1)} all-to-all(bf16[16,56,128]{2,1,0:T(8,128)(2,1)S(1)} %shard_map.111), channel_id=1, replica_groups=mesh['elem'=64,'plane'=16] {'plane'}, dimensions={0} | all-to-all | bytes 458752 | tf_op jit(solution)/shard_map/all_to_all | solution.py:435
  64.5 1.1 %shard_map.112 = bf16[768,144]{1,0:T(8,128)(2,1)} custom-call(bf16[16,56,128]{2,1,0:T(8,128)(2,1)S(1)} %all_to_all.11.in_ref), custom_call_target="tpu_custom_call" | custom-call | tf_op jit(solution)/shard_map/pallas_call | solution.py:436
Async XLA Ops:
  0.0 26.2 %copy-start.3 = (bf16[80,128]{1,0:T(8,128)(2,1)S(1)}, bf16[80,128]{1,0:T(8,128)(2,1)}, u32[]{:S(2)}) copy-start(bf16[80,128]{1,0:T(8,128)(2,1)} %constant.24.pick_hbm.pick_ref) | copy-start | bytes 61444
  2.9 21.9 %collective-permute-start = (bf16[2,8,16,128]{3,2,1,0:T(8,128)(2,1)S(1)}, bf16[2,8,16,128]{3,2,1,0:T(8,128)(2,1)S(1)}, u32[]{:S(2)}, u32[]{:S(2)}) collective-permute-start(bf16[2,8,16,128]{3,2,1,0:T(8,128)(2,1)S(1)} %get-tuple-element.12), channel_id=1, source_target_pairs={{0,16},{16,32},{32,48},{48,64},{64,80},{80,96},{96,112},{112,128},... | collective-permute-start | bytes 196616 | tf_op jit(solution)/shard_map/ppermute | solution.py:414
  4.8 21.4 %collective-permute-start.1 = (bf16[2,8,16,128]{3,2,1,0:T(8,128)(2,1)S(1)}, bf16[2,8,16,128]{3,2,1,0:T(8,128)(2,1)S(1)}, u32[]{:S(2)}, u32[]{:S(2)}) collective-permute-start(bf16[2,8,16,128]{3,2,1,0:T(8,128)(2,1)S(1)} %get-tuple-element.13), channel_id=1, source_target_pairs={{16,0},{32,16},{48,32},{64,48},{80,64},{96,80},{112,96},{128,112},... | collective-permute-start | bytes 196616 | tf_op jit(solution)/shard_map/ppermute | solution.py:415
  26.2 23.2 %copy-start.1 = (bf16[512,768]{1,0:T(8,128)(2,1)S(1)}, bf16[512,768]{1,0:T(8,128)(2,1)}, u32[]{:S(2)}) copy-start(bf16[512,768]{1,0:T(8,128)(2,1)} %constant.27.synth_ref) | copy-start | bytes 2359300
  27.1 22.3 %copy-start = (bf16[512,768]{1,0:T(8,128)(2,1)S(1)}, bf16[512,768]{1,0:T(8,128)(2,1)}, u32[]{:S(2)}) copy-start(bf16[512,768]{1,0:T(8,128)(2,1)} %constant.28.analysis_ref) | copy-start | bytes 2359300
  27.2 22.3 %copy-start.2 = (bf16[2,216,144]{2,1,0:T(8,128)(2,1)S(1)}, bf16[2,216,144]{2,1,0:T(8,128)(2,1)}, u32[]{:S(2)}) copy-start(bf16[2,216,144]{2,1,0:T(8,128)(2,1)} %constant.25.table_ref) | copy-start | bytes 373252
  27.2 22.3 %copy-start.4 = (bf16[2,144,40]{2,1,0:T(8,128)(2,1)S(1)}, bf16[2,144,40]{2,1,0:T(8,128)(2,1)}, u32[]{:S(2)}) copy-start(bf16[2,144,40]{2,1,0:T(8,128)(2,1)} %constant.26.place_ref) | copy-start | bytes 69124

commit v7 on v6

--- a/solution.py
+++ b/solution.py
@@ -113,7 +113,8 @@
 
 def neighbours(blocks):
     me = lax.axis_index("elem")
-    return me, (lax.bitwise_and(me + blocks - 1, blocks - 1), lax.bitwise_and(me + 1, blocks - 1))
+    step = 2 * lax.bitwise_and(me, 1) - 1
+    return me, (lax.bitwise_and(me + step + blocks, blocks - 1), me - step)
 
 
 def start_copies(pairs, sems):
@@ -138,7 +139,7 @@
 
 
 def pack_kernel(
-    blocks, partner_hbm, side_hbm, flip_hbm, metric_hbm, v_hbm, table_hbm, pick_hbm, send_ref, own_ref, prev_ref, next_ref, plan_ref,
+    blocks, partner_hbm, side_hbm, flip_hbm, metric_hbm, v_hbm, table_hbm, pick_hbm, send_ref, own_ref, first_ref, second_ref, plan_ref,
     partner_ref, side_ref, flip_ref, metric_ref, v_ref, table_ref, pick_ref, rows_ref, tail_ref, place_ref, sems,
 ):
     parts = [pl.ds(256 * i, 256) for i in range(3)]
@@ -201,7 +202,7 @@
                 own_ref[at : at + 4] = grad.astype(BF16).reshape(4, 16, 128)
     plan_copy.wait()
     taken = iota((40, 128), 1) < 96
-    for i, out_ref in enumerate((prev_ref, next_ref)):
+    for i, out_ref in enumerate((first_ref, second_ref)):
         for k in range(2):
             out_ref[k] = own_ref[pl.ds(16 * place_ref[8, 2 * i + k], 8)]
     for e in range(8):
@@ -213,10 +214,10 @@
             send_ref[h, e, 96:144, :] = jnp.concatenate([tail_ref[e, 0:8], face], axis=0).astype(BF16)
 
 
-def border_kernel(plan_ref, prev_ref, next_ref, pick_ref, own_in, send_in, own_ref, send_ref, place_ref, sems):
+def border_kernel(plan_ref, first_ref, second_ref, pick_ref, own_in, send_in, own_ref, send_ref, place_ref, sems):
     (plan_copy,) = start_copies(((plan_ref, place_ref),), sems)
     reverse = reverse_faces()
-    for k, ref in ((8, prev_ref), (10, next_ref)):
+    for k, ref in ((8, first_ref), (10, second_ref)):
         for i in range(2):
             at = 16 * (k + i)
             own_ref[at : at + 8] = ref[i]
@@ -374,11 +375,11 @@
 
 def on_device(velocity_modes, metric, face_partner, face_side, face_flip):
     blocks = lax.axis_size("elem")
-    up = [(i, (i + 1) % blocks) for i in range(blocks)]
-    down = [(j, i) for i, j in up]
+    across = [((i + 1) % blocks, ((i ^ 1) + 1) % blocks) for i in range(blocks)]
+    within = [(i, i ^ 1) for i in range(blocks)]
     synth, analysis = fourier_tables(512, 768)
     pick, geometry = bf16(pick_table()), in_hbm(metric.T)
-    send, own, to_prev, to_next, plan = call(
+    send, own, to_first, to_second, plan = call(
         functools.partial(pack_kernel, blocks),
         [HBM] * 7,
         [
@@ -411,15 +412,15 @@
         in_hbm(bf16(trace_table())),
         in_hbm(pick),
     )
-    from_prev = lax.ppermute(to_next, "elem", up)
-    from_next = lax.ppermute(to_prev, "elem", down)
+    from_first = lax.ppermute(to_first, "elem", across)
+    from_second = lax.ppermute(to_second, "elem", within)
     _, send = call(
         border_kernel,
         [VMEM] * 6,
         [shape(192, 16, 128), shape(2, 8, 144, 128)],
         [pltpu.SMEM((16, 128), jnp.int32), pltpu.SemaphoreType.DMA((1,))],
         aliases={4: 0, 5: 1},
-    )(plan, from_prev, from_next, pick, own, send)
+    )(plan, from_first, from_second, pick, own, send)
     got = lax.all_to_all(send.reshape(16, 144, 128), "plane", 0, 0, tiled=True)
     out = call(
         main_kernel,

time: 65.8 us -> 71.1 us (1.081)
  blocking collectives: 34.6 us -> 40.5 us
    all_to_all x1, blocking collectives: 22.3 us -> 27.4 us  [on_device(): got = lax.all_to_all(send.reshape(16, 144, 128), 'plane', 0, 0, tiled=True)]
    all_to_all x1, blocking collectives: 12.4 us -> 13.1 us  [on_device(): out = lax.all_to_all(out, 'plane', 0, 0, tiled=True)]
where the time goes in v7:
time: 71.1 us; the launch traced here: 70.8 us
  blocking collectives  40.5 us (57%)
  starting transfers between devices  21.5 us (30%)
  Pallas kernels  7.47 us (11%)
  waiting for transfers between devices  1.22 us (2%)
    all_to_all x1, blocking collectives, on_device(): got = lax.all_to_all(send.reshape(16, 144, 128), 'plane', 0, 0, tiled=True)  27.4 us
    ppermute x1, starting transfers between devices, on_device(): from_first = lax.ppermute(to_first, 'elem', across)  19.5 us
    all_to_all x1, blocking collectives, on_device(): out = lax.all_to_all(out, 'plane', 0, 0, tiled=True)  13.1 us
    pallas_call x1, Pallas kernels, on_device(): call(functools.partial(pack_kernel, blocks), [HBM] * 7, [shape(2, 8, 144,...  2.86 us
    pallas_call x1, Pallas kernels, on_device(): call(main_kernel, [HBM, VMEM, VMEM, VMEM, VMEM, VMEM], shape(16, 56, 128)...  2.66 us
    ppermute x1, starting transfers between devices, on_device(): from_second = lax.ppermute(to_second, 'elem', within)  1.92 us
  transfers between devices with their start and end apart: 2, of which 2 were waited for; matrix products, arithmetic and copies ran while one was open for 0% of the time, Pallas kernels for 0%

profile of v7, /device:TPU:2, one launch (start us, length us, event | category | flops | bytes accessed | tf_op | source)
XLA Modules:
  0.0 70.8 jit_solution(17232084120536200312)
XLA Ops:
  0.0 0.0 copy-start.3
  0.0 2.9 %shard_map.109 = (bf16[2,8,144,128]{3,2,1,0:T(8,128)(2,1)S(1)}, bf16[192,16,128]{2,1,0:T(8,128)(2,1)S(1)}, bf16[2,8,16,128]{3,2,1,0:T(8,128)(2,1)S(1)}, bf16[2,8,16,128]{3,2,1,0:T(8,128)(2,1)S(1)}, s32[16,128]{1,0:T(8,128)S(1)}) custom-call(s32[4,8]{1,0:T(4,128)} %bitcast.11, s32[4,8]{1,0:T(4,128)} %bitcast.12, s32[4,8]{1,0:T(4,128)} %bitcast.13, ...), custom_call_target="tpu_custom_call" | custom-call | tf_op jit(solution)/shard_map/pallas_call | solution.py:382
  2.9 19.5 %collective-permute-start = (bf16[2,8,16,128]{3,2,1,0:T(8,128)(2,1)S(1)}, bf16[2,8,16,128]{3,2,1,0:T(8,128)(2,1)S(1)}, u32[]{:S(2)}, u32[]{:S(2)}) collective-permute-start(bf16[2,8,16,128]{3,2,1,0:T(8,128)(2,1)S(1)} %get-tuple-element.12), channel_id=1, source_target_pairs={{16,32},{32,16},{48,64},{64,48},{80,96},{96,80},{112,128},{128,112... | collective-permute-start | bytes 196616 | tf_op jit(solution)/shard_map/ppermute | solution.py:415
  22.4 1.9 %collective-permute-start.1 = (bf16[2,8,16,128]{3,2,1,0:T(8,128)(2,1)S(1)}, bf16[2,8,16,128]{3,2,1,0:T(8,128)(2,1)S(1)}, u32[]{:S(2)}, u32[]{:S(2)}) collective-permute-start(bf16[2,8,16,128]{3,2,1,0:T(8,128)(2,1)S(1)} %get-tuple-element.13), channel_id=1, source_target_pairs={{0,16},{16,0},{32,48},{48,32},{64,80},{80,64},{96,112},{112,96},{1... | collective-permute-start | bytes 196616 | tf_op jit(solution)/shard_map/ppermute | solution.py:416
  24.3 0.4 collective-permute-done.first_ref
  24.7 0.8 %collective-permute-done.1.second_ref = bf16[2,8,16,128]{3,2,1,0:T(8,128)(2,1)S(1)} collective-permute-done((bf16[2,8,16,128]{3,2,1,0:T(8,128)(2,1)S(1)}, bf16[2,8,16,128]{3,2,1,0:T(8,128)(2,1)S(1)}, u32[]{:S(2)}, u32[]{:S(2)}) %collective-permute-start.1) | collective-permute-done | bytes 65568 | tf_op jit(solution)/shard_map/ppermute | solution.py:416
  25.6 0.0 copy-done.3
  25.6 0.0 copy-start.1
  25.6 0.9 %shard_map.110 = (bf16[192,16,128]{2,1,0:T(8,128)(2,1)S(1)}, bf16[2,8,144,128]{3,2,1,0:T(8,128)(2,1)S(1)}) custom-call(s32[16,128]{1,0:T(8,128)S(1)} %get-tuple-element.11.plan_ref, bf16[2,8,16,128]{3,2,1,0:T(8,128)(2,1)S(1)} %collective-permute-done.first_ref, ...), custom_call_target="tpu_custom_call", output_to_operand_aliasing={{0}: (4, {}), {1}: (5, {})} | custom-call | tf_op jit(solution)/shard_map/pallas_call | solution.py:417
  26.5 0.0 copy-start
  26.5 0.0 copy-start.2
  26.5 0.0 copy-start.4
  26.5 27.4 %all_to_all.10.got_ref = bf16[16,144,128]{2,1,0:T(8,128)(2,1)S(1)} all-to-all(bf16[16,144,128]{2,1,0:T(8,128)(2,1)S(1)} %bitcast.7), channel_id=1, replica_groups=mesh['elem'=64,'plane'=16] {'plane'}, dimensions={0} | all-to-all | bytes 1179648 | tf_op jit(solution)/shard_map/all_to_all | solution.py:424
  53.9 0.0 copy-done.1
  53.9 0.0 copy-done
  53.9 0.0 copy-done.2
  53.9 0.0 copy-done.4
  53.9 2.7 %shard_map.111 = bf16[16,56,128]{2,1,0:T(8,128)(2,1)S(1)} custom-call(f32[4,8]{1,0:T(4,128)} %bitcast.10, bf16[16,144,128]{2,1,0:T(8,128)(2,1)S(1)} %all_to_all.10.got_ref, bf16[2,216,144]{2,1,0:T(8,128)(2,1)S(1)} %copy-done.2, bf16[2,144,40]{2,1,0:T(8,128)(2,1)S(1)} %copy-done.4, bf16[512,768]{1,0:T(8,128)(2,1)S(1)} %copy-done.1, bf16[512,768]{1,0:T(8,128)(2,1)S(1)} %copy-done), custom_call_target="tpu_custom_call" | custom-call | tf_op jit(solution)/shard_map/pallas_call | solution.py:425
  56.6 13.1 %all_to_all.11.in_ref = bf16[16,56,128]{2,1,0:T(8,128)(2,1)S(1)} all-to-all(bf16[16,56,128]{2,1,0:T(8,128)(2,1)S(1)} %shard_map.111), channel_id=1, replica_groups=mesh['elem'=64,'plane'=16] {'plane'}, dimensions={0} | all-to-all | bytes 458752 | tf_op jit(solution)/shard_map/all_to_all | solution.py:436
  69.7 1.1 %shard_map.112 = bf16[768,144]{1,0:T(8,128)(2,1)} custom-call(bf16[16,56,128]{2,1,0:T(8,128)(2,1)S(1)} %all_to_all.11.in_ref), custom_call_target="tpu_custom_call" | custom-call | tf_op jit(solution)/shard_map/pallas_call | solution.py:437
Async XLA Ops:
  0.0 25.6 %copy-start.3 = (bf16[80,128]{1,0:T(8,128)(2,1)S(1)}, bf16[80,128]{1,0:T(8,128)(2,1)}, u32[]{:S(2)}) copy-start(bf16[80,128]{1,0:T(8,128)(2,1)} %constant.24.pick_hbm.pick_ref) | copy-start | bytes 61444
  2.9 21.9 %collective-permute-start = (bf16[2,8,16,128]{3,2,1,0:T(8,128)(2,1)S(1)}, bf16[2,8,16,128]{3,2,1,0:T(8,128)(2,1)S(1)}, u32[]{:S(2)}, u32[]{:S(2)}) collective-permute-start(bf16[2,8,16,128]{3,2,1,0:T(8,128)(2,1)S(1)} %get-tuple-element.12), channel_id=1, source_target_pairs={{16,32},{32,16},{48,64},{64,48},{80,96},{96,80},{112,128},{128,112... | collective-permute-start | bytes 196616 | tf_op jit(solution)/shard_map/ppermute | solution.py:415
  22.4 3.1 %collective-permute-start.1 = (bf16[2,8,16,128]{3,2,1,0:T(8,128)(2,1)S(1)}, bf16[2,8,16,128]{3,2,1,0:T(8,128)(2,1)S(1)}, u32[]{:S(2)}, u32[]{:S(2)}) collective-permute-start(bf16[2,8,16,128]{3,2,1,0:T(8,128)(2,1)S(1)} %get-tuple-element.13), channel_id=1, source_target_pairs={{0,16},{16,0},{32,48},{48,32},{64,80},{80,64},{96,112},{112,96},{1... | collective-permute-start | bytes 196616 | tf_op jit(solution)/shard_map/ppermute | solution.py:416
  25.6 28.4 %copy-start.1 = (bf16[512,768]{1,0:T(8,128)(2,1)S(1)}, bf16[512,768]{1,0:T(8,128)(2,1)}, u32[]{:S(2)}) copy-start(bf16[512,768]{1,0:T(8,128)(2,1)} %constant.27.synth_ref) | copy-start | bytes 2359300
  26.5 27.5 %copy-start = (bf16[512,768]{1,0:T(8,128)(2,1)S(1)}, bf16[512,768]{1,0:T(8,128)(2,1)}, u32[]{:S(2)}) copy-start(bf16[512,768]{1,0:T(8,128)(2,1)} %constant.28.analysis_ref) | copy-start | bytes 2359300
  26.5 27.4 %copy-start.2 = (bf16[2,216,144]{2,1,0:T(8,128)(2,1)S(1)}, bf16[2,216,144]{2,1,0:T(8,128)(2,1)}, u32[]{:S(2)}) copy-start(bf16[2,216,144]{2,1,0:T(8,128)(2,1)} %constant.25.table_ref) | copy-start | bytes 373252
  26.5 27.4 %copy-start.4 = (bf16[2,144,40]{2,1,0:T(8,128)(2,1)S(1)}, bf16[2,144,40]{2,1,0:T(8,128)(2,1)}, u32[]{:S(2)}) copy-start(bf16[2,144,40]{2,1,0:T(8,128)(2,1)} %constant.26.place_ref) | copy-start | bytes 69124

commit v8 on v6

--- a/solution.py
+++ b/solution.py
@@ -36,11 +36,11 @@
 
 def trace_table():
     _, xi, eta = legendre_tables()
-    table = np.zeros((272, 144))
+    table = np.zeros((144, 144))
     table[np.arange(16), 128 + np.arange(16)] = 1.0
     for face in range(4):
         q = face_points(face)
-        for at, rows in ((16, xi[q]), (80, eta[q]), (144, xi[q[::-1]]), (208, eta[q[::-1]])):
+        for at, rows in ((16, xi[q]), (80, eta[q])):
             table[at + 16 * face : at + 16 * face + 12] = rows
     return table
 
@@ -137,9 +137,9 @@
     return reduce(reduce(x, axis=1, keepdims=True), axis=0, keepdims=True)
 
 
-def pack_kernel(
-    blocks, partner_hbm, side_hbm, flip_hbm, metric_hbm, v_hbm, table_hbm, pick_hbm, send_ref, own_ref, prev_ref, next_ref, plan_ref,
-    partner_ref, side_ref, flip_ref, metric_ref, v_ref, table_ref, pick_ref, rows_ref, tail_ref, place_ref, sems,
+def trace_kernel(
+    blocks, partner_hbm, side_hbm, flip_hbm, metric_hbm, v_hbm, table_hbm, rows_ref, tail_ref, own_ref, prev_ref, next_ref, plan_ref,
+    partner_ref, side_ref, flip_ref, metric_ref, v_ref, table_ref, place_ref, sems,
 ):
     parts = [pl.ds(256 * i, 256) for i in range(3)]
     copies = start_copies(
@@ -150,7 +150,6 @@
             (metric_hbm, metric_ref),
             (side_hbm, side_ref),
             (flip_hbm, flip_ref),
-            (pick_hbm, pick_ref),
         ],
         sems,
     )
@@ -185,25 +184,32 @@
     plan_ref[8:9, 0:8] = ends.astype(jnp.int32)
     (plan_copy,) = start_copies(((plan_ref, place_ref),), sems)
     table = table_ref[...]
-    pick = pick_ref[...]
     for e in range(8):
-        rows = rows_ref[e]
-        out = dot_nt(table, rows)
+        out = dot_nt(table, rows_ref[e])
         tail_ref[e] = out[0:16]
-        for h in range(2):
-            send_ref[h, e, 0:96, :] = rows[0:96, 0:128]
-        for flip in range(2):
-            xi = out[16 + 128 * flip : 80 + 128 * flip]
-            eta = out[80 + 128 * flip : 144 + 128 * flip]
-            for g in range(2):
-                grad = xi * metric_ref[2 * g, e] + eta * metric_ref[2 * g + 1, e]
-                at = 16 * e + 8 * flip + 4 * g
-                own_ref[at : at + 4] = grad.astype(BF16).reshape(4, 16, 128)
+        xi, eta = out[16:80], out[80:144]
+        for g in range(2):
+            grad = xi * metric_ref[2 * g, e] + eta * metric_ref[2 * g + 1, e]
+            at = 16 * e + 4 * g
+            own_ref[at : at + 4] = grad.astype(BF16).reshape(4, 16, 128)
     plan_copy.wait()
-    taken = iota((40, 128), 1) < 96
     for i, out_ref in enumerate((prev_ref, next_ref)):
         for k in range(2):
             out_ref[k] = own_ref[pl.ds(16 * place_ref[8, 2 * i + k], 8)]
+
+
+def pack_kernel(plan_ref, rows_ref, tail_ref, own_in, pick_ref, send_ref, own_ref, place_ref, sems):
+    (plan_copy,) = start_copies(((plan_ref, place_ref),), sems)
+    pick = pick_ref[...]
+    taken = iota((40, 128), 1) < 96
+    reverse = reverse_faces()
+    for e in range(8):
+        forward = own_ref[16 * e : 16 * e + 8].reshape(128, 128)
+        own_ref[16 * e + 8 : 16 * e + 16] = dot(reverse, forward).astype(BF16).reshape(8, 16, 128)
+        rows = rows_ref[e, 0:96, 0:128]
+        for h in range(2):
+            send_ref[h, e, 0:96, :] = rows
+    plan_copy.wait()
     for e in range(8):
         out = average(own_ref, pick, e, [place_ref[f, e] for f in range(4)])
         upper = tail_ref[e, 8:16]
@@ -378,30 +384,29 @@
     down = [(j, i) for i, j in up]
     synth, analysis = fourier_tables(512, 768)
     pick, geometry = bf16(pick_table()), in_hbm(metric.T)
-    send, own, to_prev, to_next, plan = call(
-        functools.partial(pack_kernel, blocks),
-        [HBM] * 7,
+    plan_shape = jax.ShapeDtypeStruct((16, 128), jnp.int32)
+    small = pltpu.VMEM((4, 8), jnp.int32)
+    rows, tail, own, to_prev, to_next, plan = call(
+        functools.partial(trace_kernel, blocks),
+        [HBM] * 6,
         [
-            shape(2, 8, 144, 128),
+            shape(8, 128, 144),
+            jax.ShapeDtypeStruct((8, 16, 128), F32),
             shape(192, 16, 128),
             shape(2, 8, 16, 128),
             shape(2, 8, 16, 128),
-            jax.ShapeDtypeStruct((16, 128), jnp.int32),
+            plan_shape,
         ],
         [
-            pltpu.VMEM((4, 8), jnp.int32),
-            pltpu.VMEM((4, 8), jnp.int32),
-            pltpu.VMEM((4, 8), jnp.int32),
+            small,
+            small,
+            small,
             pltpu.SMEM((4, 8), F32),
             pltpu.VMEM((768, 144), BF16),
-            pltpu.VMEM((272, 144), BF16),
-            pltpu.VMEM((80, 128), BF16),
-            pltpu.VMEM((8, 128, 144), BF16),
-            pltpu.VMEM((8, 16, 128), F32),
+            pltpu.VMEM((144, 144), BF16),
             pltpu.SMEM((16, 128), jnp.int32),
-            pltpu.SemaphoreType.DMA((9,)),
+            pltpu.SemaphoreType.DMA((8,)),
         ],
-        out_specs=[VMEM] * 5,
     )(
         in_hbm(face_partner.T),
         in_hbm(face_side.T),
@@ -409,10 +414,16 @@
         geometry,
         in_hbm(velocity_modes.reshape(768, 144)),
         in_hbm(bf16(trace_table())),
-        in_hbm(pick),
     )
     from_prev = lax.ppermute(to_next, "elem", up)
     from_next = lax.ppermute(to_prev, "elem", down)
+    send, own = call(
+        pack_kernel,
+        [VMEM] * 5,
+        [shape(2, 8, 144, 128), shape(192, 16, 128)],
+        [pltpu.SMEM((16, 128), jnp.int32), pltpu.SemaphoreType.DMA((1,))],
+        aliases={3: 1},
+    )(plan, rows, tail, own, pick)
     _, send = call(
         border_kernel,
         [VMEM] * 6,

time: 65.8 us -> 65.4 us (level)
  waiting for transfers between devices: 1.88 us -> 0.93 us
    pallas_call x1 -> x2, Pallas kernels: 2.86 us -> 3.38 us  [the longest x1 2.45 us: on_device(): call(functools.partial(trace_kernel, blocks), [HBM] * 6, [shape(8, 128, 1...]
  transfers between devices with their start and end apart: 2 -> 2, of which waited for: 2 -> 1; matrix products, arithmetic and copies ran while one was open for 0% -> 0% of each run, Pallas kernels for 0% -> 1%
where the time goes in v8:
time: 65.4 us; the launch traced here: 65.1 us
  blocking collectives  34.6 us (53%)
  starting transfers between devices  21.5 us (33%)
  Pallas kernels  8.01 us (12%)
  waiting for transfers between devices  0.93 us (1%)
    all_to_all x1, blocking collectives, on_device(): got = lax.all_to_all(send.reshape(16, 144, 128), 'plane', 0, 0, tiled=True)  22.3 us
    ppermute x1, starting transfers between devices, on_device(): from_next = lax.ppermute(to_prev, 'elem', down)  19.5 us
    all_to_all x1, blocking collectives, on_device(): out = lax.all_to_all(out, 'plane', 0, 0, tiled=True)  12.3 us
    pallas_call x1, Pallas kernels, on_device(): call(main_kernel, [HBM, VMEM, VMEM, VMEM, VMEM, VMEM], shape(16, 56, 128)...  2.68 us
    pallas_call x1, Pallas kernels, on_device(): call(functools.partial(trace_kernel, blocks), [HBM] * 6, [shape(8, 128, 1...  2.45 us
    ppermute x1, starting transfers between devices, on_device(): from_prev = lax.ppermute(to_next, 'elem', up)  1.92 us
  transfers between devices with their start and end apart: 2, of which 1 were waited for; matrix products, arithmetic and copies ran while one was open for 0% of the time, Pallas kernels for 1%

profile of v8, /device:TPU:2, one launch (start us, length us, event | category | flops | bytes accessed | tf_op | source)
XLA Modules:
  0.0 65.1 jit_solution(10551041974118025472)
XLA Ops:
  0.0 0.0 copy-start.3
  0.0 2.5 %shard_map.109 = (bf16[8,128,144]{2,1,0:T(8,128)(2,1)S(1)}, f32[8,16,128]{2,1,0:T(8,128)S(1)}, bf16[192,16,128]{2,1,0:T(8,128)(2,1)S(1)}, bf16[2,8,16,128]{3,2,1...) custom-call(s32[4,8]{1,0:T(4,128)} %bitcast.11, s32[4,8]{1,0:T(4,128)} %bitcast.12, ...), custom_call_target="tpu_custom_call" | custom-call | tf_op jit(solution)/shard_map/pallas_call | solution.py:389
  2.5 1.9 %collective-permute-start = (bf16[2,8,16,128]{3,2,1,0:T(8,128)(2,1)S(1)}, bf16[2,8,16,128]{3,2,1,0:T(8,128)(2,1)S(1)}, u32[]{:S(2)}, u32[]{:S(2)}) collective-permute-start(bf16[2,8,16,128]{3,2,1,0:T(8,128)(2,1)S(1)} %get-tuple-element.15), channel_id=1, source_target_pairs={{0,16},{16,32},{32,48},{48,64},{64,80},{80,96},{96,112},{112,128},... | collective-permute-start | bytes 196616 | tf_op jit(solution)/shard_map/ppermute | solution.py:418
  4.4 19.5 %collective-permute-start.1 = (bf16[2,8,16,128]{3,2,1,0:T(8,128)(2,1)S(1)}, bf16[2,8,16,128]{3,2,1,0:T(8,128)(2,1)S(1)}, u32[]{:S(2)}, u32[]{:S(2)}) collective-permute-start(bf16[2,8,16,128]{3,2,1,0:T(8,128)(2,1)S(1)} %get-tuple-element.16), channel_id=1, source_target_pairs={{16,0},{32,16},{48,32},{64,48},{80,64},{96,80},{112,96},{128,112},... | collective-permute-start | bytes 196616 | tf_op jit(solution)/shard_map/ppermute | solution.py:419
  23.9 0.0 copy-done.3
  23.9 0.9 %shard_map.110 = (bf16[2,8,144,128]{3,2,1,0:T(8,128)(2,1)S(1)}, bf16[192,16,128]{2,1,0:T(8,128)(2,1)S(1)}) custom-call(s32[16,128]{1,0:T(8,128)S(1)} %get-tuple-element.14.plan_ref, bf16[8,128,144]{2,1,0:T(8,128)(2,1)S(1)} %get-tuple-element.17.rows_ref, f32[8,16,128]{2,1,0:T(8,128)S(1)} %get-tuple-element.18.tail_ref, ...), custom_call_target="tpu_custom_call", output_to_operand_aliasing={{1}: (3, {})} | custom-call | tf_op jit(solution)/shard_map/pallas_call | solution.py:420
  24.9 0.0 collective-permute-done.prev_ref
  24.9 0.9 %collective-permute-done.1.next_ref = bf16[2,8,16,128]{3,2,1,0:T(8,128)(2,1)S(1)} collective-permute-done((bf16[2,8,16,128]{3,2,1,0:T(8,128)(2,1)S(1)}, bf16[2,8,16,128]{3,2,1,0:T(8,128)(2,1)S(1)}, u32[]{:S(2)}, u32[]{:S(2)}) %collective-permute-start.1) | collective-permute-done | bytes 65568 | tf_op jit(solution)/shard_map/ppermute | solution.py:419
  25.8 0.0 copy-start.1
  25.8 0.9 %shard_map.111 = (bf16[192,16,128]{2,1,0:T(8,128)(2,1)S(1)}, bf16[2,8,144,128]{3,2,1,0:T(8,128)(2,1)S(1)}) custom-call(s32[16,128]{1,0:T(8,128)S(1)} %get-tuple-element.14.plan_ref, bf16[2,8,16,128]{3,2,1,0:T(8,128)(2,1)S(1)} %collective-permute-done.prev_ref, ...), custom_call_target="tpu_custom_call", output_to_operand_aliasing={{0}: (4, {}), {1}: (5, {})} | custom-call | tf_op jit(solution)/shard_map/pallas_call | solution.py:427
  26.7 0.0 copy-start
  26.7 0.0 copy-start.2
  26.8 0.0 copy-start.4
  26.8 22.3 %all_to_all.10.got_ref = bf16[16,144,128]{2,1,0:T(8,128)(2,1)S(1)} all-to-all(bf16[16,144,128]{2,1,0:T(8,128)(2,1)S(1)} %bitcast.7), channel_id=1, replica_groups=mesh['elem'=64,'plane'=16] {'plane'}, dimensions={0} | all-to-all | bytes 1179648 | tf_op jit(solution)/shard_map/all_to_all | solution.py:434
  49.0 0.0 copy-done.1
  49.0 0.0 copy-done
  49.0 0.0 copy-done.2
  49.0 0.0 copy-done.4
  49.1 2.7 %shard_map.112 = bf16[16,56,128]{2,1,0:T(8,128)(2,1)S(1)} custom-call(f32[4,8]{1,0:T(4,128)} %bitcast.10, bf16[16,144,128]{2,1,0:T(8,128)(2,1)S(1)} %all_to_all.10.got_ref, bf16[2,216,144]{2,1,0:T(8,128)(2,1)S(1)} %copy-done.2, bf16[2,144,40]{2,1,0:T(8,128)(2,1)S(1)} %copy-done.4, bf16[512,768]{1,0:T(8,128)(2,1)S(1)} %copy-done.1, bf16[512,768]{1,0:T(8,128)(2,1)S(1)} %copy-done), custom_call_target="tpu_custom_call" | custom-call | tf_op jit(solution)/shard_map/pallas_call | solution.py:435
  51.7 12.3 %all_to_all.11.in_ref = bf16[16,56,128]{2,1,0:T(8,128)(2,1)S(1)} all-to-all(bf16[16,56,128]{2,1,0:T(8,128)(2,1)S(1)} %shard_map.112), channel_id=1, replica_groups=mesh['elem'=64,'plane'=16] {'plane'}, dimensions={0} | all-to-all | bytes 458752 | tf_op jit(solution)/shard_map/all_to_all | solution.py:446
  64.1 1.1 %shard_map.113 = bf16[768,144]{1,0:T(8,128)(2,1)} custom-call(bf16[16,56,128]{2,1,0:T(8,128)(2,1)S(1)} %all_to_all.11.in_ref), custom_call_target="tpu_custom_call" | custom-call | tf_op jit(solution)/shard_map/pallas_call | solution.py:447
Async XLA Ops:
  0.0 23.9 %copy-start.3 = (bf16[80,128]{1,0:T(8,128)(2,1)S(1)}, bf16[80,128]{1,0:T(8,128)(2,1)}, u32[]{:S(2)}) copy-start(bf16[80,128]{1,0:T(8,128)(2,1)} %constant.24.pick_ref) | copy-start | bytes 61444
  2.5 22.4 %collective-permute-start = (bf16[2,8,16,128]{3,2,1,0:T(8,128)(2,1)S(1)}, bf16[2,8,16,128]{3,2,1,0:T(8,128)(2,1)S(1)}, u32[]{:S(2)}, u32[]{:S(2)}) collective-permute-start(bf16[2,8,16,128]{3,2,1,0:T(8,128)(2,1)S(1)} %get-tuple-element.15), channel_id=1, source_target_pairs={{0,16},{16,32},{32,48},{48,64},{64,80},{80,96},{96,112},{112,128},... | collective-permute-start | bytes 196616 | tf_op jit(solution)/shard_map/ppermute | solution.py:418
  4.4 21.4 %collective-permute-start.1 = (bf16[2,8,16,128]{3,2,1,0:T(8,128)(2,1)S(1)}, bf16[2,8,16,128]{3,2,1,0:T(8,128)(2,1)S(1)}, u32[]{:S(2)}, u32[]{:S(2)}) collective-permute-start(bf16[2,8,16,128]{3,2,1,0:T(8,128)(2,1)S(1)} %get-tuple-element.16), channel_id=1, source_target_pairs={{16,0},{32,16},{48,32},{64,48},{80,64},{96,80},{112,96},{128,112},... | collective-permute-start | bytes 196616 | tf_op jit(solution)/shard_map/ppermute | solution.py:419
  25.8 23.2 %copy-start.1 = (bf16[512,768]{1,0:T(8,128)(2,1)S(1)}, bf16[512,768]{1,0:T(8,128)(2,1)}, u32[]{:S(2)}) copy-start(bf16[512,768]{1,0:T(8,128)(2,1)} %constant.27.synth_ref) | copy-start | bytes 2359300
  26.7 22.3 %copy-start = (bf16[512,768]{1,0:T(8,128)(2,1)S(1)}, bf16[512,768]{1,0:T(8,128)(2,1)}, u32[]{:S(2)}) copy-start(bf16[512,768]{1,0:T(8,128)(2,1)} %constant.28.analysis_ref) | copy-start | bytes 2359300
  26.7 22.3 %copy-start.2 = (bf16[2,216,144]{2,1,0:T(8,128)(2,1)S(1)}, bf16[2,216,144]{2,1,0:T(8,128)(2,1)}, u32[]{:S(2)}) copy-start(bf16[2,216,144]{2,1,0:T(8,128)(2,1)} %constant.25.table_ref) | copy-start | bytes 373252
  26.8 22.3 %copy-start.4 = (bf16[2,144,40]{2,1,0:T(8,128)(2,1)S(1)}, bf16[2,144,40]{2,1,0:T(8,128)(2,1)}, u32[]{:S(2)}) copy-start(bf16[2,144,40]{2,1,0:T(8,128)(2,1)} %constant.26.place_ref) | copy-start | bytes 69124
